TPU v7x, 32 devices: a whole 2x2x4 slice. The times are simulated.
32 devices in a mesh: dp: 8 (over y, x, core), tensor: 4 (over z).
Axes of the slice: x: 2, y: 2, z: 4, core: 2. Of those that a mesh axis runs over, the one named last changes fastest.
Arguments:
- picture_encoder_result: bfloat16 [2816, 1024], P('dp'), may hold values from -0.59765625 to 0.59765625
- sentence_encoder_result: bfloat16 [11264, 1024], P(('dp', 'tensor')), may hold values from -0.59765625 to 0.59765625
- picture_projector_matrix: bfloat16 [1024, 1024], P(None, 'tensor'), may hold values from -0.1875 to 0.1875
- sentence_projector_matrix: bfloat16 [1024, 1024], P(None, 'tensor'), may hold values from -0.1875 to 0.1875
- sentences_for_picture: int32 [2816], replicated, may hold values from 1 to 8, 11264 in all
- sharpness_factor: float32 [1], replicated, may hold values from 30 to 60
- score_offset_term: float32 [1], replicated, may hold values from -8 to -4
Outputs:
- grad_img: bfloat16 [2816, 1024], P('dp', 'tensor')
- grad_cap: bfloat16 [11264, 1024], P(('dp', 'tensor'))
Inputs may be any that keep to these rules, and one draw needn't show every extreme that they name: The counts sum to 11264; the captions of image m are the consecutive rows start[m] to start[m] + sentences_for_picture[m] - 1 of sentence_encoder_result, where start[m] is the sum of the counts of images before m; some image has 8.
All inputs are finite; a program needn't handle non-finite values.
Results may differ from a plain program's by a relative error of at most 0.014.
Values may be sent and summed in bfloat16 or wider, within the bound.
No kernel may reach another device: no remote copies, remote signals or barrier semaphores. Data moves between devices by JAX's collectives and lax.ppermute only.
A program may use at most 64 MiB of HBM per device.

v0:
```python
import functools

import jax
import jax.numpy as jnp
from jax import lax
from jax.experimental import pallas as pl
from jax.experimental.pallas import tpu as pltpu
from jax.sharding import PartitionSpec as P


epsilon = 1e-06
CORES = 2
ROWS_Y = 2
CHUNK = 32
PARTS = 2
LOG2E = 1.4426950408889634
F32 = jnp.float32
BF16 = jnp.bfloat16


def contract_last(a, b):
    return lax.dot_general(a, b, (((1,), (1,)), ((), ())), preferred_element_type=F32)


def contract_first(a, b):
    return lax.dot_general(a, b, (((0,), (0,)), ((), ())), preferred_element_type=F32)


def lane_sums(partial):
    ones = jnp.ones((128, 128), BF16)
    upper = partial.astype(BF16)
    lower = (partial - upper.astype(F32)).astype(BF16)
    return jnp.dot(upper, ones, preferred_element_type=F32) + jnp.dot(lower, ones, preferred_element_type=F32)


def folded(pieces):
    while len(pieces) > 1:
        pieces = [pieces[n] + pieces[n + 1] for n in range(0, len(pieces) - 1, 2)] + (
            pieces[-1:] if len(pieces) % 2 else []
        )
    return pieces[0]


def cut(ref, row, lane, height=16):
    return ref[row : row + height, lane * 128 : lane * 128 + 128]


def forward(x, w, raw, z, scales, top, rows):
    lanes = w.shape[1] // 128
    raw[top : top + rows, :] = jnp.dot(x[top : top + rows, :], w[...], preferred_element_type=F32)
    for r in range(top, top + rows, 16):
        value = [cut(raw, r, n) for n in range(lanes)]
        scales[r : r + 16, :] = folded([v * v for v in value])
    scales[top : top + rows, :] = lax.rsqrt(lane_sums(scales[top : top + rows, :]) + epsilon)
    for r in range(top, top + rows, 16):
        scale = scales[r : r + 16, :]
        for n in range(lanes):
            z[r : r + 16, n * 128 : n * 128 + 128] = (cut(raw, r, n) * scale).astype(BF16)


def back(source, raw, scales, raw_offset, offset, count, out, along):
    lanes = source.shape[1] // 128
    for r in range(offset, offset + count, 16):
        there = raw_offset + r
        along[r : r + 16, :] = folded([cut(source, r, n) * cut(raw, there, n) for n in range(lanes)])
    along[offset : offset + count, :] = lane_sums(along[offset : offset + count, :])
    for r in range(offset, offset + count, 16):
        there = raw_offset + r
        scale = scales[there : there + 16, :]
        pull = along[r : r + 16, :] * (scale * scale * scale)
        for n in range(lanes):
            value = scale * cut(source, r, n) - pull * cut(raw, there, n)
            out[r - offset : r - offset + 16, n * 128 : n * 128 + 128] = value.astype(out.dtype)


class Copies:
    def __init__(self, sem):
        self.sem, self.used = sem, 0

    def start(self, src, dst):
        copy = pltpu.make_async_copy(src, dst, self.sem.at[self.used])
        self.used += 1
        copy.start()
        return copy


def wait_all(copies):
    for copy in copies:
        copy.wait()


def pair_kernel(lay, *refs):
    n_cap, n_img, n_pc, n_pi = lay["n_cap"], lay["n_img"], lay["n_pc"], lay["n_pi"]
    rows, img_rows = lay["rows"], lay["img_rows"]
    slots, width = lay["slots"], lay["width"]
    at = 0

    def take(count):
        nonlocal at
        got = refs[at : at + count]
        at += count
        return got

    (place,) = take(1)
    cap_x, img_x = take(n_cap), take(n_img)
    (wc_own,) = take(1)
    wc_pieces = take((slots - 1) * n_pc)
    (wi_own,) = take(1)
    wi_pieces = take((slots - 1) * n_pi)
    first, last, weight, position, factors = take(5)
    out_send = take((n_img - 1) * PARTS)
    out_coef, out_zc, out_zi, out_rc, out_ri, out_sc, out_si, out_wc, out_wi = take(9)
    xc, xi, zc, zi, raw_c, raw_i, sc_c, sc_i, wc, wi, logits, coef, dz, along, sem = take(15)

    depth = wc.shape[0]
    moves = Copies(sem)
    copies = {}
    for name, own, pieces, full, n_p, base in (
        ("c", wc_own, wc_pieces, wc, n_pc, 0),
        ("i", wi_own, wi_pieces, wi, n_pi, n_pc),
    ):
        step = depth // n_p
        copies[name] = [moves.start(own, full.at[:, pl.ds(0, width)])]
        for k in range(1, slots):
            for r in range(n_p):
                offset = pl.multiple_of(place[base + r], step)
                copies[name].append(
                    moves.start(
                        pieces[(k - 1) * n_p + r],
                        full.at[pl.ds(offset, step), pl.ds(k * width, width)],
                    )
                )
    for q in range(n_cap):
        copies["c"].append(moves.start(cap_x[q], xc.at[pl.ds(q * rows, rows), :]))
    for q in range(n_img):
        copies["i"].append(moves.start(img_x[q], xi.at[pl.ds(q * img_rows, img_rows), :]))

    outs = []
    wait_all(copies["c"])
    outs.append(moves.start(wc, out_wc))
    for q in range(n_cap):
        forward(xc, wc, raw_c, zc, sc_c, q * rows, rows)
    outs += [moves.start(raw_c, out_rc), moves.start(zc, out_zc), moves.start(sc_c, out_sc)]
    wait_all(copies["i"])
    outs.append(moves.start(wi, out_wi))
    for q in range(n_img):
        forward(xi, wi, raw_i, zi, sc_i, q * img_rows, img_rows)
    outs += [moves.start(raw_i, out_ri), moves.start(zi, out_zi), moves.start(sc_i, out_si)]

    sharp = factors[0]
    slope, level = -LOG2E * sharp, -LOG2E * factors[1]
    spot = position[...]
    columns = n_cap * rows
    part = img_rows // PARTS
    for j in range(n_img):
        base = j * img_rows
        logits[...] = contract_last(zi[pl.ds(base, img_rows), :], zc[...])

        def chunk(r, _):
            here = pl.multiple_of(base + r * CHUNK, 16)
            line = pl.ds(pl.multiple_of(r * CHUNK, 16), CHUNK)
            touched = place[n_pc + n_pi + j * (img_rows // CHUNK) + r] != 0

            @pl.when(touched)
            def _():
                lo = first[pl.ds(here, CHUNK), :]
                hi = last[pl.ds(here, CHUNK), :]
                plus = weight[pl.ds(here, CHUNK), :]
                for c in range(0, columns, 128):
                    value = logits[line, pl.ds(c, 128)] * slope + level
                    col = spot[:, c : c + 128]
                    inside = (col >= lo) & (col < hi)
                    power = jnp.exp2(jnp.where(inside, -value, value))
                    share = jnp.where(inside, plus, sharp) / (1.0 + power)
                    coef[pl.ds(here, CHUNK), pl.ds(c, 128)] = share.astype(BF16)

            @pl.when(jnp.logical_not(touched))
            def _():
                for c in range(0, columns, 128):
                    power = jnp.exp2(logits[line, pl.ds(c, 128)] * slope + level)
                    coef[pl.ds(here, CHUNK), pl.ds(c, 128)] = (sharp / (1.0 + power)).astype(BF16)

            return 0

        lax.fori_loop(0, img_rows // CHUNK, chunk, 0)
        outs.append(moves.start(coef.at[pl.ds(base, img_rows), :], out_coef.at[pl.ds(base, img_rows), :]))
        if j < n_img - 1:
            dz[...] = jnp.dot(coef[pl.ds(base, img_rows), :], zc[...], preferred_element_type=F32)
            for p in range(PARTS):
                back(dz, raw_i, sc_i, base, p * part, part, out_send[j * PARTS + p], along)
    wait_all(outs)


def caption_kernel(lay, coef_in, zi_in, rc_in, sc_in, out_core, out_next, out_own, coef, zi, raw, scales, dz, along, sem):
    n_cap, rows = lay["n_cap"], lay["rows"]
    moves = Copies(sem)
    early = [moves.start(coef_in, coef), moves.start(zi_in, zi)]
    late = [moves.start(rc_in, raw), moves.start(sc_in, scales)]
    wait_all(early)
    dz[...] = contract_first(coef[...], zi[...])
    wait_all(late)
    half = n_cap // 2
    back(dz, raw, scales, 0, 0, half * rows, out_core, along)
    if half > 1:
        back(dz, raw, scales, 0, half * rows, (half - 1) * rows, out_next, along)
    back(dz, raw, scales, 0, (n_cap - 1) * rows, rows, out_own, along)


def image_kernel(lay, coef_in, zc_in, ri_in, si_in, *refs):
    out_own, (coef, zc, raw, scales, dz, along, sem) = refs[:PARTS], refs[PARTS:]
    rows, top = lay["img_rows"], (lay["n_img"] - 1) * lay["img_rows"]
    part = pl.ds(top, rows)
    moves = Copies(sem)
    early = [moves.start(coef_in.at[part, :], coef), moves.start(zc_in, zc)]
    late = [moves.start(ri_in.at[part, :], raw), moves.start(si_in.at[part, :], scales)]
    wait_all(early)
    dz[...] = jnp.dot(coef[...], zc[...], preferred_element_type=F32)
    wait_all(late)
    for p in range(PARTS):
        back(dz, raw, scales, 0, p * (rows // PARTS), rows // PARTS, out_own[p], along)


def whole(*args):
    img_x, cap_x, img_w, cap_w, counts, sharp, shift = args
    n_dp, slots = lax.axis_size("dp"), lax.axis_size("tensor")
    n_y = ROWS_Y
    n_x = n_dp // (n_y * CORES)
    rows = cap_x.shape[0]
    img_rows = img_x.shape[0]
    depth, width = cap_w.shape
    me = lax.axis_index("dp")
    mine = lax.axis_index("tensor")
    core = me % CORES
    pos_x = (me // CORES) % n_x
    pos_y = me // (CORES * n_x)

    def number(y, x, c):
        return (y * n_x + x) * CORES + c

    def from_y(value, k):
        pairs = [
            (number((y + k) % n_y, x, c), number(y, x, c))
            for y in range(n_y)
            for x in range(n_x)
            for c in range(CORES)
        ]
        return lax.ppermute(value, "dp", pairs)

    def from_x(value, k):
        pairs = [
            (number(y, (x + k) % n_x, c), number(y, x, c))
            for y in range(n_y)
            for x in range(n_x)
            for c in range(CORES)
        ]
        return lax.ppermute(value, "dp", pairs)

    def from_core(value):
        return lax.ppermute(value, "dp", [(s, s ^ 1) for s in range(n_dp)])

    def from_z(value, k):
        return lax.ppermute(value, "tensor", [((t + k) % slots, t) for t in range(slots)])

    cap_same = [cap_x] + [from_x(cap_x, k) for k in range(1, n_x)]
    img_all = [from_y(img_x, k) for k in range(1, n_y)] + [img_x]
    cap_other = [from_core(block) for block in cap_same]
    cap_all = cap_other + cap_same[1:] + cap_same[:1]

    n_pc, n_pi = n_x * CORES, n_y * CORES
    step_c, step_i = depth // n_pc, depth // n_pi
    own = jnp.concatenate(
        [
            lax.dynamic_slice_in_dim(cap_w, (pos_x * CORES + core) * step_c, step_c, axis=0),
            lax.dynamic_slice_in_dim(img_w, (pos_y * CORES + core) * step_i, step_i, axis=0),
        ]
    )
    far = slots // 2
    got = {k: from_z(own, k) for k in range(1, slots) if k != far}
    own, _ = lax.optimization_barrier((own, tuple(got.values())))
    got[far] = from_z(own, far)

    cap_pieces, img_pieces = {}, {}
    for k in list(range(1, far)) + list(range(far + 1, slots)) + [far]:
        cap_line = [got[k][:step_c]]
        cap_line += [from_x(cap_line[0], j) for j in range(1, n_x)]
        img_line = [got[k][step_c:]]
        img_line += [from_y(img_line[0], j) for j in range(1, n_y)]
        cap_pieces[k] = cap_line + [from_core(value) for value in cap_line]
        img_pieces[k] = img_line + [from_core(value) for value in img_line]
    cap_pieces = [piece for k in range(1, slots) for piece in cap_pieces[k]]
    img_pieces = [piece for k in range(1, slots) for piece in img_pieces[k]]

    def places(n_line, pos, step):
        return [((pos + j) % n_line * CORES + c) * step for c in (core, 1 - core) for j in range(n_line)]

    place = jnp.stack(places(n_x, pos_x, step_c) + places(n_y, pos_y, step_i)).astype(jnp.int32)

    ends = jnp.cumsum(counts)
    starts = ends - counts

    def of_image(values):
        blocks = []
        for k in list(range(1, n_y)) + [0]:
            owner = number((pos_y + k) % n_y, pos_x, core)
            blocks.append(lax.dynamic_slice_in_dim(values, owner * img_rows, img_rows))
        return jnp.concatenate(blocks)[:, None]

    first = of_image(starts)
    last = of_image(ends)
    weight = -sharp[0] / of_image(counts).astype(F32)
    order = [(k, 1 - core) for k in range(n_x)] + [(k, core) for k in range(1, n_x)] + [(0, core)]
    heads = [(number(pos_y, (pos_x + k) % n_x, c) * slots + mine) * rows for k, c in order]
    position = jnp.concatenate([head + jnp.arange(rows, dtype=jnp.int32) for head in heads])[None, :]
    low, high = first[::CHUNK, 0], last[CHUNK - 1 :: CHUNK, 0]
    touched = functools.reduce(jnp.logical_or, [(low < head + rows) & (high > head) for head in heads])
    place = jnp.concatenate([place, touched.astype(jnp.int32)])
    factors = jnp.concatenate([sharp, shift])

    n_cap, n_img = n_x * CORES, n_y
    lay = dict(n_cap=n_cap, n_img=n_img, rows=rows, img_rows=img_rows, n_pc=n_pc, n_pi=n_pi, slots=slots, width=width)
    full = slots * width
    c_rows, i_rows = n_cap * rows, n_img * img_rows
    hbm = pl.BlockSpec(memory_space=pltpu.HBM)
    vmem = pl.BlockSpec(memory_space=pltpu.VMEM)
    smem = pl.BlockSpec(memory_space=pltpu.SMEM)

    def of(shape, dtype):
        return jax.ShapeDtypeStruct(shape, dtype)

    def params(mib):
        return pltpu.CompilerParams(vmem_limit_bytes=mib * 2**20)

    def cost(flops, mib):
        return pl.CostEstimate(flops=flops, bytes_accessed=mib * 2**20, transcendentals=0)

    pair = 2 * c_rows * i_rows * full
    operands = [place] + cap_all + img_all + [cap_w] + cap_pieces + [img_w] + img_pieces
    specs = [smem] + [hbm] * (len(operands) - 1) + [vmem] * 4 + [smem]
    operands += [first, last, weight, position, factors]
    n_copies = 2 + (slots - 1) * (n_pc + n_pi) + n_cap + n_img + 8 + n_img
    shared = (
        of((i_rows, c_rows), BF16),
        of((c_rows, full), BF16),
        of((i_rows, full), BF16),
        of((c_rows, full), F32),
        of((i_rows, full), F32),
        of((c_rows, 128), F32),
        of((i_rows, 128), F32),
        of((depth, full), BF16),
        of((depth, full), BF16),
    )
    half = img_rows // PARTS
    n_send = (n_y - 1) * PARTS
    made = pl.pallas_call(
        functools.partial(pair_kernel, lay),
        out_shape=tuple(of((half, full), BF16) for _ in range(n_send)) + shared,
        in_specs=specs,
        out_specs=[vmem] * n_send + [hbm] * len(shared),
        scratch_shapes=[
            pltpu.VMEM((c_rows, depth), BF16),
            pltpu.VMEM((i_rows, depth), BF16),
            pltpu.VMEM((c_rows, full), BF16),
            pltpu.VMEM((i_rows, full), BF16),
            pltpu.VMEM((c_rows, full), F32),
            pltpu.VMEM((i_rows, full), F32),
            pltpu.VMEM((c_rows, 128), F32),
            pltpu.VMEM((i_rows, 128), F32),
            pltpu.VMEM((depth, full), BF16),
            pltpu.VMEM((depth, full), BF16),
            pltpu.VMEM((img_rows, c_rows), F32),
            pltpu.VMEM((i_rows, c_rows), BF16),
            pltpu.VMEM((img_rows, full), F32),
            pltpu.VMEM((img_rows, 128), F32),
            pltpu.SemaphoreType.DMA((n_copies,)),
        ],
        compiler_params=params(60),
        cost_estimate=cost((c_rows + i_rows) * depth * full * 2 + pair * 3 // 2, 30),
        name="pairs",
    )(*operands)

    img_send = made[:n_send]
    coef, zc, zi, raw_c, raw_i, sc_c, sc_i, wc, wi = made[n_send:]

    img_sent = [
        [from_y(img_send[(k - 1) * PARTS + p], n_y - k) for k in range(1, n_y)] for p in range(PARTS)
    ]

    cap_core, cap_next, cap_own = pl.pallas_call(
        functools.partial(caption_kernel, lay),
        out_shape=(
            of((n_x * rows, full), BF16),
            of((max(n_x - 1, 1) * rows, full), F32),
            of((rows, full), F32),
        ),
        in_specs=[hbm] * 4,
        out_specs=[vmem] * 3,
        scratch_shapes=[
            pltpu.VMEM((i_rows, c_rows), BF16),
            pltpu.VMEM((i_rows, full), BF16),
            pltpu.VMEM((c_rows, full), F32),
            pltpu.VMEM((c_rows, 128), F32),
            pltpu.VMEM((c_rows, full), F32),
            pltpu.VMEM((c_rows, 128), F32),
            pltpu.SemaphoreType.DMA((4,)),
        ],
        compiler_params=params(60),
        cost_estimate=cost(pair, 20),
        name="captions",
    )(coef, zi, raw_c, sc_c)
    crossed = from_core(cap_core)

    img_own = pl.pallas_call(
        functools.partial(image_kernel, lay),
        out_shape=[of((half, full), F32)] * PARTS,
        in_specs=[hbm] * 4,
        out_specs=[vmem] * PARTS,
        scratch_shapes=[
            pltpu.VMEM((img_rows, c_rows), BF16),
            pltpu.VMEM((c_rows, full), BF16),
            pltpu.VMEM((img_rows, full), F32),
            pltpu.VMEM((img_rows, 128), F32),
            pltpu.VMEM((img_rows, full), F32),
            pltpu.VMEM((img_rows, 128), F32),
            pltpu.SemaphoreType.DMA((4,)),
        ],
        compiler_params=params(60),
        cost_estimate=cost(pair // n_img, 8),
        name="images",
    )(coef, zc, raw_i, sc_i)

    cap_total = cap_own + crossed[:rows].astype(F32)
    for k in range(1, n_x):
        sent = cap_next[(k - 1) * rows : k * rows] + crossed[k * rows : (k + 1) * rows].astype(F32)
        cap_total = cap_total + from_x(sent.astype(BF16), n_x - k).astype(F32)
    grad_cap = contract_last(cap_total.astype(BF16), wc).astype(BF16)

    share = depth // slots
    grad_img = []
    for p in range(PARTS):
        img_total = img_own[p]
        for arrived in img_sent[p]:
            img_total = img_total + arrived.astype(F32)
        img_part = contract_last(img_total.astype(BF16), wi)

        def columns_of(k):
            return lax.dynamic_slice_in_dim(img_part, (mine + k) % slots * share, share, axis=1)

        arrived = [from_z(columns_of(slots - k).astype(BF16), k) for k in range(1, slots)]
        grad_img.append(functools.reduce(lambda a, b: a + b.astype(F32), arrived, columns_of(0)).astype(BF16))
    return (jnp.concatenate(grad_img), grad_cap)


def solution(mesh):
    in_specs = (
        P("dp", None),
        P(("dp", "tensor"), None),
        P(None, "tensor"),
        P(None, "tensor"),
        P(),
        P(),
        P(),
    )
    out_specs = (P("dp", "tensor"), P(("dp", "tensor"), None))
    return jax.shard_map(whole, mesh=mesh, in_specs=in_specs, out_specs=out_specs, check_vma=False)
```

profile of v0, /device:TPU:0, one launch (start us, length us, event | category | flops | bytes accessed | tf_op | source)
XLA Modules:
  0.0 131.4 jit_solution(9728353032739633343)
XLA Ops:
  1.7 5.1 %collective-permute-start.4 = (bf16[512,256]{1,0:T(8,128)(2,1)S(1)}, bf16[512,256]{1,0:T(8,128)(2,1)S(1)}, u32[]{:S(2)}, u32[]{:S(2)}) collective-permute-start(bf16[512,256]{1,0:T(8,128)(2,1)S(1)} %pad_maximum_fusion), channel_id=1, source_target_pairs={{1,0},{2,1},{3,2},{0,3},{5,4},{6,5},{7,6},{4,7},{9,8},{10,9},{11,1... | collective-permute-start | bytes 786440 | tf_op jit(solution)/shard_map/ppermute | solution.py:262
  6.9 1.5 %collective-permute-start.1 = (bf16[352,1024]{1,0:T(8,128)(2,1)}, bf16[352,1024]{1,0:T(8,128)(2,1)}, u32[]{:S(2)}, u32[]{:S(2)}) collective-permute-start(bf16[352,1024]{1,0:T(8,128)(2,1)} %refs_4_.1), channel_id=1, source_target_pairs={{8,0},{12,4},{0,8},{4,12},{24,16},{28,20},{16,24},{20,28},{9,1},{1... | collective-permute-start | bytes 2162696 | tf_op jit(solution)/shard_map/ppermute | solution.py:256
  10.4 8.6 %collective-permute-done.8 = bf16[512,256]{1,0:T(8,128)(2,1)S(1)} collective-permute-done((bf16[512,256]{1,0:T(8,128)(2,1)S(1)}, bf16[512,256]{1,0:T(8,128)(2,1)S(1)}, u32[]{:S(2)}, u32[]{:S(2)}) %collective-permute-start.8) | collective-permute-done | bytes 262176 | tf_op jit(solution)/shard_map/ppermute | solution.py:262
  19.0 1.6 %collective-permute-start.13 = (bf16[256,256]{1,0:T(8,128)(2,1)S(1)}, bf16[256,256]{1,0:T(8,128)(2,1)S(1)}, u32[]{:S(2)}, u32[]{:S(2)}) collective-permute-start(bf16[256,256]{1,0:T(8,128)(2,1)S(1)} %get-tuple-element.45.refs_16_), channel_id=1, source_target_pairs={{8,0},{12,4},{0,8},{4,12},{24,16},{28,20},{16,24},{20,28},{9,1},{1... | collective-permute-start | bytes 393224 | tf_op jit(solution)/shard_map/ppermute | solution.py:256
  20.6 1.6 %collective-permute-start.16 = (bf16[256,256]{1,0:T(8,128)(2,1)S(1)}, bf16[256,256]{1,0:T(8,128)(2,1)S(1)}, u32[]{:S(2)}, u32[]{:S(2)}) collective-permute-start(bf16[256,256]{1,0:T(8,128)(2,1)S(1)} %get-tuple-element.48.refs_21_), channel_id=1, source_target_pairs={{16,0},{20,4},{24,8},{28,12},{0,16},{4,20},{8,24},{12,28},{17,1},{... | collective-permute-start | bytes 393224 | tf_op jit(solution)/shard_map/ppermute | solution.py:247
  22.9 4.6 %collective-permute-done.13.refs_17_ = bf16[256,256]{1,0:T(8,128)(2,1)S(1)} collective-permute-done((bf16[256,256]{1,0:T(8,128)(2,1)S(1)}, bf16[256,256]{1,0:T(8,128)(2,1)S(1)}, u32[]{:S(2)}, u32[]{:S(2)}) %collective-permute-start.13) | collective-permute-done | bytes 131104 | tf_op jit(solution)/shard_map/ppermute | solution.py:256
  27.5 1.5 %collective-permute-start.5 = (bf16[256,256]{1,0:T(8,128)(2,1)S(1)}, bf16[256,256]{1,0:T(8,128)(2,1)S(1)}, u32[]{:S(2)}, u32[]{:S(2)}) collective-permute-start(bf16[256,256]{1,0:T(8,128)(2,1)S(1)} %get-tuple-element.49.refs_8_), channel_id=1, source_target_pairs={{8,0},{12,4},{0,8},{4,12},{24,16},{28,20},{16,24},{20,28},{9,1},{1... | collective-permute-start | bytes 393224 | tf_op jit(solution)/shard_map/ppermute | solution.py:256
  30.8 1.7 %collective-permute-done.5.refs_9_ = bf16[256,256]{1,0:T(8,128)(2,1)S(1)} collective-permute-done((bf16[256,256]{1,0:T(8,128)(2,1)S(1)}, bf16[256,256]{1,0:T(8,128)(2,1)S(1)}, u32[]{:S(2)}, u32[]{:S(2)}) %collective-permute-start.5) | collective-permute-done | bytes 131104 | tf_op jit(solution)/shard_map/ppermute | solution.py:256
  34.9 8.2 %collective-permute-done.9 = bf16[512,256]{1,0:T(8,128)(2,1)S(1)} collective-permute-done((bf16[512,256]{1,0:T(8,128)(2,1)S(1)}, bf16[512,256]{1,0:T(8,128)(2,1)S(1)}, u32[]{:S(2)}, u32[]{:S(2)}) %collective-permute-start.9) | collective-permute-done | bytes 262176 | tf_op jit(solution)/shard_map/ppermute | solution.py:262
  43.8 1.6 %collective-permute-start.3 = (bf16[352,1024]{1,0:T(8,128)(2,1)S(1)}, bf16[352,1024]{1,0:T(8,128)(2,1)}, u32[]{:S(2)}, u32[]{:S(2)}) collective-permute-start(bf16[352,1024]{1,0:T(8,128)(2,1)S(1)} %copy-done.11), channel_id=1, source_target_pairs={{16,0},{20,4},{24,8},{28,12},{0,16},{4,20},{8,24},{12,28},{17,1},{... | collective-permute-start | bytes 2162696 | tf_op jit(solution)/shard_map/ppermute | solution.py:247
  47.2 3.3 %collective-permute-done.10.refs_13_ = bf16[256,256]{1,0:T(8,128)(2,1)S(1)} collective-permute-done((bf16[256,256]{1,0:T(8,128)(2,1)S(1)}, bf16[256,256]{1,0:T(8,128)(2,1)S(1)}, u32[]{:S(2)}, u32[]{:S(2)}) %collective-permute-start.10) | collective-permute-done | bytes 131104 | tf_op jit(solution)/shard_map/ppermute | solution.py:256
  50.5 14.3 %collective-permute-done.19.refs_26_ = bf16[256,256]{1,0:T(8,128)(2,1)} collective-permute-done((bf16[256,256]{1,0:T(8,128)(2,1)S(1)}, bf16[256,256]{1,0:T(8,128)(2,1)}, u32[]{:S(2)}, u32[]{:S(2)}) %collective-permute-start.19) | collective-permute-done | bytes 131104 | tf_op jit(solution)/shard_map/ppermute | solution.py:247
  70.9 18.8 %pairs.1 = (bf16[176,1024]{1,0:T(8,128)(2,1)}, bf16[176,1024]{1,0:T(8,128)(2,1)}, bf16[704,1408]{1,0:T(8,128)(2,1)}, bf16[1408,1024]{1,0:T(8,128)(2,1)}, bf16[70...) custom-call(s32[30]{0:T(128)} %concatenate.37.refs_0_, ...), custom_call_target="tpu_custom_call" | custom-call | flops 7474249728 | bytes 31457280 | tf_op jit(solution)/shard_map/pairs/pallas_call | solution.py:354
  89.7 7.3 %captions.1 = (bf16[704,1024]{1,0:T(8,128)(2,1)}, f32[352,1024]{1,0:T(8,128)}, f32[352,1024]{1,0:T(8,128)}) custom-call(bf16[704,1408]{1,0:T(8,128)(2,1)} %get-tuple-element.20.coef_in, bf16[704,1024]{1,0:T(8,128)(2,1)} %get-tuple-element.29.zi_in, f32[1408,1024]{1,0:T(8,128)} %get-tuple-element.30.rc_in, f32[1408,128]{1,0:T(8,128)} %get-tuple-element.31.sc_in), custom_call_target="tpu_custom_call" | custom-call | flops 2030043136 | bytes 20971520 | tf_op jit(solution)/shard_map/captions/pallas_call | solution.py:388
  97.5 1.5 %collective-permute-start.25 = (bf16[176,1024]{1,0:T(8,128)(2,1)}, bf16[176,1024]{1,0:T(8,128)(2,1)S(1)}, u32[]{:S(2)}, u32[]{:S(2)}) collective-permute-start(bf16[176,1024]{1,0:T(8,128)(2,1)} %get-tuple-element.25), channel_id=1, source_target_pairs={{16,0},{20,4},{24,8},{28,12},{0,16},{4,20},{8,24},{12,28},{17,1},{... | collective-permute-start | bytes 1081352 | tf_op jit(solution)/shard_map/ppermute | solution.py:247
  99.5 5.1 %images.1 = (f32[176,1024]{1,0:T(8,128)}, f32[176,1024]{1,0:T(8,128)}) custom-call(bf16[704,1408]{1,0:T(8,128)(2,1)} %get-tuple-element.20.coef_in, bf16[1408,1024]{1,0:T(8,128)(2,1)} %get-tuple-element.21.zc_in, f32[704,1024]{1,0:T(8,128)} %get-tuple-element.22.ri_in, f32[704,128]{1,0:T(8,128)} %get-tuple-element.23.si_in), custom_call_target="tpu_custom_call" | custom-call | flops 1015021568 | bytes 8388608 | tf_op jit(solution)/shard_map/images/pallas_call | solution.py:412
  104.6 4.4 %collective-permute-done.25 = bf16[176,1024]{1,0:T(8,128)(2,1)S(1)} collective-permute-done((bf16[176,1024]{1,0:T(8,128)(2,1)}, bf16[176,1024]{1,0:T(8,128)(2,1)S(1)}, u32[]{:S(2)}, u32[]{:S(2)}) %collective-permute-start.25) | collective-permute-done | bytes 360480 | tf_op jit(solution)/shard_map/ppermute | solution.py:247
  109.0 2.1 %fusion.1 = f32[176,1024]{1,0:T(8,128)S(1)} fusion(bf16[1024,1024]{1,0:T(8,128)(2,1)S(1)} %copy-done, f32[176,1024]{1,0:T(8,128)} %get-tuple-element.24, bf16[176,1024]{1,0:T(8,128)(2,1)S(1)} %collective-permute-done.25), kind=kOutput, calls=%fused_computation.6 | convolution fusion | flops 369639424 | bytes 3899392 | tf_op jit(solution)/shard_map/dot_general | solution.py:22
  114.0 2.0 %collective-permute-done.29 = bf16[176,1024]{1,0:T(8,128)(2,1)} collective-permute-done((bf16[176,1024]{1,0:T(8,128)(2,1)}, bf16[176,1024]{1,0:T(8,128)(2,1)}, u32[]{:S(2)}, u32[]{:S(2)}) %collective-permute-start.29) | collective-permute-done | bytes 360480 | tf_op jit(solution)/shard_map/ppermute | solution.py:247
  116.0 2.0 %fusion.2 = f32[176,1024]{1,0:T(8,128)S(1)} fusion(bf16[1024,1024]{1,0:T(8,128)(2,1)S(1)} %copy-done, f32[176,1024]{1,0:T(8,128)S(1)} %copy-done.2, bf16[176,1024]{1,0:T(8,128)(2,1)} %collective-permute-done.29), kind=kOutput, calls=%fused_computation.7 | convolution fusion | flops 369639424 | bytes 3899392 | tf_op jit(solution)/shard_map/dot_general | solution.py:22
  118.0 1.4 %collective-permute-start.30 = (bf16[176,256]{1,0:T(8,128)(2,1)S(1)}, bf16[176,256]{1,0:T(8,128)(2,1)S(1)}, u32[]{:S(2)}, u32[]{:S(2)}) collective-permute-start(bf16[176,256]{1,0:T(8,128)(2,1)S(1)} %get-tuple-element.41), channel_id=1, source_target_pairs={{1,0},{2,1},{3,2},{0,3},{5,4},{6,5},{7,6},{4,7},{9,8},{10,9},{11,1... | collective-permute-start | bytes 270344 | tf_op jit(solution)/shard_map/ppermute | solution.py:262
  121.4 1.5 %collective-permute-done.30 = bf16[176,256]{1,0:T(8,128)(2,1)S(1)} collective-permute-done((bf16[176,256]{1,0:T(8,128)(2,1)S(1)}, bf16[176,256]{1,0:T(8,128)(2,1)S(1)}, u32[]{:S(2)}, u32[]{:S(2)}) %collective-permute-start.30) | collective-permute-done | bytes 90144 | tf_op jit(solution)/shard_map/ppermute | solution.py:262
  122.9 5.9 %collective-permute-done.31 = bf16[176,256]{1,0:T(8,128)(2,1)S(1)} collective-permute-done((bf16[176,256]{1,0:T(8,128)(2,1)S(1)}, bf16[176,256]{1,0:T(8,128)(2,1)S(1)}, u32[]{:S(2)}, u32[]{:S(2)}) %collective-permute-start.31) | collective-permute-done | bytes 90144 | tf_op jit(solution)/shard_map/ppermute | solution.py:262
  129.5 1.9 %convolution_convert_fusion = bf16[352,1024]{1,0:T(8,128)(2,1)} fusion(bf16[1024,1024]{1,0:T(8,128)(2,1)S(1)} %copy-done.24, bf16[352,1024]{1,0:T(8,128)(2,1)S(1)} %collective-permute-done.34, f32[352,1024]{1,0:T(8,128)S(1)} %copy-done.9, bf16[704,1024]{1,0:T(8,128)(2,1)S(1)} %collective-permute-done.33), kind=kOutput, calls=%fused_computation.2 | convolution fusion | flops 740360192 | bytes 5701632 | tf_op jit(solution)/shard_map/dot_general | solution.py:22
  (140 shorter events, 21.6 us)
Async XLA Ops:
  1.7 18.8 %collective-permute-start.4 = (bf16[512,256]{1,0:T(8,128)(2,1)S(1)}, bf16[512,256]{1,0:T(8,128)(2,1)S(1)}, u32[]{:S(2)}, u32[]{:S(2)}) collective-permute-start(bf16[512,256]{1,0:T(8,128)(2,1)S(1)} %pad_maximum_fusion), channel_id=1, source_target_pairs={{1,0},{2,1},{3,2},{0,3},{5,4},{6,5},{7,6},{4,7},{9,8},{10,9},{11,1... | collective-permute-start | bytes 786440 | tf_op jit(solution)/shard_map/ppermute | solution.py:262
  6.9 12.1 %collective-permute-start.8 = (bf16[512,256]{1,0:T(8,128)(2,1)S(1)}, bf16[512,256]{1,0:T(8,128)(2,1)S(1)}, u32[]{:S(2)}, u32[]{:S(2)}) collective-permute-start(bf16[512,256]{1,0:T(8,128)(2,1)S(1)} %pad_maximum_fusion), channel_id=1, source_target_pairs={{3,0},{0,1},{1,2},{2,3},{7,4},{4,5},{5,6},{6,7},{11,8},{8,9},{9,10... | collective-permute-start | bytes 786440 | tf_op jit(solution)/shard_map/ppermute | solution.py:262
  6.9 39.5 %collective-permute-start.1 = (bf16[352,1024]{1,0:T(8,128)(2,1)}, bf16[352,1024]{1,0:T(8,128)(2,1)}, u32[]{:S(2)}, u32[]{:S(2)}) collective-permute-start(bf16[352,1024]{1,0:T(8,128)(2,1)} %refs_4_.1), channel_id=1, source_target_pairs={{8,0},{12,4},{0,8},{4,12},{24,16},{28,20},{16,24},{20,28},{9,1},{1... | collective-permute-start | bytes 2162696 | tf_op jit(solution)/shard_map/ppermute | solution.py:256
  19.0 8.5 %collective-permute-start.13 = (bf16[256,256]{1,0:T(8,128)(2,1)S(1)}, bf16[256,256]{1,0:T(8,128)(2,1)S(1)}, u32[]{:S(2)}, u32[]{:S(2)}) collective-permute-start(bf16[256,256]{1,0:T(8,128)(2,1)S(1)} %get-tuple-element.45.refs_16_), channel_id=1, source_target_pairs={{8,0},{12,4},{0,8},{4,12},{24,16},{28,20},{16,24},{20,28},{9,1},{1... | collective-permute-start | bytes 393224 | tf_op jit(solution)/shard_map/ppermute | solution.py:256
  20.6 9.2 %collective-permute-start.16 = (bf16[256,256]{1,0:T(8,128)(2,1)S(1)}, bf16[256,256]{1,0:T(8,128)(2,1)S(1)}, u32[]{:S(2)}, u32[]{:S(2)}) collective-permute-start(bf16[256,256]{1,0:T(8,128)(2,1)S(1)} %get-tuple-element.48.refs_21_), channel_id=1, source_target_pairs={{16,0},{20,4},{24,8},{28,12},{0,16},{4,20},{8,24},{12,28},{17,1},{... | collective-permute-start | bytes 393224 | tf_op jit(solution)/shard_map/ppermute | solution.py:247
  22.3 10.2 %collective-permute-start.14 = (bf16[256,256]{1,0:T(8,128)(2,1)S(1)}, bf16[256,256]{1,0:T(8,128)(2,1)S(1)}, u32[]{:S(2)}, u32[]{:S(2)}) collective-permute-start(bf16[256,256]{1,0:T(8,128)(2,1)S(1)} %get-tuple-element.45.refs_16_), channel_id=1, source_target_pairs={{0,4},{4,0},{8,12},{12,8},{16,20},{20,16},{24,28},{28,24},{1,5},{5... | collective-permute-start | bytes 393224 | tf_op jit(solution)/shard_map/ppermute | solution.py:259
  22.3 8.4 %collective-permute-start.22 = (bf16[256,256]{1,0:T(8,128)(2,1)S(1)}, bf16[256,256]{1,0:T(8,128)(2,1)S(1)}, u32[]{:S(2)}, u32[]{:S(2)}) collective-permute-start(bf16[256,256]{1,0:T(8,128)(2,1)S(1)} %get-tuple-element.44.refs_29_), channel_id=1, source_target_pairs={{16,0},{20,4},{24,8},{28,12},{0,16},{4,20},{8,24},{12,28},{17,1},{... | collective-permute-start | bytes 393224 | tf_op jit(solution)/shard_map/ppermute | solution.py:247
  29.8 13.3 %collective-permute-start.9 = (bf16[512,256]{1,0:T(8,128)(2,1)S(1)}, bf16[512,256]{1,0:T(8,128)(2,1)S(1)}, u32[]{:S(2)}, u32[]{:S(2)}) collective-permute-start(bf16[512,256]{1,0:T(8,128)(2,1)S(1)} %pad_maximum_fusion), channel_id=1, source_target_pairs={{2,0},{3,1},{0,2},{1,3},{6,4},{7,5},{4,6},{5,7},{10,8},{11,9},{8,1... | collective-permute-start | bytes 786440 | tf_op jit(solution)/shard_map/ppermute | solution.py:262
  34.2 8.9 %collective-permute-start.15 = (bf16[256,256]{1,0:T(8,128)(2,1)S(1)}, bf16[256,256]{1,0:T(8,128)(2,1)S(1)}, u32[]{:S(2)}, u32[]{:S(2)}) collective-permute-start(bf16[256,256]{1,0:T(8,128)(2,1)S(1)} %collective-permute-done.13.refs_17_), channel_id=1, source_target_pairs={{0,4},{4,0},{8,12},{12,8},{16,20},{20,16},{24,28},{28,24},{1,5},{5... | collective-permute-start | bytes 393224 | tf_op jit(solution)/shard_map/ppermute | solution.py:259
  34.4 9.4 %collective-permute-start.18 = (bf16[256,256]{1,0:T(8,128)(2,1)S(1)}, bf16[256,256]{1,0:T(8,128)(2,1)S(1)}, u32[]{:S(2)}, u32[]{:S(2)}) collective-permute-start(bf16[256,256]{1,0:T(8,128)(2,1)S(1)} %collective-permute-done.16.refs_22_), channel_id=1, source_target_pairs={{0,4},{4,0},{8,12},{12,8},{16,20},{20,16},{24,28},{28,24},{1,5},{5... | collective-permute-start | bytes 393224 | tf_op jit(solution)/shard_map/ppermute | solution.py:259
  34.8 10.5 %collective-permute-start.24 = (bf16[256,256]{1,0:T(8,128)(2,1)S(1)}, bf16[256,256]{1,0:T(8,128)(2,1)S(1)}, u32[]{:S(2)}, u32[]{:S(2)}) collective-permute-start(bf16[256,256]{1,0:T(8,128)(2,1)S(1)} %collective-permute-done.22.refs_30_), channel_id=1, source_target_pairs={{0,4},{4,0},{8,12},{12,8},{16,20},{20,16},{24,28},{28,24},{1,5},{5... | collective-permute-start | bytes 393224 | tf_op jit(solution)/shard_map/ppermute | solution.py:259
  43.2 27.6 %collective-permute-start = (bf16[352,1024]{1,0:T(8,128)(2,1)S(1)}, bf16[352,1024]{1,0:T(8,128)(2,1)}, u32[]{:S(2)}, u32[]{:S(2)}) collective-permute-start(bf16[352,1024]{1,0:T(8,128)(2,1)S(1)} %copy-done.10), channel_id=1, source_target_pairs={{0,4},{4,0},{8,12},{12,8},{16,20},{20,16},{24,28},{28,24},{1,5},{5... | collective-permute-start | bytes 2162696 | tf_op jit(solution)/shard_map/ppermute | solution.py:259
  43.8 27.0 %collective-permute-start.3 = (bf16[352,1024]{1,0:T(8,128)(2,1)S(1)}, bf16[352,1024]{1,0:T(8,128)(2,1)}, u32[]{:S(2)}, u32[]{:S(2)}) collective-permute-start(bf16[352,1024]{1,0:T(8,128)(2,1)S(1)} %copy-done.11), channel_id=1, source_target_pairs={{16,0},{20,4},{24,8},{28,12},{0,16},{4,20},{8,24},{12,28},{17,1},{... | collective-permute-start | bytes 2162696 | tf_op jit(solution)/shard_map/ppermute | solution.py:247
  45.9 18.9 %collective-permute-start.19 = (bf16[256,256]{1,0:T(8,128)(2,1)S(1)}, bf16[256,256]{1,0:T(8,128)(2,1)}, u32[]{:S(2)}, u32[]{:S(2)}) collective-permute-start(bf16[256,256]{1,0:T(8,128)(2,1)S(1)} %get-tuple-element.46.refs_25_), channel_id=1, source_target_pairs={{16,0},{20,4},{24,8},{28,12},{0,16},{4,20},{8,24},{12,28},{17,1},{... | collective-permute-start | bytes 393224 | tf_op jit(solution)/shard_map/ppermute | solution.py:247
  46.4 24.4 %collective-permute-start.2 = (bf16[352,1024]{1,0:T(8,128)(2,1)}, bf16[352,1024]{1,0:T(8,128)(2,1)}, u32[]{:S(2)}, u32[]{:S(2)}) collective-permute-start(bf16[352,1024]{1,0:T(8,128)(2,1)} %collective-permute-done.1.refs_3_), channel_id=1, source_target_pairs={{0,4},{4,0},{8,12},{12,8},{16,20},{20,16},{24,28},{28,24},{1,5},{5... | collective-permute-start | bytes 2162696 | tf_op jit(solution)/shard_map/ppermute | solution.py:259
  50.5 14.3 %collective-permute-start.11 = (bf16[256,256]{1,0:T(8,128)(2,1)S(1)}, bf16[256,256]{1,0:T(8,128)(2,1)S(1)}, u32[]{:S(2)}, u32[]{:S(2)}) collective-permute-start(bf16[256,256]{1,0:T(8,128)(2,1)S(1)} %get-tuple-element.47.refs_12_), channel_id=1, source_target_pairs={{0,4},{4,0},{8,12},{12,8},{16,20},{20,16},{24,28},{28,24},{1,5},{5... | collective-permute-start | bytes 393224 | tf_op jit(solution)/shard_map/ppermute | solution.py:259
  97.0 16.1 %collective-permute-start.33 = (bf16[704,1024]{1,0:T(8,128)(2,1)}, bf16[704,1024]{1,0:T(8,128)(2,1)S(1)}, u32[]{:S(2)}, u32[]{:S(2)}) collective-permute-start(bf16[704,1024]{1,0:T(8,128)(2,1)} %get-tuple-element.33), channel_id=1, source_target_pairs={{0,4},{4,0},{8,12},{12,8},{16,20},{20,16},{24,28},{28,24},{1,5},{5... | collective-permute-start | bytes 4325384 | tf_op jit(solution)/shard_map/ppermute | solution.py:259
  97.5 11.5 %collective-permute-start.25 = (bf16[176,1024]{1,0:T(8,128)(2,1)}, bf16[176,1024]{1,0:T(8,128)(2,1)S(1)}, u32[]{:S(2)}, u32[]{:S(2)}) collective-permute-start(bf16[176,1024]{1,0:T(8,128)(2,1)} %get-tuple-element.25), channel_id=1, source_target_pairs={{16,0},{20,4},{24,8},{28,12},{0,16},{4,20},{8,24},{12,28},{17,1},{... | collective-permute-start | bytes 1081352 | tf_op jit(solution)/shard_map/ppermute | solution.py:247
  99.0 17.0 %collective-permute-start.29 = (bf16[176,1024]{1,0:T(8,128)(2,1)}, bf16[176,1024]{1,0:T(8,128)(2,1)}, u32[]{:S(2)}, u32[]{:S(2)}) collective-permute-start(bf16[176,1024]{1,0:T(8,128)(2,1)} %get-tuple-element.28), channel_id=1, source_target_pairs={{16,0},{20,4},{24,8},{28,12},{0,16},{4,20},{8,24},{12,28},{17,1},{... | collective-permute-start | bytes 1081352 | tf_op jit(solution)/shard_map/ppermute | solution.py:247
  111.1 8.4 %collective-permute-start.26 = (bf16[176,256]{1,0:T(8,128)(2,1)S(1)}, bf16[176,256]{1,0:T(8,128)(2,1)S(1)}, u32[]{:S(2)}, u32[]{:S(2)}) collective-permute-start(bf16[176,256]{1,0:T(8,128)(2,1)S(1)} %get-tuple-element.38), channel_id=1, source_target_pairs={{1,0},{2,1},{3,2},{0,3},{5,4},{6,5},{7,6},{4,7},{9,8},{10,9},{11,1... | collective-permute-start | bytes 270344 | tf_op jit(solution)/shard_map/ppermute | solution.py:262
  112.4 8.4 %collective-permute-start.27 = (bf16[176,256]{1,0:T(8,128)(2,1)S(1)}, bf16[176,256]{1,0:T(8,128)(2,1)S(1)}, u32[]{:S(2)}, u32[]{:S(2)}) collective-permute-start(bf16[176,256]{1,0:T(8,128)(2,1)S(1)} %get-tuple-element.40), channel_id=1, source_target_pairs={{2,0},{3,1},{0,2},{1,3},{6,4},{7,5},{4,6},{5,7},{10,8},{11,9},{8,1... | collective-permute-start | bytes 270344 | tf_op jit(solution)/shard_map/ppermute | solution.py:262
  112.4 9.0 %collective-permute-start.28 = (bf16[176,256]{1,0:T(8,128)(2,1)S(1)}, bf16[176,256]{1,0:T(8,128)(2,1)S(1)}, u32[]{:S(2)}, u32[]{:S(2)}) collective-permute-start(bf16[176,256]{1,0:T(8,128)(2,1)S(1)} %get-tuple-element.39), channel_id=1, source_target_pairs={{3,0},{0,1},{1,2},{2,3},{7,4},{4,5},{5,6},{6,7},{11,8},{8,9},{9,10... | collective-permute-start | bytes 270344 | tf_op jit(solution)/shard_map/ppermute | solution.py:262
  113.4 16.1 %collective-permute-start.34 = (bf16[352,1024]{1,0:T(8,128)(2,1)S(1)}, bf16[352,1024]{1,0:T(8,128)(2,1)S(1)}, u32[]{:S(2)}, u32[]{:S(2)}) collective-permute-start(bf16[352,1024]{1,0:T(8,128)(2,1)S(1)} %add_convert_fusion.1), channel_id=1, source_target_pairs={{8,0},{12,4},{0,8},{4,12},{24,16},{28,20},{16,24},{20,28},{9,1},{1... | collective-permute-start | bytes 2162696 | tf_op jit(solution)/shard_map/ppermute | solution.py:256
  119.5 9.3 %collective-permute-start.31 = (bf16[176,256]{1,0:T(8,128)(2,1)S(1)}, bf16[176,256]{1,0:T(8,128)(2,1)S(1)}, u32[]{:S(2)}, u32[]{:S(2)}) collective-permute-start(bf16[176,256]{1,0:T(8,128)(2,1)S(1)} %get-tuple-element.43), channel_id=1, source_target_pairs={{2,0},{3,1},{0,2},{1,3},{6,4},{7,5},{4,6},{5,7},{10,8},{11,9},{8,1... | collective-permute-start | bytes 270344 | tf_op jit(solution)/shard_map/ppermute | solution.py:262
  (36 other events, 744.3 us)
where the time goes:
time: 132 us; the launch traced here: 131 us
  waiting for transfers between devices  55.4 us (42%)
  Pallas kernels  31.2 us (24%)
  starting transfers between devices  25.9 us (20%)
  local copies, waits for them, and re-layouts  5.93 us (4%)
  matrix products  5.93 us (4%)
  other arithmetic  4.53 us (3%)
  between operations  2.46 us (2%)
    ppermute x9, waiting for transfers between devices, from_z(): lax.ppermute(value, 'tensor', [((t + k) % slots, t) for t in range(slots)])  24.3 us
    ppermute x6, waiting for transfers between devices, from_y(): return lax.ppermute(value, 'dp', pairs)  20.7 us
    pallas_call x1, Pallas kernels, whole(): pl.pallas_call(functools.partial(pair_kernel, lay), out_shape=tuple((of((...  18.8 us
    ppermute x9, starting transfers between devices, from_z(): lax.ppermute(value, 'tensor', [((t + k) % slots, t) for t in range(slots)])  11.1 us
    ppermute x5, waiting for transfers between devices, from_x(): return lax.ppermute(value, 'dp', pairs)  9.64 us
    pallas_call x1, Pallas kernels, whole(): pl.pallas_call(functools.partial(caption_kernel, lay), out_shape=(of((n_x...  7.32 us
    ppermute x6, starting transfers between devices, from_y(): return lax.ppermute(value, 'dp', pairs)  6.28 us
    dot_general x3, matrix products, contract_last(): lax.dot_general(a, b, (((1,), (1,)), ((), ())), preferred_element_type=F32)  5.93 us
  transfers between devices with their start and end apart: 35, of which 12 were waited for; matrix products, arithmetic and copies ran while one was open for 10% of the time, Pallas kernels for 4%

commit v1 on v0

v1 whole, which is shorter than its diff:
```python
import functools

import jax
import jax.numpy as jnp
from jax import lax
from jax.experimental import pallas as pl
from jax.experimental.pallas import tpu as pltpu
from jax.sharding import PartitionSpec as P


epsilon = 1e-06
CORES = 2
ROWS_Y = 2
CHUNK = 32
PARTS = 2
LOG2E = 1.4426950408889634
F32 = jnp.float32
BF16 = jnp.bfloat16


def contract_last(a, b):
    return lax.dot_general(a, b, (((1,), (1,)), ((), ())), preferred_element_type=F32)


def contract_first(a, b):
    return lax.dot_general(a, b, (((0,), (0,)), ((), ())), preferred_element_type=F32)


def split_rows(rows):
    units = rows // 16
    heights = [(units // PARTS + (n < units % PARTS)) * 16 for n in range(PARTS)]
    return [(sum(heights[:n]), heights[n]) for n in range(PARTS)]


def lane_sums(partial):
    ones = jnp.ones((128, 128), BF16)
    upper = partial.astype(BF16)
    lower = (partial - upper.astype(F32)).astype(BF16)
    return jnp.dot(upper, ones, preferred_element_type=F32) + jnp.dot(lower, ones, preferred_element_type=F32)


def folded(pieces):
    while len(pieces) > 1:
        pieces = [pieces[n] + pieces[n + 1] for n in range(0, len(pieces) - 1, 2)] + (
            pieces[-1:] if len(pieces) % 2 else []
        )
    return pieces[0]


def cut(ref, row, lane, height=16):
    return ref[row : row + height, lane * 128 : lane * 128 + 128]


def forward(x, w, raw, z, scales, top, rows):
    lanes = w.shape[1] // 128
    raw[top : top + rows, :] = jnp.dot(x[top : top + rows, :], w[...], preferred_element_type=F32)
    for r in range(top, top + rows, 16):
        value = [cut(raw, r, n) for n in range(lanes)]
        scales[r : r + 16, :] = folded([v * v for v in value])
    scales[top : top + rows, :] = lax.rsqrt(lane_sums(scales[top : top + rows, :]) + epsilon)
    for r in range(top, top + rows, 16):
        scale = scales[r : r + 16, :]
        for n in range(lanes):
            z[r : r + 16, n * 128 : n * 128 + 128] = (cut(raw, r, n) * scale).astype(BF16)


def back(source, raw, scales, raw_offset, offset, count, out, along):
    lanes = source.shape[1] // 128
    for r in range(offset, offset + count, 16):
        there = raw_offset + r
        along[r : r + 16, :] = folded([cut(source, r, n) * cut(raw, there, n) for n in range(lanes)])
    along[offset : offset + count, :] = lane_sums(along[offset : offset + count, :])
    for r in range(offset, offset + count, 16):
        there = raw_offset + r
        scale = scales[there : there + 16, :]
        pull = along[r : r + 16, :] * (scale * scale * scale)
        for n in range(lanes):
            value = scale * cut(source, r, n) - pull * cut(raw, there, n)
            out[r - offset : r - offset + 16, n * 128 : n * 128 + 128] = value.astype(out.dtype)


class Copies:
    def __init__(self, sem):
        self.sem, self.used = sem, 0

    def start(self, src, dst):
        copy = pltpu.make_async_copy(src, dst, self.sem.at[self.used])
        self.used += 1
        copy.start()
        return copy


def wait_all(copies):
    for copy in copies:
        copy.wait()


def place_weight(moves, own, pieces, groups, full, n_p, width, place, base):
    step = full.shape[0] // n_p
    copies = [moves.start(own, full.at[:, pl.ds(0, width)])]
    for g, group in enumerate(groups):
        for r in range(n_p):
            offset = pl.multiple_of(place[base + r], step)
            for n, k in enumerate(group):
                source = pieces[g * n_p + r].at[pl.ds(n * step, step), :]
                copies.append(moves.start(source, full.at[pl.ds(offset, step), pl.ds(k * width, width)]))
    return copies


class Operands:
    def __init__(self, refs):
        self.refs = list(refs)

    def take(self, count):
        got, self.refs = self.refs[:count], self.refs[count:]
        return got

    def one(self):
        return self.take(1)[0]


def pair_kernel(lay, *refs):
    n_cap, n_img, n_pc, n_pi = lay["n_cap"], lay["n_img"], lay["n_pc"], lay["n_pi"]
    rows, img_rows = lay["rows"], lay["img_rows"]
    groups, width = lay["groups"], lay["width"]
    args = Operands(refs)
    place, cap_x, img_x = args.one(), args.take(n_cap), args.take(n_img)
    own_c, pieces_c = args.one(), args.take(len(groups) * n_pc)
    own_i, pieces_i = args.one(), args.take(len(groups) * n_pi)
    first, last, weight, position, factors = args.take(5)
    out_img = args.take(n_img * PARTS)
    out_coef, out_zi, out_rc, out_sc, out_wc, out_wi = args.take(6)
    xc, xi, zc, zi, raw_c, raw, sc_c, scales, wc, wi, logits, coef, dz, along, sem = args.take(15)

    moves = Copies(sem)
    heads_c = place_weight(moves, own_c, pieces_c, groups, wc, n_pc, width, place, 0)
    features_c = [moves.start(cap_x[q], xc.at[pl.ds(q * rows, rows), :]) for q in range(n_cap)]
    heads_i = place_weight(moves, own_i, pieces_i, groups, wi, n_pi, width, place, n_pc)
    features_i = [moves.start(img_x[q], xi.at[pl.ds(q * img_rows, img_rows), :]) for q in range(n_img)]
    wait_all(heads_c)
    outs = [moves.start(wc, out_wc)]
    for q in range(n_cap):
        features_c[q].wait()
        forward(xc, wc, raw_c, zc, sc_c, q * rows, rows)
        here = pl.ds(q * rows, rows)
        outs.append(moves.start(raw_c.at[here, :], out_rc.at[here, :]))
    outs.append(moves.start(sc_c, out_sc))
    wait_all(heads_i)
    outs.append(moves.start(wi, out_wi))
    for q in range(n_img):
        features_i[q].wait()
        forward(xi, wi, raw, zi, scales, q * img_rows, img_rows)
    outs.append(moves.start(zi, out_zi))

    sharp = factors[0]
    slope, level = -LOG2E * sharp, -LOG2E * factors[1]
    spot = position[...]
    columns = n_cap * rows
    for j in range(n_img):
        base = j * img_rows
        logits[...] = contract_last(zi[pl.ds(base, img_rows), :], zc[...])

        def chunk(r, _):
            here = pl.multiple_of(base + r * CHUNK, 16)
            line = pl.ds(pl.multiple_of(r * CHUNK, 16), CHUNK)
            touched = place[n_pc + n_pi + j * (img_rows // CHUNK) + r] != 0

            @pl.when(touched)
            def _():
                lo = first[pl.ds(here, CHUNK), :]
                hi = last[pl.ds(here, CHUNK), :]
                plus = weight[pl.ds(here, CHUNK), :]
                for c in range(0, columns, 128):
                    value = logits[line, pl.ds(c, 128)] * slope + level
                    col = spot[:, c : c + 128]
                    inside = (col >= lo) & (col < hi)
                    power = jnp.exp2(jnp.where(inside, -value, value))
                    share = jnp.where(inside, plus, sharp) / (1.0 + power)
                    coef[pl.ds(here, CHUNK), pl.ds(c, 128)] = share.astype(BF16)

            @pl.when(jnp.logical_not(touched))
            def _():
                for c in range(0, columns, 128):
                    power = jnp.exp2(logits[line, pl.ds(c, 128)] * slope + level)
                    coef[pl.ds(here, CHUNK), pl.ds(c, 128)] = (sharp / (1.0 + power)).astype(BF16)

            return 0

        lax.fori_loop(0, img_rows // CHUNK, chunk, 0)
        outs.append(moves.start(coef.at[pl.ds(base, img_rows), :], out_coef.at[pl.ds(base, img_rows), :]))
        dz[...] = jnp.dot(coef[pl.ds(base, img_rows), :], zc[...], preferred_element_type=F32)
        for p, (top, height) in enumerate(split_rows(img_rows)):
            back(dz, raw, scales, base, top, height, out_img[j * PARTS + p], along)
    wait_all(outs)


def caption_kernel(span, heights, coef_in, zi_in, rc_in, sc_in, *refs):
    results, (coef, zi, raw, scales, dz, along), sums, sem = refs[:2], refs[2:8], refs[8:10], refs[10]
    low, high, top = span
    moves = Copies(sem)
    early = [moves.start(zi_in, zi), moves.start(coef_in.at[:, pl.ds(low, high - low)], coef)]
    late = [moves.start(sc_in.at[pl.ds(low, high - low), :], scales), moves.start(rc_in.at[pl.ds(low, high - low), :], raw)]
    wait_all(early)
    dz[...] = contract_first(coef[...], zi[...])
    wait_all(late)
    outs, offset = [], top - low
    for n, height in enumerate(heights):
        back(dz, raw, scales, 0, offset, height, sums[n], along)
        outs.append(moves.start(sums[n], results[n]))
        offset += height
    wait_all(outs)


def whole(*args):
    img_x, cap_x, img_w, cap_w, counts, sharp, shift = args
    n_dp, slots = lax.axis_size("dp"), lax.axis_size("tensor")
    n_y = ROWS_Y
    n_x = n_dp // (n_y * CORES)
    rows = cap_x.shape[0]
    img_rows = img_x.shape[0]
    depth, width = cap_w.shape
    me = lax.axis_index("dp")
    mine = lax.axis_index("tensor")
    core = me % CORES
    pos_x = (me // CORES) % n_x
    pos_y = me // (CORES * n_x)

    def number(y, x, c):
        return (y * n_x + x) * CORES + c

    def from_y(value, k):
        pairs = [
            (number((y + k) % n_y, x, c), number(y, x, c))
            for y in range(n_y)
            for x in range(n_x)
            for c in range(CORES)
        ]
        return lax.ppermute(value, "dp", pairs)

    def from_x(value, k):
        pairs = [
            (number(y, (x + k) % n_x, c), number(y, x, c))
            for y in range(n_y)
            for x in range(n_x)
            for c in range(CORES)
        ]
        return lax.ppermute(value, "dp", pairs)

    def from_core(value):
        return lax.ppermute(value, "dp", [(s, s ^ 1) for s in range(n_dp)])

    def from_z(value, k):
        return lax.ppermute(value, "tensor", [((t + k) % slots, t) for t in range(slots)])

    cap_same = [cap_x] + [from_x(cap_x, k) for k in range(1, n_x)]
    img_all = [from_y(img_x, k) for k in range(1, n_y)] + [img_x]
    cap_other = [from_core(block) for block in cap_same]
    cap_all = cap_other[1:] + cap_same[1:] + cap_other[:1] + cap_same[:1]

    n_pc, n_pi = n_x * CORES, n_y * CORES
    step_c, step_i = depth // n_pc, depth // n_pi

    def places(n_line, pos, step):
        return [((pos + j) % n_line * CORES + c) * step for c in (core, 1 - core) for j in range(n_line)]

    place = jnp.stack(places(n_x, pos_x, step_c) + places(n_y, pos_y, step_i)).astype(jnp.int32)

    ends = jnp.cumsum(counts)
    starts = ends - counts

    def of_image(values):
        blocks = []
        for k in list(range(1, n_y)) + [0]:
            owner = number((pos_y + k) % n_y, pos_x, core)
            blocks.append(lax.dynamic_slice_in_dim(values, owner * img_rows, img_rows))
        return jnp.concatenate(blocks)[:, None]

    first = of_image(starts)
    last = of_image(ends)
    weight = -sharp[0] / of_image(counts).astype(F32)
    order = [(k, c) for c in (1 - core, core) for k in range(1, n_x)] + [(0, 1 - core), (0, core)]
    heads = [(number(pos_y, (pos_x + k) % n_x, c) * slots + mine) * rows for k, c in order]
    position = jnp.concatenate([head + jnp.arange(rows, dtype=jnp.int32) for head in heads])[None, :]
    low, high = first[::CHUNK, 0], last[CHUNK - 1 :: CHUNK, 0]
    touched = functools.reduce(jnp.logical_or, [(low < head + rows) & (high > head) for head in heads])
    place = jnp.concatenate([place, touched.astype(jnp.int32)])
    factors = jnp.concatenate([sharp, shift])

    far = slots // 2
    near = [k for n in range(1, far) for k in (n, slots - n)]
    groups = [near, [far]]
    own = jnp.concatenate(
        [
            lax.dynamic_slice_in_dim(cap_w, (pos_x * CORES + core) * step_c, step_c, axis=0),
            lax.dynamic_slice_in_dim(img_w, (pos_y * CORES + core) * step_i, step_i, axis=0),
        ]
    )
    slices = {k: from_z(own, k) for k in near}
    tables = (place, first, last, weight, position)
    own, _, tables = lax.optimization_barrier((own, tuple(slices.values()), tables))
    place, first, last, weight, position = tables
    slices[far] = from_z(own, far)

    cap_pieces, img_pieces = [], []
    for group in groups:
        cap_line = [jnp.concatenate([slices[k][:step_c] for k in group])]
        img_line = [jnp.concatenate([slices[k][step_c:] for k in group])]
        cap_line += [from_x(cap_line[0], j) for j in range(1, n_x)]
        img_line += [from_y(img_line[0], j) for j in range(1, n_y)]
        cap_pieces += cap_line + [from_core(value) for value in cap_line]
        img_pieces += img_line + [from_core(value) for value in img_line]

    n_cap, n_img = n_x * CORES, n_y
    lay = dict(n_cap=n_cap, n_img=n_img, rows=rows, img_rows=img_rows, n_pc=n_pc, n_pi=n_pi, width=width)
    lay.update(groups=groups)
    full = slots * width
    c_rows, i_rows = n_cap * rows, n_img * img_rows
    hbm = pl.BlockSpec(memory_space=pltpu.HBM)
    vmem = pl.BlockSpec(memory_space=pltpu.VMEM)
    smem = pl.BlockSpec(memory_space=pltpu.SMEM)

    def of(shape, dtype):
        return jax.ShapeDtypeStruct(shape, dtype)

    def params(mib):
        return pltpu.CompilerParams(vmem_limit_bytes=mib * 2**20)

    def cost(flops, mib):
        return pl.CostEstimate(flops=flops, bytes_accessed=mib * 2**20, transcendentals=0)

    pair = 2 * c_rows * i_rows * full
    heights = [height for _, height in split_rows(img_rows)]
    n_out = n_img * PARTS
    n_copies = 2 + (slots - 1) * (n_pc + n_pi) + 2 * n_cap + 2 * n_img + 4
    operands = [place] + cap_all + img_all + [cap_w] + cap_pieces + [img_w] + img_pieces
    specs = [smem] + [hbm] * (len(operands) - 1) + [vmem] * 4 + [smem]
    operands += [first, last, weight, position, factors]
    n_send = (n_img - 1) * PARTS
    made = pl.pallas_call(
        functools.partial(pair_kernel, lay),
        out_shape=tuple(of((heights[n % PARTS], full), BF16 if n < n_send else F32) for n in range(n_out))
        + (
            of((i_rows, c_rows), BF16),
            of((i_rows, full), BF16),
            of((c_rows, full), F32),
            of((c_rows, 128), F32),
            of((depth, full), BF16),
            of((depth, full), BF16),
        ),
        in_specs=specs,
        out_specs=[vmem] * n_out + [hbm] * 6,
        scratch_shapes=[
            pltpu.VMEM((c_rows, depth), BF16),
            pltpu.VMEM((i_rows, depth), BF16),
            pltpu.VMEM((c_rows, full), BF16),
            pltpu.VMEM((i_rows, full), BF16),
            pltpu.VMEM((c_rows, full), F32),
            pltpu.VMEM((i_rows, full), F32),
            pltpu.VMEM((c_rows, 128), F32),
            pltpu.VMEM((i_rows, 128), F32),
            pltpu.VMEM((depth, full), BF16),
            pltpu.VMEM((depth, full), BF16),
            pltpu.VMEM((img_rows, c_rows), F32),
            pltpu.VMEM((i_rows, c_rows), BF16),
            pltpu.VMEM((img_rows, full), F32),
            pltpu.VMEM((img_rows, 128), F32),
            pltpu.SemaphoreType.DMA((n_copies,)),
        ],
        compiler_params=params(60),
        cost_estimate=cost((c_rows + i_rows) * depth * full * 2 + 2 * pair, 20),
        name="pairs",
    )(*operands)
    img_send, img_own = made[:n_send], made[n_send:n_out]
    coef, zi, raw_c, sc_c, wc, wi = made[n_out:]

    img_sent = []
    for p in range(PARTS):
        parts = [img_send[(k - 1) * PARTS + p] for k in range(1, n_y)]
        img_sent.append([from_y(parts[k - 1], n_y - k) for k in range(1, n_y)])

    def caption_sums(top, heights):
        low = top // 128 * 128
        high = min(-(-(top + sum(heights)) // 128) * 128, c_rows)
        span = high - low
        return pl.pallas_call(
            functools.partial(caption_kernel, (low, high, top), heights),
            out_shape=(of((heights[0], full), BF16), of((heights[1], full), F32)),
            in_specs=[hbm] * 4,
            out_specs=[hbm] * 2,
            scratch_shapes=[
                pltpu.VMEM((i_rows, span), BF16),
                pltpu.VMEM((i_rows, full), BF16),
                pltpu.VMEM((span, full), F32),
                pltpu.VMEM((span, 128), F32),
                pltpu.VMEM((span, full), F32),
                pltpu.VMEM((span, 128), F32),
                pltpu.VMEM((heights[0], full), BF16),
                pltpu.VMEM((heights[1], full), F32),
                pltpu.SemaphoreType.DMA((6,)),
            ],
            compiler_params=params(60),
            cost_estimate=cost(2 * span * i_rows * full, 10),
            name="captions",
        )(coef, zi, raw_c, sc_c)

    others = (n_x - 1) * rows
    arrived = []
    if others:
        to_core, to_next = caption_sums(0, (others, others))
        crossed = from_core(to_core)
        for k in range(1, n_x):
            here = slice((k - 1) * rows, k * rows)
            sent = (to_next[here] + crossed[here].astype(F32)).astype(BF16)
            arrived.append(from_x(sent, n_x - k))
    to_core, cap_own = caption_sums(2 * others, (rows, rows))
    crossed = from_core(to_core)
    cap_total = functools.reduce(lambda a, b: a + b.astype(F32), arrived, cap_own + crossed.astype(F32))
    grad_cap = contract_last(cap_total.astype(BF16), wc).astype(BF16)

    share = depth // slots
    grad_img = []
    for p in range(PARTS):
        img_total = img_own[p]
        for arrived in img_sent[p]:
            img_total = img_total + arrived.astype(F32)
        img_part = contract_last(img_total.astype(BF16), wi)

        def columns_of(k):
            return lax.dynamic_slice_in_dim(img_part, (mine + k) % slots * share, share, axis=1)

        arrived = [from_z(columns_of(slots - k).astype(BF16), k) for k in range(1, slots)]
        grad_img.append(functools.reduce(lambda a, b: a + b.astype(F32), arrived, columns_of(0)).astype(BF16))
    return (jnp.concatenate(grad_img), grad_cap)


def solution(mesh):
    in_specs = (
        P("dp", None),
        P(("dp", "tensor"), None),
        P(None, "tensor"),
        P(None, "tensor"),
        P(),
        P(),
        P(),
    )
    out_specs = (P("dp", "tensor"), P(("dp", "tensor"), None))
    return jax.shard_map(whole, mesh=mesh, in_specs=in_specs, out_specs=out_specs, check_vma=False)
```

time: 132 us -> 115 us (0.87)
  waiting for transfers between devices: 55.4 us -> 40.6 us
  matrix products: 5.93 us -> 3.52 us
  local copies, waits for them, and re-layouts: 5.93 us -> 7.58 us
    ppermute x9, waiting for transfers between devices: 24.3 us -> 16.2 us  [from_z(): lax.ppermute(value, 'tensor', [((t + k) % slots, t) for t in range(slots)])]
    ppermute x6 -> x5, waiting for transfers between devices: 20.7 us -> 12.8 us  [from_y(): return lax.ppermute(value, 'dp', pairs)]
    dot_general x3, matrix products: 5.93 us -> 3.52 us  [contract_last(): lax.dot_general(a, b, (((1,), (1,)), ((), ())), preferred_element_type=F32)]
    optimization_barrier x0 -> x2, local copies, waits for them, and re-layouts: none -> 1.86 us  [whole(): lax.optimization_barrier((own, tuple(slices.values()), tables))]
    broadcast_in_dim x4 -> x2, local copies, waits for them, and re-layouts: 1.84 us -> 0.01 us  [of_image(): return jnp.concatenate(blocks)[:, None]]
    pallas_call x2, Pallas kernels: 12.4 us -> 10.6 us  [caption_sums(): pl.pallas_call(functools.partial(caption_kernel, (low, high, top), height...]
    unnamed x50 -> x46, local copies, waits for them, and re-layouts: 0.11 us -> 1.67 us
    ppermute x5 -> x4, waiting for transfers between devices: 9.64 us -> 10.4 us  [from_x(): return lax.ppermute(value, 'dp', pairs)]
  transfers between devices with their start and end apart: 35 -> 30, of which waited for: 12 -> 12; matrix products, arithmetic and copies ran while one was open for 10% -> 10% of each run, Pallas kernels for 4% -> 9%
where the time goes in v1:
time: 115 us
  waiting for transfers between devices  40.6 us (35%)
  Pallas kernels  30.1 us (26%)
  starting transfers between devices  25.8 us (22%)
  local copies, waits for them, and re-layouts  7.58 us (7%)
  other arithmetic  4.65 us (4%)
  matrix products  3.52 us (3%)
  between operations  2.39 us (2%)
    pallas_call x1, Pallas kernels, whole(): pl.pallas_call(functools.partial(pair_kernel, lay), out_shape=tuple((of((...  19.4 us
    ppermute x9, waiting for transfers between devices, from_z(): lax.ppermute(value, 'tensor', [((t + k) % slots, t) for t in range(slots)])  16.2 us
    ppermute x5, waiting for transfers between devices, from_y(): return lax.ppermute(value, 'dp', pairs)  12.8 us
    ppermute x9, starting transfers between devices, from_z(): lax.ppermute(value, 'tensor', [((t + k) % slots, t) for t in range(slots)])  12.4 us
    pallas_call x2, Pallas kernels, caption_sums(): pl.pallas_call(functools.partial(caption_kernel, (low, high, top), height...  10.6 us
    ppermute x4, waiting for transfers between devices, from_x(): return lax.ppermute(value, 'dp', pairs)  10.4 us
    ppermute x5, starting transfers between devices, from_y(): return lax.ppermute(value, 'dp', pairs)  5.7 us
    ppermute x4, starting transfers between devices, from_x(): return lax.ppermute(value, 'dp', pairs)  5.15 us
  transfers between devices with their start and end apart: 30, of which 12 were waited for; matrix products, arithmetic and copies ran while one was open for 10% of the time, Pallas kernels for 9%

profile of v1, /device:TPU:0, one launch (start us, length us, event | category | flops | bytes accessed | tf_op | source)
XLA Modules:
  0.0 114.6 jit_solution(8978358626001516511)
XLA Ops:
  1.7 5.1 %collective-permute-start = (bf16[512,256]{1,0:T(8,128)(2,1)S(1)}, bf16[512,256]{1,0:T(8,128)(2,1)S(1)}, u32[]{:S(2)}, u32[]{:S(2)}) collective-permute-start(bf16[512,256]{1,0:T(8,128)(2,1)S(1)} %pad_maximum_fusion), channel_id=1, source_target_pairs={{1,0},{2,1},{3,2},{0,3},{5,4},{6,5},{7,6},{4,7},{9,8},{10,9},{11,1... | collective-permute-start | bytes 786440 | tf_op jit(solution)/shard_map/ppermute | solution.py:253
  6.9 1.5 %collective-permute-start.2 = (bf16[352,1024]{1,0:T(8,128)(2,1)}, bf16[352,1024]{1,0:T(8,128)(2,1)S(1)}, u32[]{:S(2)}, u32[]{:S(2)}) collective-permute-start(bf16[352,1024]{1,0:T(8,128)(2,1)} %refs_4_.1), channel_id=1, source_target_pairs={{8,0},{12,4},{0,8},{4,12},{24,16},{28,20},{16,24},{20,28},{9,1},{1... | collective-permute-start | bytes 2162696 | tf_op jit(solution)/shard_map/ppermute | solution.py:247
  14.9 4.1 %collective-permute-done.1 = bf16[512,256]{1,0:T(8,128)(2,1)S(1)} collective-permute-done((bf16[512,256]{1,0:T(8,128)(2,1)S(1)}, bf16[512,256]{1,0:T(8,128)(2,1)S(1)}, u32[]{:S(2)}, u32[]{:S(2)}) %collective-permute-start.1) | collective-permute-done | bytes 262176 | tf_op jit(solution)/shard_map/ppermute | solution.py:253
  19.0 1.6 %collective-permute-start.13 = (bf16[512,256]{1,0:T(8,128)(2,1)S(1)}, bf16[512,256]{1,0:T(8,128)(2,1)S(1)}, u32[]{:S(2)}, u32[]{:S(2)}) collective-permute-start(bf16[512,256]{1,0:T(8,128)(2,1)S(1)} %pad_maximum_fusion.2.refs_17_), channel_id=1, source_target_pairs={{16,0},{20,4},{24,8},{28,12},{0,16},{4,20},{8,24},{12,28},{17,1},{... | collective-permute-start | bytes 786440 | tf_op jit(solution)/shard_map/ppermute | solution.py:238
  20.6 1.6 %collective-permute-start.6 = (bf16[512,256]{1,0:T(8,128)(2,1)S(1)}, bf16[512,256]{1,0:T(8,128)(2,1)}, u32[]{:S(2)}, u32[]{:S(2)}) collective-permute-start(bf16[512,256]{1,0:T(8,128)(2,1)S(1)} %pad_maximum_fusion.1.refs_8_), channel_id=1, source_target_pairs={{8,0},{12,4},{0,8},{4,12},{24,16},{28,20},{16,24},{20,28},{9,1},{1... | collective-permute-start | bytes 786440 | tf_op jit(solution)/shard_map/ppermute | solution.py:247
  22.9 3.3 %collective-permute-done.13.refs_18_ = bf16[512,256]{1,0:T(8,128)(2,1)S(1)} collective-permute-done((bf16[512,256]{1,0:T(8,128)(2,1)S(1)}, bf16[512,256]{1,0:T(8,128)(2,1)S(1)}, u32[]{:S(2)}, u32[]{:S(2)}) %collective-permute-start.13) | collective-permute-done | bytes 262176 | tf_op jit(solution)/shard_map/ppermute | solution.py:238
  26.3 1.5 %collective-permute-start.5 = (bf16[352,1024]{1,0:T(8,128)(2,1)S(1)}, bf16[352,1024]{1,0:T(8,128)(2,1)S(1)}, u32[]{:S(2)}, u32[]{:S(2)}) collective-permute-start(bf16[352,1024]{1,0:T(8,128)(2,1)S(1)} %copy-done.10), channel_id=1, source_target_pairs={{16,0},{20,4},{24,8},{28,12},{0,16},{4,20},{8,24},{12,28},{17,1},{... | collective-permute-start | bytes 2162696 | tf_op jit(solution)/shard_map/ppermute | solution.py:238
  27.8 2.6 %collective-permute-done.6.refs_9_ = bf16[512,256]{1,0:T(8,128)(2,1)} collective-permute-done((bf16[512,256]{1,0:T(8,128)(2,1)S(1)}, bf16[512,256]{1,0:T(8,128)(2,1)}, u32[]{:S(2)}, u32[]{:S(2)}) %collective-permute-start.6) | collective-permute-done | bytes 262176 | tf_op jit(solution)/shard_map/ppermute | solution.py:247
  30.4 4.9 %collective-permute-done.9 = bf16[512,256]{1,0:T(8,128)(2,1)S(1)} collective-permute-done((bf16[512,256]{1,0:T(8,128)(2,1)S(1)}, bf16[512,256]{1,0:T(8,128)(2,1)S(1)}, u32[]{:S(2)}, u32[]{:S(2)}) %collective-permute-start.9) | collective-permute-done | bytes 262176 | tf_op jit(solution)/shard_map/ppermute | solution.py:253
  37.4 4.1 %collective-permute-done.10.refs_13_ = bf16[256,256]{1,0:T(8,128)(2,1)S(1)} collective-permute-done((bf16[256,256]{1,0:T(8,128)(2,1)S(1)}, bf16[256,256]{1,0:T(8,128)(2,1)S(1)}, u32[]{:S(2)}, u32[]{:S(2)}) %collective-permute-start.10) | collective-permute-done | bytes 131104 | tf_op jit(solution)/shard_map/ppermute | solution.py:247
  41.5 3.9 %collective-permute-done.16.refs_22_ = bf16[256,256]{1,0:T(8,128)(2,1)} collective-permute-done((bf16[256,256]{1,0:T(8,128)(2,1)S(1)}, bf16[256,256]{1,0:T(8,128)(2,1)}, u32[]{:S(2)}, u32[]{:S(2)}) %collective-permute-start.16) | collective-permute-done | bytes 131104 | tf_op jit(solution)/shard_map/ppermute | solution.py:238
  52.5 19.4 %pairs.1 = (bf16[176,1024]{1,0:T(8,128)(2,1)}, bf16[176,1024]{1,0:T(8,128)(2,1)}, f32[176,1024]{1,0:T(8,128)}, f32[176,1024]{1,0:T(8,128)}, bf16[704,1408]{1,0:T...) custom-call(s32[30]{0:T(128)} %concatenate.44.refs_0_, ...), custom_call_target="tpu_custom_call" | custom-call | flops 8489271296 | bytes 20971520 | tf_op jit(solution)/shard_map/pairs/pallas_call | solution.py:339
  71.9 1.5 %collective-permute-start.19 = (bf16[176,1024]{1,0:T(8,128)(2,1)}, bf16[176,1024]{1,0:T(8,128)(2,1)S(1)}, u32[]{:S(2)}, u32[]{:S(2)}) collective-permute-start(bf16[176,1024]{1,0:T(8,128)(2,1)} %get-tuple-element.29), channel_id=1, source_target_pairs={{16,0},{20,4},{24,8},{28,12},{0,16},{4,20},{8,24},{12,28},{17,1},{... | collective-permute-start | bytes 1081352 | tf_op jit(solution)/shard_map/ppermute | solution.py:238
  73.4 5.2 %captions.3 = (bf16[352,1024]{1,0:T(8,128)(2,1)}, f32[352,1024]{1,0:T(8,128)}) custom-call(bf16[704,1408]{1,0:T(8,128)(2,1)} %get-tuple-element.33.coef_in, bf16[704,1024]{1,0:T(8,128)(2,1)} %get-tuple-element.34.zi_in, f32[1408,1024]{1,0:T(8,128)} %get-tuple-element.35.rc_in, f32[1408,128]{1,0:T(8,128)} %get-tuple-element.36.sc_in), custom_call_target="tpu_custom_call" | custom-call | flops 1107296256 | bytes 10485760 | tf_op jit(solution)/shard_map/captions/pallas_call | solution.py:385
  78.9 5.4 %captions.2 = (bf16[352,1024]{1,0:T(8,128)(2,1)}, f32[352,1024]{1,0:T(8,128)}) custom-call(bf16[704,1408]{1,0:T(8,128)(2,1)} %get-tuple-element.33.coef_in, bf16[704,1024]{1,0:T(8,128)(2,1)} %get-tuple-element.34.zi_in, f32[1408,1024]{1,0:T(8,128)} %get-tuple-element.35.rc_in, f32[1408,128]{1,0:T(8,128)} %get-tuple-element.36.sc_in), custom_call_target="tpu_custom_call" | custom-call | flops 1107296256 | bytes 10485760 | tf_op jit(solution)/shard_map/captions/pallas_call | solution.py:385
  86.3 2.4 %collective-permute-start.20 = (bf16[176,256]{1,0:T(8,128)(2,1)S(1)}, bf16[176,256]{1,0:T(8,128)(2,1)S(1)}, u32[]{:S(2)}, u32[]{:S(2)}) collective-permute-start(bf16[176,256]{1,0:T(8,128)(2,1)S(1)} %get-tuple-element.44), channel_id=1, source_target_pairs={{1,0},{2,1},{3,2},{0,3},{5,4},{6,5},{7,6},{4,7},{9,8},{10,9},{11,1... | collective-permute-start | bytes 270344 | tf_op jit(solution)/shard_map/ppermute | solution.py:253
  89.8 5.6 %collective-permute-done.23 = bf16[176,1024]{1,0:T(8,128)(2,1)S(1)} collective-permute-done((bf16[176,1024]{1,0:T(8,128)(2,1)}, bf16[176,1024]{1,0:T(8,128)(2,1)S(1)}, u32[]{:S(2)}, u32[]{:S(2)}) %collective-permute-start.23) | collective-permute-done | bytes 360480 | tf_op jit(solution)/shard_map/ppermute | solution.py:238
  95.4 1.5 %collective-permute-start.29 = (bf16[352,1024]{1,0:T(8,128)(2,1)S(1)}, bf16[352,1024]{1,0:T(8,128)(2,1)S(1)}, u32[]{:S(2)}, u32[]{:S(2)}) collective-permute-start(bf16[352,1024]{1,0:T(8,128)(2,1)S(1)} %add_convert_fusion.1), channel_id=1, source_target_pairs={{8,0},{12,4},{0,8},{4,12},{24,16},{28,20},{16,24},{20,28},{9,1},{1... | collective-permute-start | bytes 2162696 | tf_op jit(solution)/shard_map/ppermute | solution.py:247
  97.9 1.2 %collective-permute-start.24 = (bf16[176,256]{1,0:T(8,128)(2,1)S(1)}, bf16[176,256]{1,0:T(8,128)(2,1)S(1)}, u32[]{:S(2)}, u32[]{:S(2)}) collective-permute-start(bf16[176,256]{1,0:T(8,128)(2,1)S(1)} %get-tuple-element.47), channel_id=1, source_target_pairs={{1,0},{2,1},{3,2},{0,3},{5,4},{6,5},{7,6},{4,7},{9,8},{10,9},{11,1... | collective-permute-start | bytes 270344 | tf_op jit(solution)/shard_map/ppermute | solution.py:253
  99.1 2.0 %collective-permute-start.25 = (bf16[176,256]{1,0:T(8,128)(2,1)S(1)}, bf16[176,256]{1,0:T(8,128)(2,1)S(1)}, u32[]{:S(2)}, u32[]{:S(2)}) collective-permute-start(bf16[176,256]{1,0:T(8,128)(2,1)S(1)} %get-tuple-element.49), channel_id=1, source_target_pairs={{2,0},{3,1},{0,2},{1,3},{6,4},{7,5},{4,6},{5,7},{10,8},{11,9},{8,1... | collective-permute-start | bytes 270344 | tf_op jit(solution)/shard_map/ppermute | solution.py:253
  101.1 1.9 %collective-permute-done.24 = bf16[176,256]{1,0:T(8,128)(2,1)S(1)} collective-permute-done((bf16[176,256]{1,0:T(8,128)(2,1)S(1)}, bf16[176,256]{1,0:T(8,128)(2,1)S(1)}, u32[]{:S(2)}, u32[]{:S(2)}) %collective-permute-start.24) | collective-permute-done | bytes 90144 | tf_op jit(solution)/shard_map/ppermute | solution.py:253
  103.0 5.3 %collective-permute-done.25 = bf16[176,256]{1,0:T(8,128)(2,1)S(1)} collective-permute-done((bf16[176,256]{1,0:T(8,128)(2,1)S(1)}, bf16[176,256]{1,0:T(8,128)(2,1)S(1)}, u32[]{:S(2)}, u32[]{:S(2)}) %collective-permute-start.25) | collective-permute-done | bytes 90144 | tf_op jit(solution)/shard_map/ppermute | solution.py:253
  109.1 3.7 %collective-permute-done.29 = bf16[352,1024]{1,0:T(8,128)(2,1)S(1)} collective-permute-done((bf16[352,1024]{1,0:T(8,128)(2,1)S(1)}, bf16[352,1024]{1,0:T(8,128)(2,1)S(1)}, u32[]{:S(2)}, u32[]{:S(2)}) %collective-permute-start.29) | collective-permute-done | bytes 720928 | tf_op jit(solution)/shard_map/ppermute | solution.py:247
  112.8 1.8 %convolution_convert_fusion = bf16[352,1024]{1,0:T(8,128)(2,1)} fusion(bf16[1024,1024]{1,0:T(8,128)(2,1)S(1)} %copy-done.22, bf16[352,1024]{1,0:T(8,128)(2,1)S(1)} %collective-permute-done.29, f32[352,1024]{1,0:T(8,128)S(1)} %copy-done.8, bf16[352,1024]{1,0:T(8,128)(2,1)S(1)} %collective-permute-done.27), kind=kOutput, calls=%fused_computation.2 | convolution fusion | flops 740360192 | bytes 5701632 | tf_op jit(solution)/shard_map/dot_general | solution.py:22
  (128 shorter events, 21.1 us)
Async XLA Ops:
  1.7 13.1 %collective-permute-start = (bf16[512,256]{1,0:T(8,128)(2,1)S(1)}, bf16[512,256]{1,0:T(8,128)(2,1)S(1)}, u32[]{:S(2)}, u32[]{:S(2)}) collective-permute-start(bf16[512,256]{1,0:T(8,128)(2,1)S(1)} %pad_maximum_fusion), channel_id=1, source_target_pairs={{1,0},{2,1},{3,2},{0,3},{5,4},{6,5},{7,6},{4,7},{9,8},{10,9},{11,1... | collective-permute-start | bytes 786440 | tf_op jit(solution)/shard_map/ppermute | solution.py:253
  6.9 12.1 %collective-permute-start.1 = (bf16[512,256]{1,0:T(8,128)(2,1)S(1)}, bf16[512,256]{1,0:T(8,128)(2,1)S(1)}, u32[]{:S(2)}, u32[]{:S(2)}) collective-permute-start(bf16[512,256]{1,0:T(8,128)(2,1)S(1)} %pad_maximum_fusion), channel_id=1, source_target_pairs={{3,0},{0,1},{1,2},{2,3},{7,4},{4,5},{5,6},{6,7},{11,8},{8,9},{9,10... | collective-permute-start | bytes 786440 | tf_op jit(solution)/shard_map/ppermute | solution.py:253
  6.9 28.5 %collective-permute-start.2 = (bf16[352,1024]{1,0:T(8,128)(2,1)}, bf16[352,1024]{1,0:T(8,128)(2,1)S(1)}, u32[]{:S(2)}, u32[]{:S(2)}) collective-permute-start(bf16[352,1024]{1,0:T(8,128)(2,1)} %refs_4_.1), channel_id=1, source_target_pairs={{8,0},{12,4},{0,8},{4,12},{24,16},{28,20},{16,24},{20,28},{9,1},{1... | collective-permute-start | bytes 2162696 | tf_op jit(solution)/shard_map/ppermute | solution.py:247
  19.0 7.3 %collective-permute-start.13 = (bf16[512,256]{1,0:T(8,128)(2,1)S(1)}, bf16[512,256]{1,0:T(8,128)(2,1)S(1)}, u32[]{:S(2)}, u32[]{:S(2)}) collective-permute-start(bf16[512,256]{1,0:T(8,128)(2,1)S(1)} %pad_maximum_fusion.2.refs_17_), channel_id=1, source_target_pairs={{16,0},{20,4},{24,8},{28,12},{0,16},{4,20},{8,24},{12,28},{17,1},{... | collective-permute-start | bytes 786440 | tf_op jit(solution)/shard_map/ppermute | solution.py:238
  20.6 9.8 %collective-permute-start.6 = (bf16[512,256]{1,0:T(8,128)(2,1)S(1)}, bf16[512,256]{1,0:T(8,128)(2,1)}, u32[]{:S(2)}, u32[]{:S(2)}) collective-permute-start(bf16[512,256]{1,0:T(8,128)(2,1)S(1)} %pad_maximum_fusion.1.refs_8_), channel_id=1, source_target_pairs={{8,0},{12,4},{0,8},{4,12},{24,16},{28,20},{16,24},{20,28},{9,1},{1... | collective-permute-start | bytes 786440 | tf_op jit(solution)/shard_map/ppermute | solution.py:247
  22.2 13.1 %collective-permute-start.9 = (bf16[512,256]{1,0:T(8,128)(2,1)S(1)}, bf16[512,256]{1,0:T(8,128)(2,1)S(1)}, u32[]{:S(2)}, u32[]{:S(2)}) collective-permute-start(bf16[512,256]{1,0:T(8,128)(2,1)S(1)} %pad_maximum_fusion), channel_id=1, source_target_pairs={{2,0},{3,1},{0,2},{1,3},{6,4},{7,5},{4,6},{5,7},{10,8},{11,9},{8,1... | collective-permute-start | bytes 786440 | tf_op jit(solution)/shard_map/ppermute | solution.py:253
  22.9 23.9 %collective-permute-start.4 = (bf16[352,1024]{1,0:T(8,128)(2,1)S(1)}, bf16[352,1024]{1,0:T(8,128)(2,1)S(1)}, u32[]{:S(2)}, u32[]{:S(2)}) collective-permute-start(bf16[352,1024]{1,0:T(8,128)(2,1)S(1)} %copy-done.9), channel_id=1, source_target_pairs={{0,4},{4,0},{8,12},{12,8},{16,20},{20,16},{24,28},{28,24},{1,5},{5... | collective-permute-start | bytes 2162696 | tf_op jit(solution)/shard_map/ppermute | solution.py:250
  26.3 21.0 %collective-permute-start.5 = (bf16[352,1024]{1,0:T(8,128)(2,1)S(1)}, bf16[352,1024]{1,0:T(8,128)(2,1)S(1)}, u32[]{:S(2)}, u32[]{:S(2)}) collective-permute-start(bf16[352,1024]{1,0:T(8,128)(2,1)S(1)} %copy-done.10), channel_id=1, source_target_pairs={{16,0},{20,4},{24,8},{28,12},{0,16},{4,20},{8,24},{12,28},{17,1},{... | collective-permute-start | bytes 2162696 | tf_op jit(solution)/shard_map/ppermute | solution.py:238
  30.4 5.5 %collective-permute-start.14 = (bf16[512,256]{1,0:T(8,128)(2,1)S(1)}, bf16[512,256]{1,0:T(8,128)(2,1)S(1)}, u32[]{:S(2)}, u32[]{:S(2)}) collective-permute-start(bf16[512,256]{1,0:T(8,128)(2,1)S(1)} %pad_maximum_fusion.2.refs_17_), channel_id=1, source_target_pairs={{0,4},{4,0},{8,12},{12,8},{16,20},{20,16},{24,28},{28,24},{1,5},{5... | collective-permute-start | bytes 786440 | tf_op jit(solution)/shard_map/ppermute | solution.py:250
  35.3 16.5 %collective-permute-start.3 = (bf16[352,1024]{1,0:T(8,128)(2,1)S(1)}, bf16[352,1024]{1,0:T(8,128)(2,1)}, u32[]{:S(2)}, u32[]{:S(2)}) collective-permute-start(bf16[352,1024]{1,0:T(8,128)(2,1)S(1)} %collective-permute-done.2.refs_2_), channel_id=1, source_target_pairs={{0,4},{4,0},{8,12},{12,8},{16,20},{20,16},{24,28},{28,24},{1,5},{5... | collective-permute-start | bytes 2162696 | tf_op jit(solution)/shard_map/ppermute | solution.py:250
  35.9 5.5 %collective-permute-start.10 = (bf16[256,256]{1,0:T(8,128)(2,1)S(1)}, bf16[256,256]{1,0:T(8,128)(2,1)S(1)}, u32[]{:S(2)}, u32[]{:S(2)}) collective-permute-start(bf16[256,256]{1,0:T(8,128)(2,1)S(1)} %get-tuple-element.51.refs_12_), channel_id=1, source_target_pairs={{8,0},{12,4},{0,8},{4,12},{24,16},{28,20},{16,24},{20,28},{9,1},{1... | collective-permute-start | bytes 393224 | tf_op jit(solution)/shard_map/ppermute | solution.py:247
  36.9 8.5 %collective-permute-start.16 = (bf16[256,256]{1,0:T(8,128)(2,1)S(1)}, bf16[256,256]{1,0:T(8,128)(2,1)}, u32[]{:S(2)}, u32[]{:S(2)}) collective-permute-start(bf16[256,256]{1,0:T(8,128)(2,1)S(1)} %get-tuple-element.50.refs_21_), channel_id=1, source_target_pairs={{16,0},{20,4},{24,8},{28,12},{0,16},{4,20},{8,24},{12,28},{17,1},{... | collective-permute-start | bytes 393224 | tf_op jit(solution)/shard_map/ppermute | solution.py:238
  45.4 6.4 %collective-permute-start.15 = (bf16[512,256]{1,0:T(8,128)(2,1)S(1)}, bf16[512,256]{1,0:T(8,128)(2,1)}, u32[]{:S(2)}, u32[]{:S(2)}) collective-permute-start(bf16[512,256]{1,0:T(8,128)(2,1)S(1)} %collective-permute-done.13.refs_18_), channel_id=1, source_target_pairs={{0,4},{4,0},{8,12},{12,8},{16,20},{20,16},{24,28},{28,24},{1,5},{5... | collective-permute-start | bytes 786440 | tf_op jit(solution)/shard_map/ppermute | solution.py:250
  71.9 13.4 %collective-permute-start.19 = (bf16[176,1024]{1,0:T(8,128)(2,1)}, bf16[176,1024]{1,0:T(8,128)(2,1)S(1)}, u32[]{:S(2)}, u32[]{:S(2)}) collective-permute-start(bf16[176,1024]{1,0:T(8,128)(2,1)} %get-tuple-element.29), channel_id=1, source_target_pairs={{16,0},{20,4},{24,8},{28,12},{0,16},{4,20},{8,24},{12,28},{17,1},{... | collective-permute-start | bytes 1081352 | tf_op jit(solution)/shard_map/ppermute | solution.py:238
  78.7 10.9 %collective-permute-start.28 = (bf16[352,1024]{1,0:T(8,128)(2,1)}, bf16[352,1024]{1,0:T(8,128)(2,1)S(1)}, u32[]{:S(2)}, u32[]{:S(2)}) collective-permute-start(bf16[352,1024]{1,0:T(8,128)(2,1)} %get-tuple-element.40), channel_id=1, source_target_pairs={{0,4},{4,0},{8,12},{12,8},{16,20},{20,16},{24,28},{28,24},{1,5},{5... | collective-permute-start | bytes 2162696 | tf_op jit(solution)/shard_map/ppermute | solution.py:250
  84.3 24.7 %collective-permute-start.27 = (bf16[352,1024]{1,0:T(8,128)(2,1)}, bf16[352,1024]{1,0:T(8,128)(2,1)S(1)}, u32[]{:S(2)}, u32[]{:S(2)}) collective-permute-start(bf16[352,1024]{1,0:T(8,128)(2,1)} %get-tuple-element.38), channel_id=1, source_target_pairs={{0,4},{4,0},{8,12},{12,8},{16,20},{20,16},{24,28},{28,24},{1,5},{5... | collective-permute-start | bytes 2162696 | tf_op jit(solution)/shard_map/ppermute | solution.py:250
  84.7 10.7 %collective-permute-start.23 = (bf16[176,1024]{1,0:T(8,128)(2,1)}, bf16[176,1024]{1,0:T(8,128)(2,1)S(1)}, u32[]{:S(2)}, u32[]{:S(2)}) collective-permute-start(bf16[176,1024]{1,0:T(8,128)(2,1)} %get-tuple-element.32), channel_id=1, source_target_pairs={{16,0},{20,4},{24,8},{28,12},{0,16},{4,20},{8,24},{12,28},{17,1},{... | collective-permute-start | bytes 1081352 | tf_op jit(solution)/shard_map/ppermute | solution.py:238
  86.3 11.6 %collective-permute-start.20 = (bf16[176,256]{1,0:T(8,128)(2,1)S(1)}, bf16[176,256]{1,0:T(8,128)(2,1)S(1)}, u32[]{:S(2)}, u32[]{:S(2)}) collective-permute-start(bf16[176,256]{1,0:T(8,128)(2,1)S(1)} %get-tuple-element.44), channel_id=1, source_target_pairs={{1,0},{2,1},{3,2},{0,3},{5,4},{6,5},{7,6},{4,7},{9,8},{10,9},{11,1... | collective-permute-start | bytes 270344 | tf_op jit(solution)/shard_map/ppermute | solution.py:253
  88.6 10.5 %collective-permute-start.21 = (bf16[176,256]{1,0:T(8,128)(2,1)S(1)}, bf16[176,256]{1,0:T(8,128)(2,1)S(1)}, u32[]{:S(2)}, u32[]{:S(2)}) collective-permute-start(bf16[176,256]{1,0:T(8,128)(2,1)S(1)} %get-tuple-element.46), channel_id=1, source_target_pairs={{2,0},{3,1},{0,2},{1,3},{6,4},{7,5},{4,6},{5,7},{10,8},{11,9},{8,1... | collective-permute-start | bytes 270344 | tf_op jit(solution)/shard_map/ppermute | solution.py:253
  89.6 11.5 %collective-permute-start.22 = (bf16[176,256]{1,0:T(8,128)(2,1)S(1)}, bf16[176,256]{1,0:T(8,128)(2,1)S(1)}, u32[]{:S(2)}, u32[]{:S(2)}) collective-permute-start(bf16[176,256]{1,0:T(8,128)(2,1)S(1)} %get-tuple-element.45), channel_id=1, source_target_pairs={{3,0},{0,1},{1,2},{2,3},{7,4},{4,5},{5,6},{6,7},{11,8},{8,9},{9,10... | collective-permute-start | bytes 270344 | tf_op jit(solution)/shard_map/ppermute | solution.py:253
  95.4 17.3 %collective-permute-start.29 = (bf16[352,1024]{1,0:T(8,128)(2,1)S(1)}, bf16[352,1024]{1,0:T(8,128)(2,1)S(1)}, u32[]{:S(2)}, u32[]{:S(2)}) collective-permute-start(bf16[352,1024]{1,0:T(8,128)(2,1)S(1)} %add_convert_fusion.1), channel_id=1, source_target_pairs={{8,0},{12,4},{0,8},{4,12},{24,16},{28,20},{16,24},{20,28},{9,1},{1... | collective-permute-start | bytes 2162696 | tf_op jit(solution)/shard_map/ppermute | solution.py:247
  97.9 5.2 %collective-permute-start.24 = (bf16[176,256]{1,0:T(8,128)(2,1)S(1)}, bf16[176,256]{1,0:T(8,128)(2,1)S(1)}, u32[]{:S(2)}, u32[]{:S(2)}) collective-permute-start(bf16[176,256]{1,0:T(8,128)(2,1)S(1)} %get-tuple-element.47), channel_id=1, source_target_pairs={{1,0},{2,1},{3,2},{0,3},{5,4},{6,5},{7,6},{4,7},{9,8},{10,9},{11,1... | collective-permute-start | bytes 270344 | tf_op jit(solution)/shard_map/ppermute | solution.py:253
  99.1 9.2 %collective-permute-start.25 = (bf16[176,256]{1,0:T(8,128)(2,1)S(1)}, bf16[176,256]{1,0:T(8,128)(2,1)S(1)}, u32[]{:S(2)}, u32[]{:S(2)}) collective-permute-start(bf16[176,256]{1,0:T(8,128)(2,1)S(1)} %get-tuple-element.49), channel_id=1, source_target_pairs={{2,0},{3,1},{0,2},{1,3},{6,4},{7,5},{4,6},{5,7},{10,8},{11,9},{8,1... | collective-permute-start | bytes 270344 | tf_op jit(solution)/shard_map/ppermute | solution.py:253
  101.1 7.2 %collective-permute-start.26 = (bf16[176,256]{1,0:T(8,128)(2,1)S(1)}, bf16[176,256]{1,0:T(8,128)(2,1)S(1)}, u32[]{:S(2)}, u32[]{:S(2)}) collective-permute-start(bf16[176,256]{1,0:T(8,128)(2,1)S(1)} %get-tuple-element.48), channel_id=1, source_target_pairs={{3,0},{0,1},{1,2},{2,3},{7,4},{4,5},{5,6},{6,7},{11,8},{8,9},{9,10... | collective-permute-start | bytes 270344 | tf_op jit(solution)/shard_map/ppermute | solution.py:253
  (29 other events, 305.9 us)

commit v2 on v1

--- a/solution.py
+++ b/solution.py
@@ -125,36 +125,35 @@
     groups, width = lay["groups"], lay["width"]
     args = Operands(refs)
     place, cap_x, img_x = args.one(), args.take(n_cap), args.take(n_img)
-    own_c, pieces_c = args.one(), args.take(len(groups) * n_pc)
-    own_i, pieces_i = args.one(), args.take(len(groups) * n_pi)
-    first, last, weight, position, factors = args.take(5)
+    head_c, pieces_c = args.one(), args.take(len(groups) * n_pc)
+    head_i, pieces_i = args.one(), args.take(len(groups) * n_pi)
+    table, position, factors = args.take(3)
     out_img = args.take(n_img * PARTS)
-    out_coef, out_zi, out_rc, out_sc, out_wc, out_wi = args.take(6)
-    xc, xi, zc, zi, raw_c, raw, sc_c, scales, wc, wi, logits, coef, dz, along, sem = args.take(15)
+    out_core, out_next, out_own, out_wc, out_wi = args.take(5)
+    xc, xi, zc, zi, raw_c, raw, sc_c, scales, wc, wi, bounds, logits, coef, dz, dzc, along = args.take(16)
+    img_sums = args.take(n_img * PARTS)
+    to_core, to_next, own, sem = args.take(4)
 
     moves = Copies(sem)
-    heads_c = place_weight(moves, own_c, pieces_c, groups, wc, n_pc, width, place, 0)
+    heads_c = place_weight(moves, head_c, pieces_c, groups, wc, n_pc, width, place, 0)
     features_c = [moves.start(cap_x[q], xc.at[pl.ds(q * rows, rows), :]) for q in range(n_cap)]
-    heads_i = place_weight(moves, own_i, pieces_i, groups, wi, n_pi, width, place, n_pc)
+    heads_i = place_weight(moves, head_i, pieces_i, groups, wi, n_pi, width, place, n_pc)
     features_i = [moves.start(img_x[q], xi.at[pl.ds(q * img_rows, img_rows), :]) for q in range(n_img)]
     wait_all(heads_c)
     outs = [moves.start(wc, out_wc)]
     for q in range(n_cap):
         features_c[q].wait()
         forward(xc, wc, raw_c, zc, sc_c, q * rows, rows)
-        here = pl.ds(q * rows, rows)
-        outs.append(moves.start(raw_c.at[here, :], out_rc.at[here, :]))
-    outs.append(moves.start(sc_c, out_sc))
     wait_all(heads_i)
     outs.append(moves.start(wi, out_wi))
     for q in range(n_img):
         features_i[q].wait()
         forward(xi, wi, raw, zi, scales, q * img_rows, img_rows)
-    outs.append(moves.start(zi, out_zi))
 
     sharp = factors[0]
     slope, level = -LOG2E * sharp, -LOG2E * factors[1]
     spot = position[...]
+    bounds[...] = jnp.transpose(table[...])
     columns = n_cap * rows
     for j in range(n_img):
         base = j * img_rows
@@ -167,9 +166,8 @@
 
             @pl.when(touched)
             def _():
-                lo = first[pl.ds(here, CHUNK), :]
-                hi = last[pl.ds(here, CHUNK), :]
-                plus = weight[pl.ds(here, CHUNK), :]
+                bound = bounds[pl.ds(here, CHUNK), :]
+                lo, hi, plus = bound[:, 0:1], bound[:, 1:2], bound[:, 2:3]
                 for c in range(0, columns, 128):
                     value = logits[line, pl.ds(c, 128)] * slope + level
                     col = spot[:, c : c + 128]
@@ -187,27 +185,22 @@
             return 0
 
         lax.fori_loop(0, img_rows // CHUNK, chunk, 0)
-        outs.append(moves.start(coef.at[pl.ds(base, img_rows), :], out_coef.at[pl.ds(base, img_rows), :]))
+        if j == n_img - 1:
+            dzc[...] = contract_first(coef[...], zi[...])
+            others = (n_cap // 2 - 1) * rows
+            back(dzc, raw_c, sc_c, 0, 0, others, to_core.at[pl.ds(0, others), :], along)
+            back(dzc, raw_c, sc_c, 0, 2 * others, rows, to_core.at[pl.ds(others, rows), :], along)
+            outs.append(moves.start(to_core, out_core))
+            if others:
+                back(dzc, raw_c, sc_c, 0, others, others, to_next, along)
+                outs.append(moves.start(to_next, out_next))
+            back(dzc, raw_c, sc_c, 0, 2 * others + rows, rows, own, along)
+            outs.append(moves.start(own, out_own))
         dz[...] = jnp.dot(coef[pl.ds(base, img_rows), :], zc[...], preferred_element_type=F32)
         for p, (top, height) in enumerate(split_rows(img_rows)):
-            back(dz, raw, scales, base, top, height, out_img[j * PARTS + p], along)
-    wait_all(outs)
-
-
-def caption_kernel(span, heights, coef_in, zi_in, rc_in, sc_in, *refs):
-    results, (coef, zi, raw, scales, dz, along), sums, sem = refs[:2], refs[2:8], refs[8:10], refs[10]
-    low, high, top = span
-    moves = Copies(sem)
-    early = [moves.start(zi_in, zi), moves.start(coef_in.at[:, pl.ds(low, high - low)], coef)]
-    late = [moves.start(sc_in.at[pl.ds(low, high - low), :], scales), moves.start(rc_in.at[pl.ds(low, high - low), :], raw)]
-    wait_all(early)
-    dz[...] = contract_first(coef[...], zi[...])
-    wait_all(late)
-    outs, offset = [], top - low
-    for n, height in enumerate(heights):
-        back(dz, raw, scales, 0, offset, height, sums[n], along)
-        outs.append(moves.start(sums[n], results[n]))
-        offset += height
+            n = j * PARTS + p
+            back(dz, raw, scales, base, top, height, img_sums[n], along)
+            outs.append(moves.start(img_sums[n], out_img[n]))
     wait_all(outs)
 
 
@@ -268,20 +261,21 @@
     ends = jnp.cumsum(counts)
     starts = ends - counts
 
-    def of_image(values):
-        blocks = []
-        for k in list(range(1, n_y)) + [0]:
-            owner = number((pos_y + k) % n_y, pos_x, core)
-            blocks.append(lax.dynamic_slice_in_dim(values, owner * img_rows, img_rows))
-        return jnp.concatenate(blocks)[:, None]
-
-    first = of_image(starts)
-    last = of_image(ends)
-    weight = -sharp[0] / of_image(counts).astype(F32)
+    weights = -sharp[0] / counts.astype(F32)
+    limits = jnp.stack([starts.astype(F32), ends.astype(F32), weights] + [weights] * 5)
+    n_rows = n_y * img_rows
+    padded = -(-n_rows // 128) * 128
+    near_y = [number((pos_y + k) % n_y, pos_x, core) for k in list(range(1, n_y)) + [0]]
+    table = jnp.concatenate(
+        [lax.dynamic_slice_in_dim(limits, owner * img_rows, img_rows, axis=1) for owner in near_y]
+        + ([jnp.zeros((8, padded - n_rows), F32)] if padded > n_rows else []),
+        axis=1,
+    )
     order = [(k, c) for c in (1 - core, core) for k in range(1, n_x)] + [(0, 1 - core), (0, core)]
     heads = [(number(pos_y, (pos_x + k) % n_x, c) * slots + mine) * rows for k, c in order]
-    position = jnp.concatenate([head + jnp.arange(rows, dtype=jnp.int32) for head in heads])[None, :]
-    low, high = first[::CHUNK, 0], last[CHUNK - 1 :: CHUNK, 0]
+    position = jnp.concatenate([head + jnp.arange(rows, dtype=jnp.int32) for head in heads]).astype(F32)[None, :]
+    low = table[0, :n_rows].reshape(-1, CHUNK)[:, 0]
+    high = table[1, :n_rows].reshape(-1, CHUNK)[:, -1]
     touched = functools.reduce(jnp.logical_or, [(low < head + rows) & (high > head) for head in heads])
     place = jnp.concatenate([place, touched.astype(jnp.int32)])
     factors = jnp.concatenate([sharp, shift])
@@ -296,9 +290,9 @@
         ]
     )
     slices = {k: from_z(own, k) for k in near}
-    tables = (place, first, last, weight, position)
+    tables = (place, table, position, factors)
     own, _, tables = lax.optimization_barrier((own, tuple(slices.values()), tables))
-    place, first, last, weight, position = tables
+    place, table, position, factors = tables
     slices[far] = from_z(own, far)
 
     cap_pieces, img_pieces = [], []
@@ -331,24 +325,19 @@
     pair = 2 * c_rows * i_rows * full
     heights = [height for _, height in split_rows(img_rows)]
     n_out = n_img * PARTS
-    n_copies = 2 + (slots - 1) * (n_pc + n_pi) + 2 * n_cap + 2 * n_img + 4
+    n_copies = 2 + (slots - 1) * (n_pc + n_pi) + n_cap + n_img + n_img * PARTS + 5
     operands = [place] + cap_all + img_all + [cap_w] + cap_pieces + [img_w] + img_pieces
-    specs = [smem] + [hbm] * (len(operands) - 1) + [vmem] * 4 + [smem]
-    operands += [first, last, weight, position, factors]
+    specs = [smem] + [hbm] * (len(operands) - 1) + [vmem] * 2 + [smem]
+    operands += [table, position, factors]
     n_send = (n_img - 1) * PARTS
+    others = (n_x - 1) * rows
+    results = [((heights[n % PARTS], full), BF16 if n < n_send else F32) for n in range(n_out)]
+    results += [((n_x * rows, full), BF16), ((max(others, 16), full), F32), ((rows, full), F32)]
     made = pl.pallas_call(
         functools.partial(pair_kernel, lay),
-        out_shape=tuple(of((heights[n % PARTS], full), BF16 if n < n_send else F32) for n in range(n_out))
-        + (
-            of((i_rows, c_rows), BF16),
-            of((i_rows, full), BF16),
-            of((c_rows, full), F32),
-            of((c_rows, 128), F32),
-            of((depth, full), BF16),
-            of((depth, full), BF16),
-        ),
+        out_shape=tuple(of(*kind) for kind in results + [((depth, full), BF16)] * 2),
         in_specs=specs,
-        out_specs=[vmem] * n_out + [hbm] * 6,
+        out_specs=[hbm] * (len(results) + 2),
         scratch_shapes=[
             pltpu.VMEM((c_rows, depth), BF16),
             pltpu.VMEM((i_rows, depth), BF16),
@@ -360,61 +349,34 @@
             pltpu.VMEM((i_rows, 128), F32),
             pltpu.VMEM((depth, full), BF16),
             pltpu.VMEM((depth, full), BF16),
+            pltpu.VMEM((padded, 8), F32),
             pltpu.VMEM((img_rows, c_rows), F32),
             pltpu.VMEM((i_rows, c_rows), BF16),
             pltpu.VMEM((img_rows, full), F32),
-            pltpu.VMEM((img_rows, 128), F32),
+            pltpu.VMEM((c_rows, full), F32),
+            pltpu.VMEM((max(img_rows, c_rows), 128), F32),
+            *(pltpu.VMEM(*kind) for kind in results),
             pltpu.SemaphoreType.DMA((n_copies,)),
         ],
-        compiler_params=params(60),
-        cost_estimate=cost((c_rows + i_rows) * depth * full * 2 + 2 * pair, 20),
+        compiler_params=params(46),
+        cost_estimate=cost((c_rows + i_rows) * depth * full * 2 + 3 * pair, 20),
         name="pairs",
     )(*operands)
     img_send, img_own = made[:n_send], made[n_send:n_out]
-    coef, zi, raw_c, sc_c, wc, wi = made[n_out:]
+    to_core, to_next, cap_own, wc, wi = made[n_out:]
 
     img_sent = []
     for p in range(PARTS):
         parts = [img_send[(k - 1) * PARTS + p] for k in range(1, n_y)]
         img_sent.append([from_y(parts[k - 1], n_y - k) for k in range(1, n_y)])
 
-    def caption_sums(top, heights):
-        low = top // 128 * 128
-        high = min(-(-(top + sum(heights)) // 128) * 128, c_rows)
-        span = high - low
-        return pl.pallas_call(
-            functools.partial(caption_kernel, (low, high, top), heights),
-            out_shape=(of((heights[0], full), BF16), of((heights[1], full), F32)),
-            in_specs=[hbm] * 4,
-            out_specs=[hbm] * 2,
-            scratch_shapes=[
-                pltpu.VMEM((i_rows, span), BF16),
-                pltpu.VMEM((i_rows, full), BF16),
-                pltpu.VMEM((span, full), F32),
-                pltpu.VMEM((span, 128), F32),
-                pltpu.VMEM((span, full), F32),
-                pltpu.VMEM((span, 128), F32),
-                pltpu.VMEM((heights[0], full), BF16),
-                pltpu.VMEM((heights[1], full), F32),
-                pltpu.SemaphoreType.DMA((6,)),
-            ],
-            compiler_params=params(60),
-            cost_estimate=cost(2 * span * i_rows * full, 10),
-            name="captions",
-        )(coef, zi, raw_c, sc_c)
-
-    others = (n_x - 1) * rows
+    crossed = from_core(to_core)
     arrived = []
-    if others:
-        to_core, to_next = caption_sums(0, (others, others))
-        crossed = from_core(to_core)
-        for k in range(1, n_x):
-            here = slice((k - 1) * rows, k * rows)
-            sent = (to_next[here] + crossed[here].astype(F32)).astype(BF16)
-            arrived.append(from_x(sent, n_x - k))
-    to_core, cap_own = caption_sums(2 * others, (rows, rows))
-    crossed = from_core(to_core)
-    cap_total = functools.reduce(lambda a, b: a + b.astype(F32), arrived, cap_own + crossed.astype(F32))
+    for k in range(1, n_x):
+        here = slice((k - 1) * rows, k * rows)
+        sent = (to_next[here] + crossed[here].astype(F32)).astype(BF16)
+        arrived.append(from_x(sent, n_x - k))
+    cap_total = functools.reduce(lambda a, b: a + b.astype(F32), arrived, cap_own + crossed[others:].astype(F32))
     grad_cap = contract_last(cap_total.astype(BF16), wc).astype(BF16)
 
     share = depth // slots

time: 115 us -> 109 us (0.948)
  Pallas kernels: 30.1 us -> 21.2 us
  waiting for transfers between devices: 40.6 us -> 46 us
  local copies, waits for them, and re-layouts: 7.58 us -> 3.03 us
  matrix products: 3.52 us -> 6.4 us
    pallas_call x3 -> x1, Pallas kernels: 30.1 us -> 21.2 us  [whole(): pl.pallas_call(functools.partial(pair_kernel, lay), out_shape=tuple((of(*...]
    ppermute x5, waiting for transfers between devices: 12.8 us -> 16.9 us  [from_y(): return lax.ppermute(value, 'dp', pairs)]
    dot_general x3, matrix products: 3.52 us -> 6.4 us  [contract_last(): lax.dot_general(a, b, (((1,), (1,)), ((), ())), preferred_element_type=F32)]
    ppermute x4, waiting for transfers between devices: 10.4 us -> 8.21 us  [from_x(): return lax.ppermute(value, 'dp', pairs)]
    ppermute x9, waiting for transfers between devices: 16.2 us -> 18.4 us  [from_z(): lax.ppermute(value, 'tensor', [((t + k) % slots, t) for t in range(slots)])]
    optimization_barrier x2 -> x0, local copies, waits for them, and re-layouts: 1.86 us -> none  [whole(): lax.optimization_barrier((own, tuple(slices.values()), tables))]
    ppermute x12 -> x11, waiting for transfers between devices: 1.21 us -> 2.47 us  [from_core(): return lax.ppermute(value, 'dp', [(s, s ^ 1) for s in range(n_dp)])]
    convert_element_type x1, other arithmetic: 0.26 us -> 1.51 us  [whole(): sent = (to_next[here] + crossed[here].astype(F32)).astype(BF16)]
  transfers between devices with their start and end apart: 30 -> 29, of which waited for: 12 -> 18; matrix products, arithmetic and copies ran while one was open for 10% -> 8% of each run, Pallas kernels for 9% -> 0%
where the time goes in v2:
time: 109 us
  waiting for transfers between devices  46 us (42%)
  starting transfers between devices  25.7 us (24%)
  Pallas kernels  21.2 us (19%)
  matrix products  6.4 us (6%)
  other arithmetic  4.54 us (4%)
  local copies, waits for them, and re-layouts  3.03 us (3%)
  between operations  2.31 us (2%)
    pallas_call x1, Pallas kernels, whole(): pl.pallas_call(functools.partial(pair_kernel, lay), out_shape=tuple((of(*...  21.2 us
    ppermute x9, waiting for transfers between devices, from_z(): lax.ppermute(value, 'tensor', [((t + k) % slots, t) for t in range(slots)])  18.4 us
    ppermute x5, waiting for transfers between devices, from_y(): return lax.ppermute(value, 'dp', pairs)  16.9 us
    ppermute x9, starting transfers between devices, from_z(): lax.ppermute(value, 'tensor', [((t + k) % slots, t) for t in range(slots)])  13 us
    ppermute x4, waiting for transfers between devices, from_x(): return lax.ppermute(value, 'dp', pairs)  8.21 us
    dot_general x3, matrix products, contract_last(): lax.dot_general(a, b, (((1,), (1,)), ((), ())), preferred_element_type=F32)  6.4 us
    ppermute x5, starting transfers between devices, from_y(): return lax.ppermute(value, 'dp', pairs)  5.64 us
    ppermute x4, starting transfers between devices, from_x(): return lax.ppermute(value, 'dp', pairs)  5.14 us
  transfers between devices with their start and end apart: 29, of which 18 were waited for; matrix products, arithmetic and copies ran while one was open for 8% of the time, Pallas kernels for 0%

profile of v2, /device:TPU:0, one launch (start us, length us, event | category | flops | bytes accessed | tf_op | source)
XLA Modules:
  0.0 109.1 jit_solution(5033077829619048800)
XLA Ops:
  1.7 5.1 %collective-permute-start = (bf16[512,256]{1,0:T(8,128)(2,1)S(1)}, bf16[512,256]{1,0:T(8,128)(2,1)S(1)}, u32[]{:S(2)}, u32[]{:S(2)}) collective-permute-start(bf16[512,256]{1,0:T(8,128)(2,1)S(1)} %pad_maximum_fusion), channel_id=1, source_target_pairs={{1,0},{2,1},{3,2},{0,3},{5,4},{6,5},{7,6},{4,7},{9,8},{10,9},{11,1... | collective-permute-start | bytes 786440 | tf_op jit(solution)/shard_map/ppermute | solution.py:246
  6.9 1.5 %collective-permute-start.2 = (bf16[352,1024]{1,0:T(8,128)(2,1)}, bf16[352,1024]{1,0:T(8,128)(2,1)S(1)}, u32[]{:S(2)}, u32[]{:S(2)}) collective-permute-start(bf16[352,1024]{1,0:T(8,128)(2,1)} %refs_4_.1), channel_id=1, source_target_pairs={{8,0},{12,4},{0,8},{4,12},{24,16},{28,20},{16,24},{20,28},{9,1},{1... | collective-permute-start | bytes 2162696 | tf_op jit(solution)/shard_map/ppermute | solution.py:240
  13.6 5.4 %collective-permute-done.1 = bf16[512,256]{1,0:T(8,128)(2,1)S(1)} collective-permute-done((bf16[512,256]{1,0:T(8,128)(2,1)S(1)}, bf16[512,256]{1,0:T(8,128)(2,1)S(1)}, u32[]{:S(2)}, u32[]{:S(2)}) %collective-permute-start.1) | collective-permute-done | bytes 262176 | tf_op jit(solution)/shard_map/ppermute | solution.py:246
  19.0 1.6 %collective-permute-start.13 = (bf16[512,256]{1,0:T(8,128)(2,1)S(1)}, bf16[512,256]{1,0:T(8,128)(2,1)S(1)}, u32[]{:S(2)}, u32[]{:S(2)}) collective-permute-start(bf16[512,256]{1,0:T(8,128)(2,1)S(1)} %pad_maximum_fusion.2.refs_17_), channel_id=1, source_target_pairs={{16,0},{20,4},{24,8},{28,12},{0,16},{4,20},{8,24},{12,28},{17,1},{... | collective-permute-start | bytes 786440 | tf_op jit(solution)/shard_map/ppermute | solution.py:231
  20.6 1.6 %collective-permute-start.6 = (bf16[512,256]{1,0:T(8,128)(2,1)S(1)}, bf16[512,256]{1,0:T(8,128)(2,1)S(1)}, u32[]{:S(2)}, u32[]{:S(2)}) collective-permute-start(bf16[512,256]{1,0:T(8,128)(2,1)S(1)} %pad_maximum_fusion.1.refs_8_), channel_id=1, source_target_pairs={{8,0},{12,4},{0,8},{4,12},{24,16},{28,20},{16,24},{20,28},{9,1},{1... | collective-permute-start | bytes 786440 | tf_op jit(solution)/shard_map/ppermute | solution.py:240
  22.9 3.4 %collective-permute-done.13.refs_18_ = bf16[512,256]{1,0:T(8,128)(2,1)S(1)} collective-permute-done((bf16[512,256]{1,0:T(8,128)(2,1)S(1)}, bf16[512,256]{1,0:T(8,128)(2,1)S(1)}, u32[]{:S(2)}, u32[]{:S(2)}) %collective-permute-start.13) | collective-permute-done | bytes 262176 | tf_op jit(solution)/shard_map/ppermute | solution.py:231
  26.2 1.5 %collective-permute-start.5 = (bf16[352,1024]{1,0:T(8,128)(2,1)}, bf16[352,1024]{1,0:T(8,128)(2,1)S(1)}, u32[]{:S(2)}, u32[]{:S(2)}) collective-permute-start(bf16[352,1024]{1,0:T(8,128)(2,1)} %refs_6_.1), channel_id=1, source_target_pairs={{16,0},{20,4},{24,8},{28,12},{0,16},{4,20},{8,24},{12,28},{17,1},{... | collective-permute-start | bytes 2162696 | tf_op jit(solution)/shard_map/ppermute | solution.py:231
  27.8 2.5 %collective-permute-done.6.refs_9_ = bf16[512,256]{1,0:T(8,128)(2,1)S(1)} collective-permute-done((bf16[512,256]{1,0:T(8,128)(2,1)S(1)}, bf16[512,256]{1,0:T(8,128)(2,1)S(1)}, u32[]{:S(2)}, u32[]{:S(2)}) %collective-permute-start.6) | collective-permute-done | bytes 262176 | tf_op jit(solution)/shard_map/ppermute | solution.py:240
  30.3 5.0 %collective-permute-done.9 = bf16[512,256]{1,0:T(8,128)(2,1)S(1)} collective-permute-done((bf16[512,256]{1,0:T(8,128)(2,1)S(1)}, bf16[512,256]{1,0:T(8,128)(2,1)S(1)}, u32[]{:S(2)}, u32[]{:S(2)}) %collective-permute-start.9) | collective-permute-done | bytes 262176 | tf_op jit(solution)/shard_map/ppermute | solution.py:246
  37.3 4.0 %collective-permute-done.10.refs_13_ = bf16[256,256]{1,0:T(8,128)(2,1)S(1)} collective-permute-done((bf16[256,256]{1,0:T(8,128)(2,1)S(1)}, bf16[256,256]{1,0:T(8,128)(2,1)S(1)}, u32[]{:S(2)}, u32[]{:S(2)}) %collective-permute-start.10) | collective-permute-done | bytes 131104 | tf_op jit(solution)/shard_map/ppermute | solution.py:240
  41.3 4.1 %collective-permute-done.16.refs_22_ = bf16[256,256]{1,0:T(8,128)(2,1)S(1)} collective-permute-done((bf16[256,256]{1,0:T(8,128)(2,1)S(1)}, bf16[256,256]{1,0:T(8,128)(2,1)S(1)}, u32[]{:S(2)}, u32[]{:S(2)}) %collective-permute-start.16) | collective-permute-done | bytes 131104 | tf_op jit(solution)/shard_map/ppermute | solution.py:231
  48.7 21.2 %pairs.1 = (bf16[176,1024]{1,0:T(8,128)(2,1)}, bf16[176,1024]{1,0:T(8,128)(2,1)S(1)}, f32[176,1024]{1,0:T(8,128)S(1)}, f32[176,1024]{1,0:T(8,128)S(1)}, bf16[704...) custom-call(s32[30]{0:T(128)S(1)} %concatenate.45.refs_0_, ...), custom_call_target="tpu_custom_call" | custom-call | flops 10519314432 | bytes 20971520 | tf_op jit(solution)/shard_map/pairs/pallas_call | solution.py:336
  70.8 1.5 %collective-permute-start.19 = (bf16[176,1024]{1,0:T(8,128)(2,1)}, bf16[176,1024]{1,0:T(8,128)(2,1)S(1)}, u32[]{:S(2)}, u32[]{:S(2)}) collective-permute-start(bf16[176,1024]{1,0:T(8,128)(2,1)} %get-tuple-element.22), channel_id=1, source_target_pairs={{16,0},{20,4},{24,8},{28,12},{0,16},{4,20},{8,24},{12,28},{17,1},{... | collective-permute-start | bytes 1081352 | tf_op jit(solution)/shard_map/ppermute | solution.py:231
  72.8 9.5 %collective-permute-done.19 = bf16[176,1024]{1,0:T(8,128)(2,1)S(1)} collective-permute-done((bf16[176,1024]{1,0:T(8,128)(2,1)}, bf16[176,1024]{1,0:T(8,128)(2,1)S(1)}, u32[]{:S(2)}, u32[]{:S(2)}) %collective-permute-start.19) | collective-permute-done | bytes 360480 | tf_op jit(solution)/shard_map/ppermute | solution.py:231
  82.3 2.6 %fusion.1 = f32[176,1024]{1,0:T(8,128)S(1)} fusion(bf16[1024,1024]{1,0:T(8,128)(2,1)} %get-tuple-element.23, f32[176,1024]{1,0:T(8,128)S(1)} %get-tuple-element.21, bf16[176,1024]{1,0:T(8,128)(2,1)S(1)} %collective-permute-done.19), kind=kOutput, calls=%fused_computation.6 | convolution fusion | flops 369639424 | bytes 3899392 | tf_op jit(solution)/shard_map/dot_general | solution.py:22
  84.9 2.3 %collective-permute-start.20 = (bf16[176,256]{1,0:T(8,128)(2,1)S(1)}, bf16[176,256]{1,0:T(8,128)(2,1)S(1)}, u32[]{:S(2)}, u32[]{:S(2)}) collective-permute-start(bf16[176,256]{1,0:T(8,128)(2,1)S(1)} %get-tuple-element.32), channel_id=1, source_target_pairs={{1,0},{2,1},{3,2},{0,3},{5,4},{6,5},{7,6},{4,7},{9,8},{10,9},{11,1... | collective-permute-start | bytes 270344 | tf_op jit(solution)/shard_map/ppermute | solution.py:246
  88.2 1.5 %add_convert_fusion.1 = bf16[352,1024]{1,0:T(8,128)(2,1)S(1)} fusion(f32[352,1024]{1,0:T(8,128)S(1)} %copy-done.4, bf16[704,1024]{1,0:T(8,128)(2,1)} %collective-permute-done.27), kind=kLoop, calls=%fused_computation.1 | loop fusion | flops 1081344 | bytes 2883584 | tf_op jit(solution)/shard_map/convert_element_type | solution.py:377
  89.7 1.5 %collective-permute-start.28 = (bf16[352,1024]{1,0:T(8,128)(2,1)S(1)}, bf16[352,1024]{1,0:T(8,128)(2,1)S(1)}, u32[]{:S(2)}, u32[]{:S(2)}) collective-permute-start(bf16[352,1024]{1,0:T(8,128)(2,1)S(1)} %add_convert_fusion.1), channel_id=1, source_target_pairs={{8,0},{12,4},{0,8},{4,12},{24,16},{28,20},{16,24},{20,28},{9,1},{1... | collective-permute-start | bytes 2162696 | tf_op jit(solution)/shard_map/ppermute | solution.py:240
  92.2 3.9 %collective-permute-start.24 = (bf16[176,256]{1,0:T(8,128)(2,1)S(1)}, bf16[176,256]{1,0:T(8,128)(2,1)S(1)}, u32[]{:S(2)}, u32[]{:S(2)}) collective-permute-start(bf16[176,256]{1,0:T(8,128)(2,1)S(1)} %get-tuple-element.35), channel_id=1, source_target_pairs={{1,0},{2,1},{3,2},{0,3},{5,4},{6,5},{7,6},{4,7},{9,8},{10,9},{11,1... | collective-permute-start | bytes 270344 | tf_op jit(solution)/shard_map/ppermute | solution.py:246
  96.1 1.3 %collective-permute-done.21 = bf16[176,256]{1,0:T(8,128)(2,1)S(1)} collective-permute-done((bf16[176,256]{1,0:T(8,128)(2,1)S(1)}, bf16[176,256]{1,0:T(8,128)(2,1)S(1)}, u32[]{:S(2)}, u32[]{:S(2)}) %collective-permute-start.21) | collective-permute-done | bytes 90144 | tf_op jit(solution)/shard_map/ppermute | solution.py:246
  98.2 4.0 %collective-permute-done.25 = bf16[176,256]{1,0:T(8,128)(2,1)S(1)} collective-permute-done((bf16[176,256]{1,0:T(8,128)(2,1)S(1)}, bf16[176,256]{1,0:T(8,128)(2,1)S(1)}, u32[]{:S(2)}, u32[]{:S(2)}) %collective-permute-start.25) | collective-permute-done | bytes 90144 | tf_op jit(solution)/shard_map/ppermute | solution.py:246
  102.2 1.4 %collective-permute-done.26 = bf16[176,256]{1,0:T(8,128)(2,1)S(1)} collective-permute-done((bf16[176,256]{1,0:T(8,128)(2,1)S(1)}, bf16[176,256]{1,0:T(8,128)(2,1)S(1)}, u32[]{:S(2)}, u32[]{:S(2)}) %collective-permute-start.26) | collective-permute-done | bytes 90144 | tf_op jit(solution)/shard_map/ppermute | solution.py:246
  104.4 1.7 %collective-permute-done.28 = bf16[352,1024]{1,0:T(8,128)(2,1)S(1)} collective-permute-done((bf16[352,1024]{1,0:T(8,128)(2,1)S(1)}, bf16[352,1024]{1,0:T(8,128)(2,1)S(1)}, u32[]{:S(2)}, u32[]{:S(2)}) %collective-permute-start.28) | collective-permute-done | bytes 720928 | tf_op jit(solution)/shard_map/ppermute | solution.py:240
  106.1 3.0 %convolution_convert_fusion = bf16[352,1024]{1,0:T(8,128)(2,1)} fusion(bf16[1024,1024]{1,0:T(8,128)(2,1)S(1)} %copy-done.8, bf16[352,1024]{1,0:T(8,128)(2,1)S(1)} %collective-permute-done.28, f32[352,1024]{1,0:T(8,128)S(1)} %copy-done.9, bf16[704,1024]{1,0:T(8,128)(2,1)} %collective-permute-done.27), kind=kOutput, calls=%fused_computation.2 | convolution fusion | flops 740360192 | bytes 5701632 | tf_op jit(solution)/shard_map/dot_general | solution.py:22
  (105 shorter events, 15.9 us)
Async XLA Ops:
  1.7 11.8 %collective-permute-start = (bf16[512,256]{1,0:T(8,128)(2,1)S(1)}, bf16[512,256]{1,0:T(8,128)(2,1)S(1)}, u32[]{:S(2)}, u32[]{:S(2)}) collective-permute-start(bf16[512,256]{1,0:T(8,128)(2,1)S(1)} %pad_maximum_fusion), channel_id=1, source_target_pairs={{1,0},{2,1},{3,2},{0,3},{5,4},{6,5},{7,6},{4,7},{9,8},{10,9},{11,1... | collective-permute-start | bytes 786440 | tf_op jit(solution)/shard_map/ppermute | solution.py:246
  6.9 12.1 %collective-permute-start.1 = (bf16[512,256]{1,0:T(8,128)(2,1)S(1)}, bf16[512,256]{1,0:T(8,128)(2,1)S(1)}, u32[]{:S(2)}, u32[]{:S(2)}) collective-permute-start(bf16[512,256]{1,0:T(8,128)(2,1)S(1)} %pad_maximum_fusion), channel_id=1, source_target_pairs={{3,0},{0,1},{1,2},{2,3},{7,4},{4,5},{5,6},{6,7},{11,8},{8,9},{9,10... | collective-permute-start | bytes 786440 | tf_op jit(solution)/shard_map/ppermute | solution.py:246
  6.9 28.4 %collective-permute-start.2 = (bf16[352,1024]{1,0:T(8,128)(2,1)}, bf16[352,1024]{1,0:T(8,128)(2,1)S(1)}, u32[]{:S(2)}, u32[]{:S(2)}) collective-permute-start(bf16[352,1024]{1,0:T(8,128)(2,1)} %refs_4_.1), channel_id=1, source_target_pairs={{8,0},{12,4},{0,8},{4,12},{24,16},{28,20},{16,24},{20,28},{9,1},{1... | collective-permute-start | bytes 2162696 | tf_op jit(solution)/shard_map/ppermute | solution.py:240
  19.0 7.3 %collective-permute-start.13 = (bf16[512,256]{1,0:T(8,128)(2,1)S(1)}, bf16[512,256]{1,0:T(8,128)(2,1)S(1)}, u32[]{:S(2)}, u32[]{:S(2)}) collective-permute-start(bf16[512,256]{1,0:T(8,128)(2,1)S(1)} %pad_maximum_fusion.2.refs_17_), channel_id=1, source_target_pairs={{16,0},{20,4},{24,8},{28,12},{0,16},{4,20},{8,24},{12,28},{17,1},{... | collective-permute-start | bytes 786440 | tf_op jit(solution)/shard_map/ppermute | solution.py:231
  20.6 9.7 %collective-permute-start.6 = (bf16[512,256]{1,0:T(8,128)(2,1)S(1)}, bf16[512,256]{1,0:T(8,128)(2,1)S(1)}, u32[]{:S(2)}, u32[]{:S(2)}) collective-permute-start(bf16[512,256]{1,0:T(8,128)(2,1)S(1)} %pad_maximum_fusion.1.refs_8_), channel_id=1, source_target_pairs={{8,0},{12,4},{0,8},{4,12},{24,16},{28,20},{16,24},{20,28},{9,1},{1... | collective-permute-start | bytes 786440 | tf_op jit(solution)/shard_map/ppermute | solution.py:240
  22.2 13.1 %collective-permute-start.9 = (bf16[512,256]{1,0:T(8,128)(2,1)S(1)}, bf16[512,256]{1,0:T(8,128)(2,1)S(1)}, u32[]{:S(2)}, u32[]{:S(2)}) collective-permute-start(bf16[512,256]{1,0:T(8,128)(2,1)S(1)} %pad_maximum_fusion), channel_id=1, source_target_pairs={{2,0},{3,1},{0,2},{1,3},{6,4},{7,5},{4,6},{5,7},{10,8},{11,9},{8,1... | collective-permute-start | bytes 786440 | tf_op jit(solution)/shard_map/ppermute | solution.py:246
  22.9 24.0 %collective-permute-start.4 = (bf16[352,1024]{1,0:T(8,128)(2,1)}, bf16[352,1024]{1,0:T(8,128)(2,1)S(1)}, u32[]{:S(2)}, u32[]{:S(2)}) collective-permute-start(bf16[352,1024]{1,0:T(8,128)(2,1)} %refs_4_.1), channel_id=1, source_target_pairs={{0,4},{4,0},{8,12},{12,8},{16,20},{20,16},{24,28},{28,24},{1,5},{5... | collective-permute-start | bytes 2162696 | tf_op jit(solution)/shard_map/ppermute | solution.py:243
  26.2 21.1 %collective-permute-start.5 = (bf16[352,1024]{1,0:T(8,128)(2,1)}, bf16[352,1024]{1,0:T(8,128)(2,1)S(1)}, u32[]{:S(2)}, u32[]{:S(2)}) collective-permute-start(bf16[352,1024]{1,0:T(8,128)(2,1)} %refs_6_.1), channel_id=1, source_target_pairs={{16,0},{20,4},{24,8},{28,12},{0,16},{4,20},{8,24},{12,28},{17,1},{... | collective-permute-start | bytes 2162696 | tf_op jit(solution)/shard_map/ppermute | solution.py:231
  30.3 5.6 %collective-permute-start.14 = (bf16[512,256]{1,0:T(8,128)(2,1)S(1)}, bf16[512,256]{1,0:T(8,128)(2,1)S(1)}, u32[]{:S(2)}, u32[]{:S(2)}) collective-permute-start(bf16[512,256]{1,0:T(8,128)(2,1)S(1)} %pad_maximum_fusion.2.refs_17_), channel_id=1, source_target_pairs={{0,4},{4,0},{8,12},{12,8},{16,20},{20,16},{24,28},{28,24},{1,5},{5... | collective-permute-start | bytes 786440 | tf_op jit(solution)/shard_map/ppermute | solution.py:243
  35.3 13.4 %collective-permute-start.3 = (bf16[352,1024]{1,0:T(8,128)(2,1)S(1)}, bf16[352,1024]{1,0:T(8,128)(2,1)S(1)}, u32[]{:S(2)}, u32[]{:S(2)}) collective-permute-start(bf16[352,1024]{1,0:T(8,128)(2,1)S(1)} %collective-permute-done.2.refs_2_), channel_id=1, source_target_pairs={{0,4},{4,0},{8,12},{12,8},{16,20},{20,16},{24,28},{28,24},{1,5},{5... | collective-permute-start | bytes 2162696 | tf_op jit(solution)/shard_map/ppermute | solution.py:243
  35.8 5.5 %collective-permute-start.10 = (bf16[256,256]{1,0:T(8,128)(2,1)S(1)}, bf16[256,256]{1,0:T(8,128)(2,1)S(1)}, u32[]{:S(2)}, u32[]{:S(2)}) collective-permute-start(bf16[256,256]{1,0:T(8,128)(2,1)S(1)} %get-tuple-element.39.refs_12_), channel_id=1, source_target_pairs={{8,0},{12,4},{0,8},{4,12},{24,16},{28,20},{16,24},{20,28},{9,1},{1... | collective-permute-start | bytes 393224 | tf_op jit(solution)/shard_map/ppermute | solution.py:240
  36.8 8.6 %collective-permute-start.16 = (bf16[256,256]{1,0:T(8,128)(2,1)S(1)}, bf16[256,256]{1,0:T(8,128)(2,1)S(1)}, u32[]{:S(2)}, u32[]{:S(2)}) collective-permute-start(bf16[256,256]{1,0:T(8,128)(2,1)S(1)} %get-tuple-element.38.refs_21_), channel_id=1, source_target_pairs={{16,0},{20,4},{24,8},{28,12},{0,16},{4,20},{8,24},{12,28},{17,1},{... | collective-permute-start | bytes 393224 | tf_op jit(solution)/shard_map/ppermute | solution.py:231
  41.3 4.1 %collective-permute-start.11 = (bf16[256,256]{1,0:T(8,128)(2,1)S(1)}, bf16[256,256]{1,0:T(8,128)(2,1)S(1)}, u32[]{:S(2)}, u32[]{:S(2)}) collective-permute-start(bf16[256,256]{1,0:T(8,128)(2,1)S(1)} %get-tuple-element.39.refs_12_), channel_id=1, source_target_pairs={{0,4},{4,0},{8,12},{12,8},{16,20},{20,16},{24,28},{28,24},{1,5},{5... | collective-permute-start | bytes 393224 | tf_op jit(solution)/shard_map/ppermute | solution.py:243
  45.4 2.0 %collective-permute-start.15 = (bf16[512,256]{1,0:T(8,128)(2,1)S(1)}, bf16[512,256]{1,0:T(8,128)(2,1)S(1)}, u32[]{:S(2)}, u32[]{:S(2)}) collective-permute-start(bf16[512,256]{1,0:T(8,128)(2,1)S(1)} %collective-permute-done.13.refs_18_), channel_id=1, source_target_pairs={{0,4},{4,0},{8,12},{12,8},{16,20},{20,16},{24,28},{28,24},{1,5},{5... | collective-permute-start | bytes 786440 | tf_op jit(solution)/shard_map/ppermute | solution.py:243
  70.6 17.6 %collective-permute-start.27 = (bf16[704,1024]{1,0:T(8,128)(2,1)}, bf16[704,1024]{1,0:T(8,128)(2,1)}, u32[]{:S(2)}, u32[]{:S(2)}) collective-permute-start(bf16[704,1024]{1,0:T(8,128)(2,1)} %get-tuple-element.27), channel_id=1, source_target_pairs={{0,4},{4,0},{8,12},{12,8},{16,20},{20,16},{24,28},{28,24},{1,5},{5... | collective-permute-start | bytes 4325384 | tf_op jit(solution)/shard_map/ppermute | solution.py:243
  70.8 11.5 %collective-permute-start.19 = (bf16[176,1024]{1,0:T(8,128)(2,1)}, bf16[176,1024]{1,0:T(8,128)(2,1)S(1)}, u32[]{:S(2)}, u32[]{:S(2)}) collective-permute-start(bf16[176,1024]{1,0:T(8,128)(2,1)} %get-tuple-element.22), channel_id=1, source_target_pairs={{16,0},{20,4},{24,8},{28,12},{0,16},{4,20},{8,24},{12,28},{17,1},{... | collective-permute-start | bytes 1081352 | tf_op jit(solution)/shard_map/ppermute | solution.py:231
  72.3 18.9 %collective-permute-start.23 = (bf16[176,1024]{1,0:T(8,128)(2,1)}, bf16[176,1024]{1,0:T(8,128)(2,1)S(1)}, u32[]{:S(2)}, u32[]{:S(2)}) collective-permute-start(bf16[176,1024]{1,0:T(8,128)(2,1)} %copy-done.2), channel_id=1, source_target_pairs={{16,0},{20,4},{24,8},{28,12},{0,16},{4,20},{8,24},{12,28},{17,1},{... | collective-permute-start | bytes 1081352 | tf_op jit(solution)/shard_map/ppermute | solution.py:231
  84.9 11.2 %collective-permute-start.20 = (bf16[176,256]{1,0:T(8,128)(2,1)S(1)}, bf16[176,256]{1,0:T(8,128)(2,1)S(1)}, u32[]{:S(2)}, u32[]{:S(2)}) collective-permute-start(bf16[176,256]{1,0:T(8,128)(2,1)S(1)} %get-tuple-element.32), channel_id=1, source_target_pairs={{1,0},{2,1},{3,2},{0,3},{5,4},{6,5},{7,6},{4,7},{9,8},{10,9},{11,1... | collective-permute-start | bytes 270344 | tf_op jit(solution)/shard_map/ppermute | solution.py:246
  87.2 10.2 %collective-permute-start.21 = (bf16[176,256]{1,0:T(8,128)(2,1)S(1)}, bf16[176,256]{1,0:T(8,128)(2,1)S(1)}, u32[]{:S(2)}, u32[]{:S(2)}) collective-permute-start(bf16[176,256]{1,0:T(8,128)(2,1)S(1)} %get-tuple-element.34), channel_id=1, source_target_pairs={{2,0},{3,1},{0,2},{1,3},{6,4},{7,5},{4,6},{5,7},{10,8},{11,9},{8,1... | collective-permute-start | bytes 270344 | tf_op jit(solution)/shard_map/ppermute | solution.py:246
  88.1 9.2 %collective-permute-start.22 = (bf16[176,256]{1,0:T(8,128)(2,1)S(1)}, bf16[176,256]{1,0:T(8,128)(2,1)S(1)}, u32[]{:S(2)}, u32[]{:S(2)}) collective-permute-start(bf16[176,256]{1,0:T(8,128)(2,1)S(1)} %get-tuple-element.33), channel_id=1, source_target_pairs={{3,0},{0,1},{1,2},{2,3},{7,4},{4,5},{5,6},{6,7},{11,8},{8,9},{9,10... | collective-permute-start | bytes 270344 | tf_op jit(solution)/shard_map/ppermute | solution.py:246
  89.7 16.4 %collective-permute-start.28 = (bf16[352,1024]{1,0:T(8,128)(2,1)S(1)}, bf16[352,1024]{1,0:T(8,128)(2,1)S(1)}, u32[]{:S(2)}, u32[]{:S(2)}) collective-permute-start(bf16[352,1024]{1,0:T(8,128)(2,1)S(1)} %add_convert_fusion.1), channel_id=1, source_target_pairs={{8,0},{12,4},{0,8},{4,12},{24,16},{28,20},{16,24},{20,28},{9,1},{1... | collective-permute-start | bytes 2162696 | tf_op jit(solution)/shard_map/ppermute | solution.py:240
  92.2 6.0 %collective-permute-start.24 = (bf16[176,256]{1,0:T(8,128)(2,1)S(1)}, bf16[176,256]{1,0:T(8,128)(2,1)S(1)}, u32[]{:S(2)}, u32[]{:S(2)}) collective-permute-start(bf16[176,256]{1,0:T(8,128)(2,1)S(1)} %get-tuple-element.35), channel_id=1, source_target_pairs={{1,0},{2,1},{3,2},{0,3},{5,4},{6,5},{7,6},{4,7},{9,8},{10,9},{11,1... | collective-permute-start | bytes 270344 | tf_op jit(solution)/shard_map/ppermute | solution.py:246
  96.1 6.2 %collective-permute-start.25 = (bf16[176,256]{1,0:T(8,128)(2,1)S(1)}, bf16[176,256]{1,0:T(8,128)(2,1)S(1)}, u32[]{:S(2)}, u32[]{:S(2)}) collective-permute-start(bf16[176,256]{1,0:T(8,128)(2,1)S(1)} %get-tuple-element.37), channel_id=1, source_target_pairs={{2,0},{3,1},{0,2},{1,3},{6,4},{7,5},{4,6},{5,7},{10,8},{11,9},{8,1... | collective-permute-start | bytes 270344 | tf_op jit(solution)/shard_map/ppermute | solution.py:246
  97.3 6.3 %collective-permute-start.26 = (bf16[176,256]{1,0:T(8,128)(2,1)S(1)}, bf16[176,256]{1,0:T(8,128)(2,1)S(1)}, u32[]{:S(2)}, u32[]{:S(2)}) collective-permute-start(bf16[176,256]{1,0:T(8,128)(2,1)S(1)} %get-tuple-element.36), channel_id=1, source_target_pairs={{3,0},{0,1},{1,2},{2,3},{7,4},{4,5},{5,6},{6,7},{11,8},{8,9},{9,10... | collective-permute-start | bytes 270344 | tf_op jit(solution)/shard_map/ppermute | solution.py:246
  (15 other events, 133.8 us)

commit v3 on v2

--- a/solution.py
+++ b/solution.py
@@ -12,7 +12,7 @@
 CORES = 2
 ROWS_Y = 2
 CHUNK = 32
-PARTS = 2
+PARTS = 3
 LOG2E = 1.4426950408889634
 F32 = jnp.float32
 BF16 = jnp.bfloat16
@@ -157,34 +157,18 @@
     columns = n_cap * rows
     for j in range(n_img):
         base = j * img_rows
-        logits[...] = contract_last(zi[pl.ds(base, img_rows), :], zc[...])
-
-        def chunk(r, _):
-            here = pl.multiple_of(base + r * CHUNK, 16)
-            line = pl.ds(pl.multiple_of(r * CHUNK, 16), CHUNK)
-            touched = place[n_pc + n_pi + j * (img_rows // CHUNK) + r] != 0
-
-            @pl.when(touched)
-            def _():
-                bound = bounds[pl.ds(here, CHUNK), :]
-                lo, hi, plus = bound[:, 0:1], bound[:, 1:2], bound[:, 2:3]
-                for c in range(0, columns, 128):
-                    value = logits[line, pl.ds(c, 128)] * slope + level
-                    col = spot[:, c : c + 128]
-                    inside = (col >= lo) & (col < hi)
-                    power = jnp.exp2(jnp.where(inside, -value, value))
-                    share = jnp.where(inside, plus, sharp) / (1.0 + power)
-                    coef[pl.ds(here, CHUNK), pl.ds(c, 128)] = share.astype(BF16)
-
-            @pl.when(jnp.logical_not(touched))
-            def _():
-                for c in range(0, columns, 128):
-                    power = jnp.exp2(logits[line, pl.ds(c, 128)] * slope + level)
-                    coef[pl.ds(here, CHUNK), pl.ds(c, 128)] = (sharp / (1.0 + power)).astype(BF16)
-
-            return 0
-
-        lax.fori_loop(0, img_rows // CHUNK, chunk, 0)
+        logits[base : base + img_rows, :] = contract_last(zi[base : base + img_rows, :], zc[...])
+    for j in range(n_img):
+        base = j * img_rows
+        for r in range(base, base + img_rows, 16):
+            bound = bounds[r : r + 16, :]
+            lo, hi, plus = bound[:, 0:1], bound[:, 1:2], bound[:, 2:3]
+            for c in range(0, columns, 128):
+                value = logits[r : r + 16, c : c + 128] * slope + level
+                col = spot[:, c : c + 128]
+                inside = (col >= lo) & (col < hi)
+                power = jnp.exp2(jnp.where(inside, -value, value))
+                coef[r : r + 16, c : c + 128] = (jnp.where(inside, plus, sharp) / (1.0 + power)).astype(BF16)
         if j == n_img - 1:
             dzc[...] = contract_first(coef[...], zi[...])
             others = (n_cap // 2 - 1) * rows
@@ -291,9 +275,9 @@
     )
     slices = {k: from_z(own, k) for k in near}
     tables = (place, table, position, factors)
-    own, _, tables = lax.optimization_barrier((own, tuple(slices.values()), tables))
+    slices[far] = from_z(own, far)
+    slices[near[0]], tables = lax.optimization_barrier((slices[near[0]], tables))
     place, table, position, factors = tables
-    slices[far] = from_z(own, far)
 
     cap_pieces, img_pieces = [], []
     for group in groups:
@@ -350,7 +334,7 @@
             pltpu.VMEM((depth, full), BF16),
             pltpu.VMEM((depth, full), BF16),
             pltpu.VMEM((padded, 8), F32),
-            pltpu.VMEM((img_rows, c_rows), F32),
+            pltpu.VMEM((i_rows, c_rows), F32),
             pltpu.VMEM((i_rows, c_rows), BF16),
             pltpu.VMEM((img_rows, full), F32),
             pltpu.VMEM((c_rows, full), F32),
@@ -358,7 +342,7 @@
             *(pltpu.VMEM(*kind) for kind in results),
             pltpu.SemaphoreType.DMA((n_copies,)),
         ],
-        compiler_params=params(46),
+        compiler_params=params(48),
         cost_estimate=cost((c_rows + i_rows) * depth * full * 2 + 3 * pair, 20),
         name="pairs",
     )(*operands)

time: 109 us -> 126 us (1.16)
  waiting for transfers between devices: 46 us -> 53.7 us
  starting transfers between devices: 25.7 us -> 32.7 us
  local copies, waits for them, and re-layouts: 3.03 us -> 4.38 us
    ppermute x9 -> x12, starting transfers between devices: 13 us -> 17.5 us  [from_z(): lax.ppermute(value, 'tensor', [((t + k) % slots, t) for t in range(slots)])]
    ppermute x5 -> x6, waiting for transfers between devices: 16.9 us -> 21.3 us  [from_y(): return lax.ppermute(value, 'dp', pairs)]
    ppermute x5 -> x6, starting transfers between devices: 5.64 us -> 8.56 us  [from_y(): return lax.ppermute(value, 'dp', pairs)]
    ppermute x11, waiting for transfers between devices: 2.47 us -> 4.12 us  [from_core(): return lax.ppermute(value, 'dp', [(s, s ^ 1) for s in range(n_dp)])]
    unnamed x23, local copies, waits for them, and re-layouts: 0.97 us -> 2.3 us
    ppermute x9 -> x12, waiting for transfers between devices: 18.4 us -> 19.3 us  [from_z(): lax.ppermute(value, 'tensor', [((t + k) % slots, t) for t in range(slots)])]
    dot_general x3 -> x4, matrix products: 6.4 us -> 7.19 us  [contract_last(): lax.dot_general(a, b, (((1,), (1,)), ((), ())), preferred_element_type=F32)]
  transfers between devices with their start and end apart: 29 -> 33, of which waited for: 18 -> 17; matrix products, arithmetic and copies ran while one was open for 8% -> 8% of each run, Pallas kernels for 0% -> 0%
where the time goes in v3:
time: 126 us
  waiting for transfers between devices  53.7 us (43%)
  starting transfers between devices  32.7 us (26%)
  Pallas kernels  21 us (17%)
  matrix products  7.19 us (6%)
  other arithmetic  4.53 us (4%)
  local copies, waits for them, and re-layouts  4.38 us (3%)
  between operations  2.38 us (2%)
    ppermute x6, waiting for transfers between devices, from_y(): return lax.ppermute(value, 'dp', pairs)  21.3 us
    pallas_call x1, Pallas kernels, whole(): pl.pallas_call(functools.partial(pair_kernel, lay), out_shape=tuple((of(*...  21 us
    ppermute x12, waiting for transfers between devices, from_z(): lax.ppermute(value, 'tensor', [((t + k) % slots, t) for t in range(slots)])  19.3 us
    ppermute x12, starting transfers between devices, from_z(): lax.ppermute(value, 'tensor', [((t + k) % slots, t) for t in range(slots)])  17.5 us
    ppermute x4, waiting for transfers between devices, from_x(): return lax.ppermute(value, 'dp', pairs)  9.03 us
    ppermute x6, starting transfers between devices, from_y(): return lax.ppermute(value, 'dp', pairs)  8.56 us
    dot_general x4, matrix products, contract_last(): lax.dot_general(a, b, (((1,), (1,)), ((), ())), preferred_element_type=F32)  7.19 us
    ppermute x4, starting transfers between devices, from_x(): return lax.ppermute(value, 'dp', pairs)  5.36 us
  transfers between devices with their start and end apart: 33, of which 17 were waited for; matrix products, arithmetic and copies ran while one was open for 8% of the time, Pallas kernels for 0%

profile of v3, /device:TPU:0, one launch (start us, length us, event | category | flops | bytes accessed | tf_op | source)
XLA Modules:
  0.0 125.9 jit_solution(11492905254893748926)
XLA Ops:
  1.7 5.1 %collective-permute-start = (bf16[512,256]{1,0:T(8,128)(2,1)S(1)}, bf16[512,256]{1,0:T(8,128)(2,1)S(1)}, u32[]{:S(2)}, u32[]{:S(2)}) collective-permute-start(bf16[512,256]{1,0:T(8,128)(2,1)S(1)} %pad_maximum_fusion), channel_id=1, source_target_pairs={{1,0},{2,1},{3,2},{0,3},{5,4},{6,5},{7,6},{4,7},{9,8},{10,9},{11,1... | collective-permute-start | bytes 786440 | tf_op jit(solution)/shard_map/ppermute | solution.py:230
  14.2 6.0 %collective-permute-done.5 = bf16[512,256]{1,0:T(8,128)(2,1)S(1)} collective-permute-done((bf16[512,256]{1,0:T(8,128)(2,1)S(1)}, bf16[512,256]{1,0:T(8,128)(2,1)S(1)}, u32[]{:S(2)}, u32[]{:S(2)}) %collective-permute-start.5) | collective-permute-done | bytes 262176 | tf_op jit(solution)/shard_map/ppermute | solution.py:230
  20.2 1.6 %collective-permute-start.13 = (bf16[512,256]{1,0:T(8,128)(2,1)S(1)}, bf16[512,256]{1,0:T(8,128)(2,1)S(1)}, u32[]{:S(2)}, u32[]{:S(2)}) collective-permute-start(bf16[512,256]{1,0:T(8,128)(2,1)S(1)} %pad_maximum_fusion.2.refs_17_), channel_id=1, source_target_pairs={{16,0},{20,4},{24,8},{28,12},{0,16},{4,20},{8,24},{12,28},{17,1},{... | collective-permute-start | bytes 786440 | tf_op jit(solution)/shard_map/ppermute | solution.py:215
  21.8 7.4 %collective-permute-done.9 = bf16[512,256]{1,0:T(8,128)(2,1)S(1)} collective-permute-done((bf16[512,256]{1,0:T(8,128)(2,1)S(1)}, bf16[512,256]{1,0:T(8,128)(2,1)S(1)}, u32[]{:S(2)}, u32[]{:S(2)}) %collective-permute-start.9) | collective-permute-done | bytes 262176 | tf_op jit(solution)/shard_map/ppermute | solution.py:230
  29.2 1.6 %collective-permute-start.10 = (bf16[256,256]{1,0:T(8,128)(2,1)S(1)}, bf16[256,256]{1,0:T(8,128)(2,1)S(1)}, u32[]{:S(2)}, u32[]{:S(2)}) collective-permute-start(bf16[256,256]{1,0:T(8,128)(2,1)S(1)} %get-tuple-element.46.refs_12_), channel_id=1, source_target_pairs={{8,0},{12,4},{0,8},{4,12},{24,16},{28,20},{16,24},{20,28},{9,1},{1... | collective-permute-start | bytes 393224 | tf_op jit(solution)/shard_map/ppermute | solution.py:224
  30.7 1.5 %collective-permute-start.16 = (bf16[256,256]{1,0:T(8,128)(2,1)S(1)}, bf16[256,256]{1,0:T(8,128)(2,1)S(1)}, u32[]{:S(2)}, u32[]{:S(2)}) collective-permute-start(bf16[256,256]{1,0:T(8,128)(2,1)S(1)} %get-tuple-element.45.refs_21_), channel_id=1, source_target_pairs={{16,0},{20,4},{24,8},{28,12},{0,16},{4,20},{8,24},{12,28},{17,1},{... | collective-permute-start | bytes 393224 | tf_op jit(solution)/shard_map/ppermute | solution.py:215
  32.9 2.2 %collective-permute-done.10.refs_13_ = bf16[256,256]{1,0:T(8,128)(2,1)S(1)} collective-permute-done((bf16[256,256]{1,0:T(8,128)(2,1)S(1)}, bf16[256,256]{1,0:T(8,128)(2,1)S(1)}, u32[]{:S(2)}, u32[]{:S(2)}) %collective-permute-start.10) | collective-permute-done | bytes 131104 | tf_op jit(solution)/shard_map/ppermute | solution.py:224
  37.1 1.6 %collective-permute-start.4 = (bf16[352,1024]{1,0:T(8,128)(2,1)}, bf16[352,1024]{1,0:T(8,128)(2,1)S(1)}, u32[]{:S(2)}, u32[]{:S(2)}) collective-permute-start(bf16[352,1024]{1,0:T(8,128)(2,1)} %refs_6_.1), channel_id=1, source_target_pairs={{16,0},{20,4},{24,8},{28,12},{0,16},{4,20},{8,24},{12,28},{17,1},{... | collective-permute-start | bytes 2162696 | tf_op jit(solution)/shard_map/ppermute | solution.py:215
  39.8 1.6 %collective-permute-done.14.refs_19_ = bf16[512,256]{1,0:T(8,128)(2,1)S(1)} collective-permute-done((bf16[512,256]{1,0:T(8,128)(2,1)S(1)}, bf16[512,256]{1,0:T(8,128)(2,1)S(1)}, u32[]{:S(2)}, u32[]{:S(2)}) %collective-permute-start.14) | collective-permute-done | bytes 262176 | tf_op jit(solution)/shard_map/ppermute | solution.py:227
  43.3 12.2 %collective-permute-done.4.refs_5_ = bf16[352,1024]{1,0:T(8,128)(2,1)S(1)} collective-permute-done((bf16[352,1024]{1,0:T(8,128)(2,1)}, bf16[352,1024]{1,0:T(8,128)(2,1)S(1)}, u32[]{:S(2)}, u32[]{:S(2)}) %collective-permute-start.4) | collective-permute-done | bytes 720928 | tf_op jit(solution)/shard_map/ppermute | solution.py:215
  57.2 21.0 %pairs.1 = (bf16[128,1024]{1,0:T(8,128)(2,1)S(1)}, bf16[112,1024]{1,0:T(8,128)(2,1)S(1)}, bf16[112,1024]{1,0:T(8,128)(2,1)S(1)}, f32[128,1024]{1,0:T(8,128)S(1)}...) custom-call(s32[30]{0:T(128)S(1)} %concatenate.45.refs_0_, ...), custom_call_target="tpu_custom_call" | custom-call | flops 10519314432 | bytes 20971520 | tf_op jit(solution)/shard_map/pairs/pallas_call | solution.py:320
  78.3 1.8 %collective-permute-start.23 = (bf16[112,1024]{1,0:T(8,128)(2,1)S(1)}, bf16[112,1024]{1,0:T(8,128)(2,1)S(1)}, u32[]{:S(2)}, u32[]{:S(2)}) collective-permute-start(bf16[112,1024]{1,0:T(8,128)(2,1)S(1)} %get-tuple-element.27), channel_id=1, source_target_pairs={{16,0},{20,4},{24,8},{28,12},{0,16},{4,20},{8,24},{12,28},{17,1},{... | collective-permute-start | bytes 688136 | tf_op jit(solution)/shard_map/ppermute | solution.py:215
  80.3 1.7 %collective-permute-start.27 = (bf16[112,1024]{1,0:T(8,128)(2,1)S(1)}, bf16[112,1024]{1,0:T(8,128)(2,1)S(1)}, u32[]{:S(2)}, u32[]{:S(2)}) collective-permute-start(bf16[112,1024]{1,0:T(8,128)(2,1)S(1)} %get-tuple-element.29), channel_id=1, source_target_pairs={{16,0},{20,4},{24,8},{28,12},{0,16},{4,20},{8,24},{12,28},{17,1},{... | collective-permute-start | bytes 688136 | tf_op jit(solution)/shard_map/ppermute | solution.py:215
  82.1 4.7 %collective-permute-done.23 = bf16[112,1024]{1,0:T(8,128)(2,1)S(1)} collective-permute-done((bf16[112,1024]{1,0:T(8,128)(2,1)S(1)}, bf16[112,1024]{1,0:T(8,128)(2,1)S(1)}, u32[]{:S(2)}, u32[]{:S(2)}) %collective-permute-start.23) | collective-permute-done | bytes 229408 | tf_op jit(solution)/shard_map/ppermute | solution.py:215
  86.8 2.6 %fusion.2 = f32[112,1024]{1,0:T(8,128)S(1)} fusion(bf16[1024,1024]{1,0:T(8,128)(2,1)} %get-tuple-element.25, f32[112,1024]{1,0:T(8,128)S(1)} %get-tuple-element.26, bf16[112,1024]{1,0:T(8,128)(2,1)S(1)} %collective-permute-done.23), kind=kOutput, calls=%fused_computation.11 | convolution fusion | flops 235225088 | bytes 3244032 | tf_op jit(solution)/shard_map/dot_general | solution.py:22
  89.4 2.7 %collective-permute-start.24 = (bf16[112,256]{1,0:T(8,128)(2,1)S(1)}, bf16[112,256]{1,0:T(8,128)(2,1)S(1)}, u32[]{:S(2)}, u32[]{:S(2)}) collective-permute-start(bf16[112,256]{1,0:T(8,128)(2,1)S(1)} %get-tuple-element.39), channel_id=1, source_target_pairs={{1,0},{2,1},{3,2},{0,3},{5,4},{6,5},{7,6},{4,7},{9,8},{10,9},{11,1... | collective-permute-start | bytes 172040 | tf_op jit(solution)/shard_map/ppermute | solution.py:230
  92.1 3.7 %collective-permute-done.27 = bf16[112,1024]{1,0:T(8,128)(2,1)S(1)} collective-permute-done((bf16[112,1024]{1,0:T(8,128)(2,1)S(1)}, bf16[112,1024]{1,0:T(8,128)(2,1)S(1)}, u32[]{:S(2)}, u32[]{:S(2)}) %collective-permute-start.27) | collective-permute-done | bytes 229408 | tf_op jit(solution)/shard_map/ppermute | solution.py:215
  96.7 3.9 %collective-permute-start.28 = (bf16[112,256]{1,0:T(8,128)(2,1)S(1)}, bf16[112,256]{1,0:T(8,128)(2,1)S(1)}, u32[]{:S(2)}, u32[]{:S(2)}) collective-permute-start(bf16[112,256]{1,0:T(8,128)(2,1)S(1)} %get-tuple-element.42), channel_id=1, source_target_pairs={{1,0},{2,1},{3,2},{0,3},{5,4},{6,5},{7,6},{4,7},{9,8},{10,9},{11,1... | collective-permute-start | bytes 172040 | tf_op jit(solution)/shard_map/ppermute | solution.py:230
  104.6 2.8 %collective-permute-start.20 = (bf16[128,256]{1,0:T(8,128)(2,1)S(1)}, bf16[128,256]{1,0:T(8,128)(2,1)S(1)}, u32[]{:S(2)}, u32[]{:S(2)}) collective-permute-start(bf16[128,256]{1,0:T(8,128)(2,1)S(1)} %get-tuple-element.36), channel_id=1, source_target_pairs={{1,0},{2,1},{3,2},{0,3},{5,4},{6,5},{7,6},{4,7},{9,8},{10,9},{11,1... | collective-permute-start | bytes 196616 | tf_op jit(solution)/shard_map/ppermute | solution.py:230
  107.4 1.7 %collective-permute-start.32 = (bf16[352,1024]{1,0:T(8,128)(2,1)S(1)}, bf16[352,1024]{1,0:T(8,128)(2,1)S(1)}, u32[]{:S(2)}, u32[]{:S(2)}) collective-permute-start(bf16[352,1024]{1,0:T(8,128)(2,1)S(1)} %add_convert_fusion.1), channel_id=1, source_target_pairs={{8,0},{12,4},{0,8},{4,12},{24,16},{28,20},{16,24},{20,28},{9,1},{1... | collective-permute-start | bytes 2162696 | tf_op jit(solution)/shard_map/ppermute | solution.py:224
  110.1 4.3 %collective-permute-done.21 = bf16[128,256]{1,0:T(8,128)(2,1)S(1)} collective-permute-done((bf16[128,256]{1,0:T(8,128)(2,1)S(1)}, bf16[128,256]{1,0:T(8,128)(2,1)S(1)}, u32[]{:S(2)}, u32[]{:S(2)}) %collective-permute-start.21) | collective-permute-done | bytes 65568 | tf_op jit(solution)/shard_map/ppermute | solution.py:230
  114.4 1.6 %collective-permute-done.22 = bf16[128,256]{1,0:T(8,128)(2,1)S(1)} collective-permute-done((bf16[128,256]{1,0:T(8,128)(2,1)S(1)}, bf16[128,256]{1,0:T(8,128)(2,1)S(1)}, u32[]{:S(2)}, u32[]{:S(2)}) %collective-permute-start.22) | collective-permute-done | bytes 65568 | tf_op jit(solution)/shard_map/ppermute | solution.py:230
  116.7 6.2 %collective-permute-done.32 = bf16[352,1024]{1,0:T(8,128)(2,1)S(1)} collective-permute-done((bf16[352,1024]{1,0:T(8,128)(2,1)S(1)}, bf16[352,1024]{1,0:T(8,128)(2,1)S(1)}, u32[]{:S(2)}, u32[]{:S(2)}) %collective-permute-start.32) | collective-permute-done | bytes 720928 | tf_op jit(solution)/shard_map/ppermute | solution.py:224
  122.9 3.0 %convolution_convert_fusion = bf16[352,1024]{1,0:T(8,128)(2,1)} fusion(bf16[1024,1024]{1,0:T(8,128)(2,1)S(1)} %copy-done.8, bf16[352,1024]{1,0:T(8,128)(2,1)S(1)} %collective-permute-done.32, f32[352,1024]{1,0:T(8,128)S(1)} %copy-done.9, bf16[704,1024]{1,0:T(8,128)(2,1)} %collective-permute-done.31), kind=kOutput, calls=%fused_computation.2 | convolution fusion | flops 740360192 | bytes 5701632 | tf_op jit(solution)/shard_map/dot_general | solution.py:22
  (116 shorter events, 21.0 us)
Async XLA Ops:
  1.7 12.4 %collective-permute-start = (bf16[512,256]{1,0:T(8,128)(2,1)S(1)}, bf16[512,256]{1,0:T(8,128)(2,1)S(1)}, u32[]{:S(2)}, u32[]{:S(2)}) collective-permute-start(bf16[512,256]{1,0:T(8,128)(2,1)S(1)} %pad_maximum_fusion), channel_id=1, source_target_pairs={{1,0},{2,1},{3,2},{0,3},{5,4},{6,5},{7,6},{4,7},{9,8},{10,9},{11,1... | collective-permute-start | bytes 786440 | tf_op jit(solution)/shard_map/ppermute | solution.py:230
  6.9 13.3 %collective-permute-start.5 = (bf16[512,256]{1,0:T(8,128)(2,1)S(1)}, bf16[512,256]{1,0:T(8,128)(2,1)S(1)}, u32[]{:S(2)}, u32[]{:S(2)}) collective-permute-start(bf16[512,256]{1,0:T(8,128)(2,1)S(1)} %pad_maximum_fusion), channel_id=1, source_target_pairs={{3,0},{0,1},{1,2},{2,3},{7,4},{4,5},{5,6},{6,7},{11,8},{8,9},{9,10... | collective-permute-start | bytes 786440 | tf_op jit(solution)/shard_map/ppermute | solution.py:230
  6.9 22.3 %collective-permute-start.9 = (bf16[512,256]{1,0:T(8,128)(2,1)S(1)}, bf16[512,256]{1,0:T(8,128)(2,1)S(1)}, u32[]{:S(2)}, u32[]{:S(2)}) collective-permute-start(bf16[512,256]{1,0:T(8,128)(2,1)S(1)} %pad_maximum_fusion), channel_id=1, source_target_pairs={{2,0},{3,1},{0,2},{1,3},{6,4},{7,5},{4,6},{5,7},{10,8},{11,9},{8,1... | collective-permute-start | bytes 786440 | tf_op jit(solution)/shard_map/ppermute | solution.py:230
  7.9 30.8 %collective-permute-start.1 = (bf16[352,1024]{1,0:T(8,128)(2,1)}, bf16[352,1024]{1,0:T(8,128)(2,1)}, u32[]{:S(2)}, u32[]{:S(2)}) collective-permute-start(bf16[352,1024]{1,0:T(8,128)(2,1)} %refs_4_.1), channel_id=1, source_target_pairs={{8,0},{12,4},{0,8},{4,12},{24,16},{28,20},{16,24},{20,28},{9,1},{1... | collective-permute-start | bytes 2162696 | tf_op jit(solution)/shard_map/ppermute | solution.py:224
  20.2 18.5 %collective-permute-start.13 = (bf16[512,256]{1,0:T(8,128)(2,1)S(1)}, bf16[512,256]{1,0:T(8,128)(2,1)S(1)}, u32[]{:S(2)}, u32[]{:S(2)}) collective-permute-start(bf16[512,256]{1,0:T(8,128)(2,1)S(1)} %pad_maximum_fusion.2.refs_17_), channel_id=1, source_target_pairs={{16,0},{20,4},{24,8},{28,12},{0,16},{4,20},{8,24},{12,28},{17,1},{... | collective-permute-start | bytes 786440 | tf_op jit(solution)/shard_map/ppermute | solution.py:215
  29.2 5.9 %collective-permute-start.10 = (bf16[256,256]{1,0:T(8,128)(2,1)S(1)}, bf16[256,256]{1,0:T(8,128)(2,1)S(1)}, u32[]{:S(2)}, u32[]{:S(2)}) collective-permute-start(bf16[256,256]{1,0:T(8,128)(2,1)S(1)} %get-tuple-element.46.refs_12_), channel_id=1, source_target_pairs={{8,0},{12,4},{0,8},{4,12},{24,16},{28,20},{16,24},{20,28},{9,1},{1... | collective-permute-start | bytes 393224 | tf_op jit(solution)/shard_map/ppermute | solution.py:224
  32.3 7.6 %collective-permute-start.6 = (bf16[512,256]{1,0:T(8,128)(2,1)S(1)}, bf16[512,256]{1,0:T(8,128)(2,1)S(1)}, u32[]{:S(2)}, u32[]{:S(2)}) collective-permute-start(bf16[512,256]{1,0:T(8,128)(2,1)S(1)} %pad_maximum_fusion.1.refs_8_), channel_id=1, source_target_pairs={{8,0},{12,4},{0,8},{4,12},{24,16},{28,20},{16,24},{20,28},{9,1},{1... | collective-permute-start | bytes 786440 | tf_op jit(solution)/shard_map/ppermute | solution.py:224
  36.4 6.9 %collective-permute-start.3 = (bf16[352,1024]{1,0:T(8,128)(2,1)S(1)}, bf16[352,1024]{1,0:T(8,128)(2,1)S(1)}, u32[]{:S(2)}, u32[]{:S(2)}) collective-permute-start(bf16[352,1024]{1,0:T(8,128)(2,1)S(1)} %copy-done.4), channel_id=1, source_target_pairs={{0,4},{4,0},{8,12},{12,8},{16,20},{20,16},{24,28},{28,24},{1,5},{5... | collective-permute-start | bytes 2162696 | tf_op jit(solution)/shard_map/ppermute | solution.py:227
  37.1 18.5 %collective-permute-start.4 = (bf16[352,1024]{1,0:T(8,128)(2,1)}, bf16[352,1024]{1,0:T(8,128)(2,1)S(1)}, u32[]{:S(2)}, u32[]{:S(2)}) collective-permute-start(bf16[352,1024]{1,0:T(8,128)(2,1)} %refs_6_.1), channel_id=1, source_target_pairs={{16,0},{20,4},{24,8},{28,12},{0,16},{4,20},{8,24},{12,28},{17,1},{... | collective-permute-start | bytes 2162696 | tf_op jit(solution)/shard_map/ppermute | solution.py:215
  38.7 16.9 %collective-permute-start.2 = (bf16[352,1024]{1,0:T(8,128)(2,1)}, bf16[352,1024]{1,0:T(8,128)(2,1)S(1)}, u32[]{:S(2)}, u32[]{:S(2)}) collective-permute-start(bf16[352,1024]{1,0:T(8,128)(2,1)} %collective-permute-done.1.refs_2_), channel_id=1, source_target_pairs={{0,4},{4,0},{8,12},{12,8},{16,20},{20,16},{24,28},{28,24},{1,5},{5... | collective-permute-start | bytes 2162696 | tf_op jit(solution)/shard_map/ppermute | solution.py:227
  42.8 12.7 %collective-permute-start.15 = (bf16[512,256]{1,0:T(8,128)(2,1)S(1)}, bf16[512,256]{1,0:T(8,128)(2,1)S(1)}, u32[]{:S(2)}, u32[]{:S(2)}) collective-permute-start(bf16[512,256]{1,0:T(8,128)(2,1)S(1)} %collective-permute-done.13.refs_18_), channel_id=1, source_target_pairs={{0,4},{4,0},{8,12},{12,8},{16,20},{20,16},{24,28},{28,24},{1,5},{5... | collective-permute-start | bytes 786440 | tf_op jit(solution)/shard_map/ppermute | solution.py:227
  43.2 12.3 %collective-permute-start.8 = (bf16[512,256]{1,0:T(8,128)(2,1)S(1)}, bf16[512,256]{1,0:T(8,128)(2,1)S(1)}, u32[]{:S(2)}, u32[]{:S(2)}) collective-permute-start(bf16[512,256]{1,0:T(8,128)(2,1)S(1)} %collective-permute-done.6.refs_9_), channel_id=1, source_target_pairs={{0,4},{4,0},{8,12},{12,8},{16,20},{20,16},{24,28},{28,24},{1,5},{5... | collective-permute-start | bytes 786440 | tf_op jit(solution)/shard_map/ppermute | solution.py:227
  78.3 8.5 %collective-permute-start.23 = (bf16[112,1024]{1,0:T(8,128)(2,1)S(1)}, bf16[112,1024]{1,0:T(8,128)(2,1)S(1)}, u32[]{:S(2)}, u32[]{:S(2)}) collective-permute-start(bf16[112,1024]{1,0:T(8,128)(2,1)S(1)} %get-tuple-element.27), channel_id=1, source_target_pairs={{16,0},{20,4},{24,8},{28,12},{0,16},{4,20},{8,24},{12,28},{17,1},{... | collective-permute-start | bytes 688136 | tf_op jit(solution)/shard_map/ppermute | solution.py:215
  80.1 21.4 %collective-permute-start.31 = (bf16[704,1024]{1,0:T(8,128)(2,1)}, bf16[704,1024]{1,0:T(8,128)(2,1)}, u32[]{:S(2)}, u32[]{:S(2)}) collective-permute-start(bf16[704,1024]{1,0:T(8,128)(2,1)} %get-tuple-element.31), channel_id=1, source_target_pairs={{0,4},{4,0},{8,12},{12,8},{16,20},{20,16},{24,28},{28,24},{1,5},{5... | collective-permute-start | bytes 4325384 | tf_op jit(solution)/shard_map/ppermute | solution.py:227
  80.1 16.6 %collective-permute-start.19 = (bf16[128,1024]{1,0:T(8,128)(2,1)S(1)}, bf16[128,1024]{1,0:T(8,128)(2,1)S(1)}, u32[]{:S(2)}, u32[]{:S(2)}) collective-permute-start(bf16[128,1024]{1,0:T(8,128)(2,1)S(1)} %get-tuple-element.24), channel_id=1, source_target_pairs={{16,0},{20,4},{24,8},{28,12},{0,16},{4,20},{8,24},{12,28},{17,1},{... | collective-permute-start | bytes 786440 | tf_op jit(solution)/shard_map/ppermute | solution.py:215
  80.3 15.5 %collective-permute-start.27 = (bf16[112,1024]{1,0:T(8,128)(2,1)S(1)}, bf16[112,1024]{1,0:T(8,128)(2,1)S(1)}, u32[]{:S(2)}, u32[]{:S(2)}) collective-permute-start(bf16[112,1024]{1,0:T(8,128)(2,1)S(1)} %get-tuple-element.29), channel_id=1, source_target_pairs={{16,0},{20,4},{24,8},{28,12},{0,16},{4,20},{8,24},{12,28},{17,1},{... | collective-permute-start | bytes 688136 | tf_op jit(solution)/shard_map/ppermute | solution.py:215
  89.4 14.1 %collective-permute-start.24 = (bf16[112,256]{1,0:T(8,128)(2,1)S(1)}, bf16[112,256]{1,0:T(8,128)(2,1)S(1)}, u32[]{:S(2)}, u32[]{:S(2)}) collective-permute-start(bf16[112,256]{1,0:T(8,128)(2,1)S(1)} %get-tuple-element.39), channel_id=1, source_target_pairs={{1,0},{2,1},{3,2},{0,3},{5,4},{6,5},{7,6},{4,7},{9,8},{10,9},{11,1... | collective-permute-start | bytes 172040 | tf_op jit(solution)/shard_map/ppermute | solution.py:230
  92.1 12.5 %collective-permute-start.25 = (bf16[112,256]{1,0:T(8,128)(2,1)S(1)}, bf16[112,256]{1,0:T(8,128)(2,1)S(1)}, u32[]{:S(2)}, u32[]{:S(2)}) collective-permute-start(bf16[112,256]{1,0:T(8,128)(2,1)S(1)} %get-tuple-element.41), channel_id=1, source_target_pairs={{2,0},{3,1},{0,2},{1,3},{6,4},{7,5},{4,6},{5,7},{10,8},{11,9},{8,1... | collective-permute-start | bytes 172040 | tf_op jit(solution)/shard_map/ppermute | solution.py:230
  95.8 11.5 %collective-permute-start.26 = (bf16[112,256]{1,0:T(8,128)(2,1)S(1)}, bf16[112,256]{1,0:T(8,128)(2,1)S(1)}, u32[]{:S(2)}, u32[]{:S(2)}) collective-permute-start(bf16[112,256]{1,0:T(8,128)(2,1)S(1)} %get-tuple-element.40), channel_id=1, source_target_pairs={{3,0},{0,1},{1,2},{2,3},{7,4},{4,5},{5,6},{6,7},{11,8},{8,9},{9,10... | collective-permute-start | bytes 172040 | tf_op jit(solution)/shard_map/ppermute | solution.py:230
  96.7 12.4 %collective-permute-start.28 = (bf16[112,256]{1,0:T(8,128)(2,1)S(1)}, bf16[112,256]{1,0:T(8,128)(2,1)S(1)}, u32[]{:S(2)}, u32[]{:S(2)}) collective-permute-start(bf16[112,256]{1,0:T(8,128)(2,1)S(1)} %get-tuple-element.42), channel_id=1, source_target_pairs={{1,0},{2,1},{3,2},{0,3},{5,4},{6,5},{7,6},{4,7},{9,8},{10,9},{11,1... | collective-permute-start | bytes 172040 | tf_op jit(solution)/shard_map/ppermute | solution.py:230
  101.5 8.4 %collective-permute-start.29 = (bf16[112,256]{1,0:T(8,128)(2,1)S(1)}, bf16[112,256]{1,0:T(8,128)(2,1)S(1)}, u32[]{:S(2)}, u32[]{:S(2)}) collective-permute-start(bf16[112,256]{1,0:T(8,128)(2,1)S(1)} %get-tuple-element.44), channel_id=1, source_target_pairs={{2,0},{3,1},{0,2},{1,3},{6,4},{7,5},{4,6},{5,7},{10,8},{11,9},{8,1... | collective-permute-start | bytes 172040 | tf_op jit(solution)/shard_map/ppermute | solution.py:230
  103.5 6.5 %collective-permute-start.30 = (bf16[112,256]{1,0:T(8,128)(2,1)S(1)}, bf16[112,256]{1,0:T(8,128)(2,1)S(1)}, u32[]{:S(2)}, u32[]{:S(2)}) collective-permute-start(bf16[112,256]{1,0:T(8,128)(2,1)S(1)} %get-tuple-element.43), channel_id=1, source_target_pairs={{3,0},{0,1},{1,2},{2,3},{7,4},{4,5},{5,6},{6,7},{11,8},{8,9},{9,10... | collective-permute-start | bytes 172040 | tf_op jit(solution)/shard_map/ppermute | solution.py:230
  107.4 15.5 %collective-permute-start.32 = (bf16[352,1024]{1,0:T(8,128)(2,1)S(1)}, bf16[352,1024]{1,0:T(8,128)(2,1)S(1)}, u32[]{:S(2)}, u32[]{:S(2)}) collective-permute-start(bf16[352,1024]{1,0:T(8,128)(2,1)S(1)} %add_convert_fusion.1), channel_id=1, source_target_pairs={{8,0},{12,4},{0,8},{4,12},{24,16},{28,20},{16,24},{20,28},{9,1},{1... | collective-permute-start | bytes 2162696 | tf_op jit(solution)/shard_map/ppermute | solution.py:224
  109.9 6.1 %collective-permute-start.22 = (bf16[128,256]{1,0:T(8,128)(2,1)S(1)}, bf16[128,256]{1,0:T(8,128)(2,1)S(1)}, u32[]{:S(2)}, u32[]{:S(2)}) collective-permute-start(bf16[128,256]{1,0:T(8,128)(2,1)S(1)} %get-tuple-element.37), channel_id=1, source_target_pairs={{3,0},{0,1},{1,2},{2,3},{7,4},{4,5},{5,6},{6,7},{11,8},{8,9},{9,10... | collective-permute-start | bytes 196616 | tf_op jit(solution)/shard_map/ppermute | solution.py:230
  (19 other events, 170.5 us)

commit v4 on v3

--- a/solution.py
+++ b/solution.py
@@ -11,7 +11,6 @@
 epsilon = 1e-06
 CORES = 2
 ROWS_Y = 2
-CHUNK = 32
 PARTS = 3
 LOG2E = 1.4426950408889634
 F32 = jnp.float32
@@ -258,10 +257,6 @@
     order = [(k, c) for c in (1 - core, core) for k in range(1, n_x)] + [(0, 1 - core), (0, core)]
     heads = [(number(pos_y, (pos_x + k) % n_x, c) * slots + mine) * rows for k, c in order]
     position = jnp.concatenate([head + jnp.arange(rows, dtype=jnp.int32) for head in heads]).astype(F32)[None, :]
-    low = table[0, :n_rows].reshape(-1, CHUNK)[:, 0]
-    high = table[1, :n_rows].reshape(-1, CHUNK)[:, -1]
-    touched = functools.reduce(jnp.logical_or, [(low < head + rows) & (high > head) for head in heads])
-    place = jnp.concatenate([place, touched.astype(jnp.int32)])
     factors = jnp.concatenate([sharp, shift])
 
     far = slots // 2
@@ -342,7 +337,7 @@
             *(pltpu.VMEM(*kind) for kind in results),
             pltpu.SemaphoreType.DMA((n_copies,)),
         ],
-        compiler_params=params(48),
+        compiler_params=params(47),
         cost_estimate=cost((c_rows + i_rows) * depth * full * 2 + 3 * pair, 20),
         name="pairs",
     )(*operands)

time: 126 us -> 125 us (level)
  local copies, waits for them, and re-layouts: 4.38 us -> 3.11 us
where the time goes in v4:
time: 125 us; the launch traced here: 124 us
  waiting for transfers between devices  54.1 us (43%)
  starting transfers between devices  32.7 us (26%)
  Pallas kernels  20.5 us (16%)
  matrix products  7.12 us (6%)
  other arithmetic  4.43 us (4%)
  local copies, waits for them, and re-layouts  3.11 us (2%)
  between operations  2.46 us (2%)
    ppermute x6, waiting for transfers between devices, from_y(): return lax.ppermute(value, 'dp', pairs)  21.3 us
    pallas_call x1, Pallas kernels, whole(): pl.pallas_call(functools.partial(pair_kernel, lay), out_shape=tuple((of(*...  20.5 us
    ppermute x12, waiting for transfers between devices, from_z(): lax.ppermute(value, 'tensor', [((t + k) % slots, t) for t in range(slots)])  19.7 us
    ppermute x12, starting transfers between devices, from_z(): lax.ppermute(value, 'tensor', [((t + k) % slots, t) for t in range(slots)])  17.5 us
    ppermute x4, waiting for transfers between devices, from_x(): return lax.ppermute(value, 'dp', pairs)  9.01 us
    ppermute x6, starting transfers between devices, from_y(): return lax.ppermute(value, 'dp', pairs)  8.55 us
    dot_general x4, matrix products, contract_last(): lax.dot_general(a, b, (((1,), (1,)), ((), ())), preferred_element_type=F32)  7.12 us
    ppermute x4, starting transfers between devices, from_x(): return lax.ppermute(value, 'dp', pairs)  5.36 us
  transfers between devices with their start and end apart: 33, of which 17 were waited for; matrix products, arithmetic and copies ran while one was open for 8% of the time, Pallas kernels for 0%

profile of v4, /device:TPU:0, one launch (start us, length us, event | category | flops | bytes accessed | tf_op | source)
XLA Modules:
  0.0 124.5 jit_solution(10161822727112870622)
XLA Ops:
  1.7 5.1 %collective-permute-start = (bf16[512,256]{1,0:T(8,128)(2,1)S(1)}, bf16[512,256]{1,0:T(8,128)(2,1)S(1)}, u32[]{:S(2)}, u32[]{:S(2)}) collective-permute-start(bf16[512,256]{1,0:T(8,128)(2,1)S(1)} %pad_maximum_fusion), channel_id=1, source_target_pairs={{1,0},{2,1},{3,2},{0,3},{5,4},{6,5},{7,6},{4,7},{9,8},{10,9},{11,1... | collective-permute-start | bytes 786440 | tf_op jit(solution)/shard_map/ppermute | solution.py:229
  13.7 6.4 %collective-permute-done.5 = bf16[512,256]{1,0:T(8,128)(2,1)S(1)} collective-permute-done((bf16[512,256]{1,0:T(8,128)(2,1)S(1)}, bf16[512,256]{1,0:T(8,128)(2,1)S(1)}, u32[]{:S(2)}, u32[]{:S(2)}) %collective-permute-start.5) | collective-permute-done | bytes 262176 | tf_op jit(solution)/shard_map/ppermute | solution.py:229
  20.2 1.6 %collective-permute-start.13 = (bf16[512,256]{1,0:T(8,128)(2,1)S(1)}, bf16[512,256]{1,0:T(8,128)(2,1)S(1)}, u32[]{:S(2)}, u32[]{:S(2)}) collective-permute-start(bf16[512,256]{1,0:T(8,128)(2,1)S(1)} %pad_maximum_fusion.2.refs_17_), channel_id=1, source_target_pairs={{16,0},{20,4},{24,8},{28,12},{0,16},{4,20},{8,24},{12,28},{17,1},{... | collective-permute-start | bytes 786440 | tf_op jit(solution)/shard_map/ppermute | solution.py:214
  21.8 7.4 %collective-permute-done.9 = bf16[512,256]{1,0:T(8,128)(2,1)S(1)} collective-permute-done((bf16[512,256]{1,0:T(8,128)(2,1)S(1)}, bf16[512,256]{1,0:T(8,128)(2,1)S(1)}, u32[]{:S(2)}, u32[]{:S(2)}) %collective-permute-start.9) | collective-permute-done | bytes 262176 | tf_op jit(solution)/shard_map/ppermute | solution.py:229
  29.2 1.6 %collective-permute-start.10 = (bf16[256,256]{1,0:T(8,128)(2,1)S(1)}, bf16[256,256]{1,0:T(8,128)(2,1)S(1)}, u32[]{:S(2)}, u32[]{:S(2)}) collective-permute-start(bf16[256,256]{1,0:T(8,128)(2,1)S(1)} %get-tuple-element.44.refs_12_), channel_id=1, source_target_pairs={{8,0},{12,4},{0,8},{4,12},{24,16},{28,20},{16,24},{20,28},{9,1},{1... | collective-permute-start | bytes 393224 | tf_op jit(solution)/shard_map/ppermute | solution.py:223
  30.7 1.5 %collective-permute-start.16 = (bf16[256,256]{1,0:T(8,128)(2,1)S(1)}, bf16[256,256]{1,0:T(8,128)(2,1)S(1)}, u32[]{:S(2)}, u32[]{:S(2)}) collective-permute-start(bf16[256,256]{1,0:T(8,128)(2,1)S(1)} %get-tuple-element.43.refs_21_), channel_id=1, source_target_pairs={{16,0},{20,4},{24,8},{28,12},{0,16},{4,20},{8,24},{12,28},{17,1},{... | collective-permute-start | bytes 393224 | tf_op jit(solution)/shard_map/ppermute | solution.py:214
  32.9 2.2 %collective-permute-done.10.refs_13_ = bf16[256,256]{1,0:T(8,128)(2,1)S(1)} collective-permute-done((bf16[256,256]{1,0:T(8,128)(2,1)S(1)}, bf16[256,256]{1,0:T(8,128)(2,1)S(1)}, u32[]{:S(2)}, u32[]{:S(2)}) %collective-permute-start.10) | collective-permute-done | bytes 131104 | tf_op jit(solution)/shard_map/ppermute | solution.py:223
  37.1 1.6 %collective-permute-start.4 = (bf16[352,1024]{1,0:T(8,128)(2,1)}, bf16[352,1024]{1,0:T(8,128)(2,1)S(1)}, u32[]{:S(2)}, u32[]{:S(2)}) collective-permute-start(bf16[352,1024]{1,0:T(8,128)(2,1)} %refs_6_.1), channel_id=1, source_target_pairs={{16,0},{20,4},{24,8},{28,12},{0,16},{4,20},{8,24},{12,28},{17,1},{... | collective-permute-start | bytes 2162696 | tf_op jit(solution)/shard_map/ppermute | solution.py:214
  39.8 1.6 %collective-permute-done.14.refs_19_ = bf16[512,256]{1,0:T(8,128)(2,1)S(1)} collective-permute-done((bf16[512,256]{1,0:T(8,128)(2,1)S(1)}, bf16[512,256]{1,0:T(8,128)(2,1)S(1)}, u32[]{:S(2)}, u32[]{:S(2)}) %collective-permute-start.14) | collective-permute-done | bytes 262176 | tf_op jit(solution)/shard_map/ppermute | solution.py:226
  43.3 12.2 %collective-permute-done.4.refs_5_ = bf16[352,1024]{1,0:T(8,128)(2,1)S(1)} collective-permute-done((bf16[352,1024]{1,0:T(8,128)(2,1)}, bf16[352,1024]{1,0:T(8,128)(2,1)S(1)}, u32[]{:S(2)}, u32[]{:S(2)}) %collective-permute-start.4) | collective-permute-done | bytes 720928 | tf_op jit(solution)/shard_map/ppermute | solution.py:214
  56.4 20.5 %pairs.1 = (bf16[128,1024]{1,0:T(8,128)(2,1)S(1)}, bf16[112,1024]{1,0:T(8,128)(2,1)S(1)}, bf16[112,1024]{1,0:T(8,128)(2,1)S(1)}, f32[128,1024]{1,0:T(8,128)S(1)}...) custom-call(s32[8]{0:T(128)S(1)} %stack.50.refs_0_, ...), custom_call_target="tpu_custom_call" | custom-call | flops 10519314432 | bytes 20971520 | tf_op jit(solution)/shard_map/pairs/pallas_call | solution.py:315
  76.9 1.8 %collective-permute-start.23 = (bf16[112,1024]{1,0:T(8,128)(2,1)S(1)}, bf16[112,1024]{1,0:T(8,128)(2,1)S(1)}, u32[]{:S(2)}, u32[]{:S(2)}) collective-permute-start(bf16[112,1024]{1,0:T(8,128)(2,1)S(1)} %get-tuple-element.27), channel_id=1, source_target_pairs={{16,0},{20,4},{24,8},{28,12},{0,16},{4,20},{8,24},{12,28},{17,1},{... | collective-permute-start | bytes 688136 | tf_op jit(solution)/shard_map/ppermute | solution.py:214
  79.0 1.7 %collective-permute-start.27 = (bf16[112,1024]{1,0:T(8,128)(2,1)S(1)}, bf16[112,1024]{1,0:T(8,128)(2,1)S(1)}, u32[]{:S(2)}, u32[]{:S(2)}) collective-permute-start(bf16[112,1024]{1,0:T(8,128)(2,1)S(1)} %get-tuple-element.29), channel_id=1, source_target_pairs={{16,0},{20,4},{24,8},{28,12},{0,16},{4,20},{8,24},{12,28},{17,1},{... | collective-permute-start | bytes 688136 | tf_op jit(solution)/shard_map/ppermute | solution.py:214
  80.7 4.7 %collective-permute-done.23 = bf16[112,1024]{1,0:T(8,128)(2,1)S(1)} collective-permute-done((bf16[112,1024]{1,0:T(8,128)(2,1)S(1)}, bf16[112,1024]{1,0:T(8,128)(2,1)S(1)}, u32[]{:S(2)}, u32[]{:S(2)}) %collective-permute-start.23) | collective-permute-done | bytes 229408 | tf_op jit(solution)/shard_map/ppermute | solution.py:214
  85.4 2.5 %fusion.2 = f32[112,1024]{1,0:T(8,128)S(1)} fusion(bf16[1024,1024]{1,0:T(8,128)(2,1)} %get-tuple-element.25, f32[112,1024]{1,0:T(8,128)S(1)} %get-tuple-element.26, bf16[112,1024]{1,0:T(8,128)(2,1)S(1)} %collective-permute-done.23), kind=kOutput, calls=%fused_computation.11 | convolution fusion | flops 235225088 | bytes 3244032 | tf_op jit(solution)/shard_map/dot_general | solution.py:21
  88.0 2.7 %collective-permute-start.24 = (bf16[112,256]{1,0:T(8,128)(2,1)S(1)}, bf16[112,256]{1,0:T(8,128)(2,1)S(1)}, u32[]{:S(2)}, u32[]{:S(2)}) collective-permute-start(bf16[112,256]{1,0:T(8,128)(2,1)S(1)} %get-tuple-element.37), channel_id=1, source_target_pairs={{1,0},{2,1},{3,2},{0,3},{5,4},{6,5},{7,6},{4,7},{9,8},{10,9},{11,1... | collective-permute-start | bytes 172040 | tf_op jit(solution)/shard_map/ppermute | solution.py:229
  90.7 3.7 %collective-permute-done.27 = bf16[112,1024]{1,0:T(8,128)(2,1)S(1)} collective-permute-done((bf16[112,1024]{1,0:T(8,128)(2,1)S(1)}, bf16[112,1024]{1,0:T(8,128)(2,1)S(1)}, u32[]{:S(2)}, u32[]{:S(2)}) %collective-permute-start.27) | collective-permute-done | bytes 229408 | tf_op jit(solution)/shard_map/ppermute | solution.py:214
  95.3 3.9 %collective-permute-start.28 = (bf16[112,256]{1,0:T(8,128)(2,1)S(1)}, bf16[112,256]{1,0:T(8,128)(2,1)S(1)}, u32[]{:S(2)}, u32[]{:S(2)}) collective-permute-start(bf16[112,256]{1,0:T(8,128)(2,1)S(1)} %get-tuple-element.40), channel_id=1, source_target_pairs={{1,0},{2,1},{3,2},{0,3},{5,4},{6,5},{7,6},{4,7},{9,8},{10,9},{11,1... | collective-permute-start | bytes 172040 | tf_op jit(solution)/shard_map/ppermute | solution.py:229
  103.2 2.8 %collective-permute-start.20 = (bf16[128,256]{1,0:T(8,128)(2,1)S(1)}, bf16[128,256]{1,0:T(8,128)(2,1)S(1)}, u32[]{:S(2)}, u32[]{:S(2)}) collective-permute-start(bf16[128,256]{1,0:T(8,128)(2,1)S(1)} %get-tuple-element.34), channel_id=1, source_target_pairs={{1,0},{2,1},{3,2},{0,3},{5,4},{6,5},{7,6},{4,7},{9,8},{10,9},{11,1... | collective-permute-start | bytes 196616 | tf_op jit(solution)/shard_map/ppermute | solution.py:229
  106.0 1.7 %collective-permute-start.32 = (bf16[352,1024]{1,0:T(8,128)(2,1)S(1)}, bf16[352,1024]{1,0:T(8,128)(2,1)S(1)}, u32[]{:S(2)}, u32[]{:S(2)}) collective-permute-start(bf16[352,1024]{1,0:T(8,128)(2,1)S(1)} %add_convert_fusion.1), channel_id=1, source_target_pairs={{8,0},{12,4},{0,8},{4,12},{24,16},{28,20},{16,24},{20,28},{9,1},{1... | collective-permute-start | bytes 2162696 | tf_op jit(solution)/shard_map/ppermute | solution.py:223
  108.7 4.3 %collective-permute-done.21 = bf16[128,256]{1,0:T(8,128)(2,1)S(1)} collective-permute-done((bf16[128,256]{1,0:T(8,128)(2,1)S(1)}, bf16[128,256]{1,0:T(8,128)(2,1)S(1)}, u32[]{:S(2)}, u32[]{:S(2)}) %collective-permute-start.21) | collective-permute-done | bytes 65568 | tf_op jit(solution)/shard_map/ppermute | solution.py:229
  113.0 1.6 %collective-permute-done.22 = bf16[128,256]{1,0:T(8,128)(2,1)S(1)} collective-permute-done((bf16[128,256]{1,0:T(8,128)(2,1)S(1)}, bf16[128,256]{1,0:T(8,128)(2,1)S(1)}, u32[]{:S(2)}, u32[]{:S(2)}) %collective-permute-start.22) | collective-permute-done | bytes 65568 | tf_op jit(solution)/shard_map/ppermute | solution.py:229
  115.3 6.2 %collective-permute-done.32 = bf16[352,1024]{1,0:T(8,128)(2,1)S(1)} collective-permute-done((bf16[352,1024]{1,0:T(8,128)(2,1)S(1)}, bf16[352,1024]{1,0:T(8,128)(2,1)S(1)}, u32[]{:S(2)}, u32[]{:S(2)}) %collective-permute-start.32) | collective-permute-done | bytes 720928 | tf_op jit(solution)/shard_map/ppermute | solution.py:223
  121.5 2.9 %convolution_convert_fusion = bf16[352,1024]{1,0:T(8,128)(2,1)} fusion(bf16[1024,1024]{1,0:T(8,128)(2,1)S(1)} %copy-done.7, bf16[352,1024]{1,0:T(8,128)(2,1)S(1)} %collective-permute-done.32, f32[352,1024]{1,0:T(8,128)S(1)} %copy-done.8, bf16[704,1024]{1,0:T(8,128)(2,1)} %collective-permute-done.31), kind=kOutput, calls=%fused_computation.2 | convolution fusion | flops 740360192 | bytes 5701632 | tf_op jit(solution)/shard_map/dot_general | solution.py:21
  (107 shorter events, 19.7 us)
Async XLA Ops:
  1.7 12.0 %collective-permute-start = (bf16[512,256]{1,0:T(8,128)(2,1)S(1)}, bf16[512,256]{1,0:T(8,128)(2,1)S(1)}, u32[]{:S(2)}, u32[]{:S(2)}) collective-permute-start(bf16[512,256]{1,0:T(8,128)(2,1)S(1)} %pad_maximum_fusion), channel_id=1, source_target_pairs={{1,0},{2,1},{3,2},{0,3},{5,4},{6,5},{7,6},{4,7},{9,8},{10,9},{11,1... | collective-permute-start | bytes 786440 | tf_op jit(solution)/shard_map/ppermute | solution.py:229
  6.9 13.3 %collective-permute-start.5 = (bf16[512,256]{1,0:T(8,128)(2,1)S(1)}, bf16[512,256]{1,0:T(8,128)(2,1)S(1)}, u32[]{:S(2)}, u32[]{:S(2)}) collective-permute-start(bf16[512,256]{1,0:T(8,128)(2,1)S(1)} %pad_maximum_fusion), channel_id=1, source_target_pairs={{3,0},{0,1},{1,2},{2,3},{7,4},{4,5},{5,6},{6,7},{11,8},{8,9},{9,10... | collective-permute-start | bytes 786440 | tf_op jit(solution)/shard_map/ppermute | solution.py:229
  6.9 22.3 %collective-permute-start.9 = (bf16[512,256]{1,0:T(8,128)(2,1)S(1)}, bf16[512,256]{1,0:T(8,128)(2,1)S(1)}, u32[]{:S(2)}, u32[]{:S(2)}) collective-permute-start(bf16[512,256]{1,0:T(8,128)(2,1)S(1)} %pad_maximum_fusion), channel_id=1, source_target_pairs={{2,0},{3,1},{0,2},{1,3},{6,4},{7,5},{4,6},{5,7},{10,8},{11,9},{8,1... | collective-permute-start | bytes 786440 | tf_op jit(solution)/shard_map/ppermute | solution.py:229
  7.9 30.8 %collective-permute-start.1 = (bf16[352,1024]{1,0:T(8,128)(2,1)}, bf16[352,1024]{1,0:T(8,128)(2,1)}, u32[]{:S(2)}, u32[]{:S(2)}) collective-permute-start(bf16[352,1024]{1,0:T(8,128)(2,1)} %refs_4_.1), channel_id=1, source_target_pairs={{8,0},{12,4},{0,8},{4,12},{24,16},{28,20},{16,24},{20,28},{9,1},{1... | collective-permute-start | bytes 2162696 | tf_op jit(solution)/shard_map/ppermute | solution.py:223
  20.2 18.5 %collective-permute-start.13 = (bf16[512,256]{1,0:T(8,128)(2,1)S(1)}, bf16[512,256]{1,0:T(8,128)(2,1)S(1)}, u32[]{:S(2)}, u32[]{:S(2)}) collective-permute-start(bf16[512,256]{1,0:T(8,128)(2,1)S(1)} %pad_maximum_fusion.2.refs_17_), channel_id=1, source_target_pairs={{16,0},{20,4},{24,8},{28,12},{0,16},{4,20},{8,24},{12,28},{17,1},{... | collective-permute-start | bytes 786440 | tf_op jit(solution)/shard_map/ppermute | solution.py:214
  29.2 5.9 %collective-permute-start.10 = (bf16[256,256]{1,0:T(8,128)(2,1)S(1)}, bf16[256,256]{1,0:T(8,128)(2,1)S(1)}, u32[]{:S(2)}, u32[]{:S(2)}) collective-permute-start(bf16[256,256]{1,0:T(8,128)(2,1)S(1)} %get-tuple-element.44.refs_12_), channel_id=1, source_target_pairs={{8,0},{12,4},{0,8},{4,12},{24,16},{28,20},{16,24},{20,28},{9,1},{1... | collective-permute-start | bytes 393224 | tf_op jit(solution)/shard_map/ppermute | solution.py:223
  32.3 7.6 %collective-permute-start.6 = (bf16[512,256]{1,0:T(8,128)(2,1)S(1)}, bf16[512,256]{1,0:T(8,128)(2,1)S(1)}, u32[]{:S(2)}, u32[]{:S(2)}) collective-permute-start(bf16[512,256]{1,0:T(8,128)(2,1)S(1)} %pad_maximum_fusion.1.refs_8_), channel_id=1, source_target_pairs={{8,0},{12,4},{0,8},{4,12},{24,16},{28,20},{16,24},{20,28},{9,1},{1... | collective-permute-start | bytes 786440 | tf_op jit(solution)/shard_map/ppermute | solution.py:223
  36.4 6.9 %collective-permute-start.3 = (bf16[352,1024]{1,0:T(8,128)(2,1)}, bf16[352,1024]{1,0:T(8,128)(2,1)S(1)}, u32[]{:S(2)}, u32[]{:S(2)}) collective-permute-start(bf16[352,1024]{1,0:T(8,128)(2,1)} %refs_4_.1), channel_id=1, source_target_pairs={{0,4},{4,0},{8,12},{12,8},{16,20},{20,16},{24,28},{28,24},{1,5},{5... | collective-permute-start | bytes 2162696 | tf_op jit(solution)/shard_map/ppermute | solution.py:226
  37.1 18.5 %collective-permute-start.4 = (bf16[352,1024]{1,0:T(8,128)(2,1)}, bf16[352,1024]{1,0:T(8,128)(2,1)S(1)}, u32[]{:S(2)}, u32[]{:S(2)}) collective-permute-start(bf16[352,1024]{1,0:T(8,128)(2,1)} %refs_6_.1), channel_id=1, source_target_pairs={{16,0},{20,4},{24,8},{28,12},{0,16},{4,20},{8,24},{12,28},{17,1},{... | collective-permute-start | bytes 2162696 | tf_op jit(solution)/shard_map/ppermute | solution.py:214
  38.7 16.8 %collective-permute-start.2 = (bf16[352,1024]{1,0:T(8,128)(2,1)}, bf16[352,1024]{1,0:T(8,128)(2,1)S(1)}, u32[]{:S(2)}, u32[]{:S(2)}) collective-permute-start(bf16[352,1024]{1,0:T(8,128)(2,1)} %collective-permute-done.1.refs_2_), channel_id=1, source_target_pairs={{0,4},{4,0},{8,12},{12,8},{16,20},{20,16},{24,28},{28,24},{1,5},{5... | collective-permute-start | bytes 2162696 | tf_op jit(solution)/shard_map/ppermute | solution.py:226
  42.8 12.7 %collective-permute-start.15 = (bf16[512,256]{1,0:T(8,128)(2,1)S(1)}, bf16[512,256]{1,0:T(8,128)(2,1)S(1)}, u32[]{:S(2)}, u32[]{:S(2)}) collective-permute-start(bf16[512,256]{1,0:T(8,128)(2,1)S(1)} %collective-permute-done.13.refs_18_), channel_id=1, source_target_pairs={{0,4},{4,0},{8,12},{12,8},{16,20},{20,16},{24,28},{28,24},{1,5},{5... | collective-permute-start | bytes 786440 | tf_op jit(solution)/shard_map/ppermute | solution.py:226
  43.2 12.3 %collective-permute-start.8 = (bf16[512,256]{1,0:T(8,128)(2,1)S(1)}, bf16[512,256]{1,0:T(8,128)(2,1)S(1)}, u32[]{:S(2)}, u32[]{:S(2)}) collective-permute-start(bf16[512,256]{1,0:T(8,128)(2,1)S(1)} %collective-permute-done.6.refs_9_), channel_id=1, source_target_pairs={{0,4},{4,0},{8,12},{12,8},{16,20},{20,16},{24,28},{28,24},{1,5},{5... | collective-permute-start | bytes 786440 | tf_op jit(solution)/shard_map/ppermute | solution.py:226
  76.9 8.5 %collective-permute-start.23 = (bf16[112,1024]{1,0:T(8,128)(2,1)S(1)}, bf16[112,1024]{1,0:T(8,128)(2,1)S(1)}, u32[]{:S(2)}, u32[]{:S(2)}) collective-permute-start(bf16[112,1024]{1,0:T(8,128)(2,1)S(1)} %get-tuple-element.27), channel_id=1, source_target_pairs={{16,0},{20,4},{24,8},{28,12},{0,16},{4,20},{8,24},{12,28},{17,1},{... | collective-permute-start | bytes 688136 | tf_op jit(solution)/shard_map/ppermute | solution.py:214
  78.7 21.4 %collective-permute-start.31 = (bf16[704,1024]{1,0:T(8,128)(2,1)}, bf16[704,1024]{1,0:T(8,128)(2,1)}, u32[]{:S(2)}, u32[]{:S(2)}) collective-permute-start(bf16[704,1024]{1,0:T(8,128)(2,1)} %get-tuple-element.31), channel_id=1, source_target_pairs={{0,4},{4,0},{8,12},{12,8},{16,20},{20,16},{24,28},{28,24},{1,5},{5... | collective-permute-start | bytes 4325384 | tf_op jit(solution)/shard_map/ppermute | solution.py:226
  78.7 16.6 %collective-permute-start.19 = (bf16[128,1024]{1,0:T(8,128)(2,1)S(1)}, bf16[128,1024]{1,0:T(8,128)(2,1)S(1)}, u32[]{:S(2)}, u32[]{:S(2)}) collective-permute-start(bf16[128,1024]{1,0:T(8,128)(2,1)S(1)} %get-tuple-element.24), channel_id=1, source_target_pairs={{16,0},{20,4},{24,8},{28,12},{0,16},{4,20},{8,24},{12,28},{17,1},{... | collective-permute-start | bytes 786440 | tf_op jit(solution)/shard_map/ppermute | solution.py:214
  79.0 15.5 %collective-permute-start.27 = (bf16[112,1024]{1,0:T(8,128)(2,1)S(1)}, bf16[112,1024]{1,0:T(8,128)(2,1)S(1)}, u32[]{:S(2)}, u32[]{:S(2)}) collective-permute-start(bf16[112,1024]{1,0:T(8,128)(2,1)S(1)} %get-tuple-element.29), channel_id=1, source_target_pairs={{16,0},{20,4},{24,8},{28,12},{0,16},{4,20},{8,24},{12,28},{17,1},{... | collective-permute-start | bytes 688136 | tf_op jit(solution)/shard_map/ppermute | solution.py:214
  88.0 14.1 %collective-permute-start.24 = (bf16[112,256]{1,0:T(8,128)(2,1)S(1)}, bf16[112,256]{1,0:T(8,128)(2,1)S(1)}, u32[]{:S(2)}, u32[]{:S(2)}) collective-permute-start(bf16[112,256]{1,0:T(8,128)(2,1)S(1)} %get-tuple-element.37), channel_id=1, source_target_pairs={{1,0},{2,1},{3,2},{0,3},{5,4},{6,5},{7,6},{4,7},{9,8},{10,9},{11,1... | collective-permute-start | bytes 172040 | tf_op jit(solution)/shard_map/ppermute | solution.py:229
  90.7 12.5 %collective-permute-start.25 = (bf16[112,256]{1,0:T(8,128)(2,1)S(1)}, bf16[112,256]{1,0:T(8,128)(2,1)S(1)}, u32[]{:S(2)}, u32[]{:S(2)}) collective-permute-start(bf16[112,256]{1,0:T(8,128)(2,1)S(1)} %get-tuple-element.39), channel_id=1, source_target_pairs={{2,0},{3,1},{0,2},{1,3},{6,4},{7,5},{4,6},{5,7},{10,8},{11,9},{8,1... | collective-permute-start | bytes 172040 | tf_op jit(solution)/shard_map/ppermute | solution.py:229
  94.4 11.5 %collective-permute-start.26 = (bf16[112,256]{1,0:T(8,128)(2,1)S(1)}, bf16[112,256]{1,0:T(8,128)(2,1)S(1)}, u32[]{:S(2)}, u32[]{:S(2)}) collective-permute-start(bf16[112,256]{1,0:T(8,128)(2,1)S(1)} %get-tuple-element.38), channel_id=1, source_target_pairs={{3,0},{0,1},{1,2},{2,3},{7,4},{4,5},{5,6},{6,7},{11,8},{8,9},{9,10... | collective-permute-start | bytes 172040 | tf_op jit(solution)/shard_map/ppermute | solution.py:229
  95.3 12.4 %collective-permute-start.28 = (bf16[112,256]{1,0:T(8,128)(2,1)S(1)}, bf16[112,256]{1,0:T(8,128)(2,1)S(1)}, u32[]{:S(2)}, u32[]{:S(2)}) collective-permute-start(bf16[112,256]{1,0:T(8,128)(2,1)S(1)} %get-tuple-element.40), channel_id=1, source_target_pairs={{1,0},{2,1},{3,2},{0,3},{5,4},{6,5},{7,6},{4,7},{9,8},{10,9},{11,1... | collective-permute-start | bytes 172040 | tf_op jit(solution)/shard_map/ppermute | solution.py:229
  100.1 8.4 %collective-permute-start.29 = (bf16[112,256]{1,0:T(8,128)(2,1)S(1)}, bf16[112,256]{1,0:T(8,128)(2,1)S(1)}, u32[]{:S(2)}, u32[]{:S(2)}) collective-permute-start(bf16[112,256]{1,0:T(8,128)(2,1)S(1)} %get-tuple-element.42), channel_id=1, source_target_pairs={{2,0},{3,1},{0,2},{1,3},{6,4},{7,5},{4,6},{5,7},{10,8},{11,9},{8,1... | collective-permute-start | bytes 172040 | tf_op jit(solution)/shard_map/ppermute | solution.py:229
  102.1 6.5 %collective-permute-start.30 = (bf16[112,256]{1,0:T(8,128)(2,1)S(1)}, bf16[112,256]{1,0:T(8,128)(2,1)S(1)}, u32[]{:S(2)}, u32[]{:S(2)}) collective-permute-start(bf16[112,256]{1,0:T(8,128)(2,1)S(1)} %get-tuple-element.41), channel_id=1, source_target_pairs={{3,0},{0,1},{1,2},{2,3},{7,4},{4,5},{5,6},{6,7},{11,8},{8,9},{9,10... | collective-permute-start | bytes 172040 | tf_op jit(solution)/shard_map/ppermute | solution.py:229
  106.0 15.5 %collective-permute-start.32 = (bf16[352,1024]{1,0:T(8,128)(2,1)S(1)}, bf16[352,1024]{1,0:T(8,128)(2,1)S(1)}, u32[]{:S(2)}, u32[]{:S(2)}) collective-permute-start(bf16[352,1024]{1,0:T(8,128)(2,1)S(1)} %add_convert_fusion.1), channel_id=1, source_target_pairs={{8,0},{12,4},{0,8},{4,12},{24,16},{28,20},{16,24},{20,28},{9,1},{1... | collective-permute-start | bytes 2162696 | tf_op jit(solution)/shard_map/ppermute | solution.py:223
  108.5 6.1 %collective-permute-start.22 = (bf16[128,256]{1,0:T(8,128)(2,1)S(1)}, bf16[128,256]{1,0:T(8,128)(2,1)S(1)}, u32[]{:S(2)}, u32[]{:S(2)}) collective-permute-start(bf16[128,256]{1,0:T(8,128)(2,1)S(1)} %get-tuple-element.35), channel_id=1, source_target_pairs={{3,0},{0,1},{1,2},{2,3},{7,4},{4,5},{5,6},{6,7},{11,8},{8,9},{9,10... | collective-permute-start | bytes 196616 | tf_op jit(solution)/shard_map/ppermute | solution.py:229
  (18 other events, 189.0 us)
